TPU v7x, 128 devices: a whole 4x4x4 slice. The times are simulated.
128 devices in a mesh: blk: 16 (over y, x_lo, core), lag: 8 (over z, x_hi).
Axes of the slice: x: 4 (x_hi: 2, x_lo: 2; x = x_hi * 2 + x_lo), y: 4, z: 4, core: 2. Of those that a mesh axis runs over, the one named last changes fastest.
Arguments:
- raw: float32 [8192, 4096], P(('blk', 'lag')), may hold values from -60 to 60
- mask: int32 [16, 16], replicated, may hold values from 0 to 1, as said below
Outputs:
- stack: float32 [8, 8192], P(None, ('blk', 'lag'))
Inputs may be any that keep to these rules, and one draw needn't show every extreme that they name: mask is 0 or 1 and symmetric; it is 0 wherever |I - J| exceeds a limit between 8 and 14.
All inputs are finite; a program needn't handle non-finite values.
Results may differ from a plain program's by a relative error of at most 0.008.
Values may be sent and summed in bfloat16 or wider, within the bound.
No kernel may reach another device: no remote copies, remote signals or barrier semaphores. Data moves between devices by JAX's collectives and lax.ppermute only.
A program may use at most 192 MiB of HBM per device.

v0:
```python
import math

import jax
import jax.numpy as jnp
from jax import lax
from jax.sharding import PartitionSpec as P

NT = 8192
C = 4096
NB = 2048
K0 = 16
SW = 32
TAPER = 128
LAGS = 8
LAG_STEP = 32


EPS = 1e-06


def padded_2(x, sides, width):
    for axis, dim in sides:
        size, length = (lax.axis_size(axis), x.shape[dim])
        up = [(i, (i + 1) % size) for i in range(size - 1)]
        down = [(j, i) for i, j in up]
        last = lax.slice_in_dim(x, length - width, length, axis=dim)
        initial = lax.slice_in_dim(x, 0, width, axis=dim)
        before = lax.ppermute(last, axis, up)
        after = lax.ppermute(initial, axis, down)
        x = jnp.concatenate([before, x, after], axis=dim)
    return x


def taper_weights(first_bin, count):
    position = (first_bin + lax.iota(jnp.int32, count)).astype(jnp.float32)
    edge = jnp.minimum(position, NB - 1 - position)
    curve = 0.5 - 0.5 * jnp.cos(math.pi * (edge + 0.5) / TAPER)
    return jnp.where(edge < TAPER, curve, jnp.ones_like(curve))


def lag_phases(bins):
    number = lax.iota(jnp.int32, LAGS)
    shifts = LAG_STEP * (2 * number + 1 - LAGS) // 2
    return jnp.mod(shifts[:, None] * bins[None, :], NT).astype(jnp.float32) * (2 * math.pi / NT)


def moving_mean(padded):
    window = lax.reduce_window(
        padded, jnp.zeros((), padded.dtype), lax.add, (1, 2 * SW + 1), (1, 1), "VALID"
    )
    return window / (2 * SW + 1)


def rotate(own_real, own_imag, cosines, sines):
    real_part = own_real.astype(jnp.float32)[None]
    imag_part = own_imag.astype(jnp.float32)[None]
    rot_real = real_part * cosines[:, None, :] - imag_part * sines[:, None, :]
    rot_imag = real_part * sines[:, None, :] + imag_part * cosines[:, None, :]
    joined = jnp.concatenate([rot_real, rot_imag], axis=2).astype(jnp.bfloat16)
    return joined.reshape(joined.shape[0] * joined.shape[1], joined.shape[2])


def diagonal_sums(product, rows):
    count = product.shape[2]
    padded = jnp.pad(product, ((0, 0), (0, 0), (0, rows)))
    width = count + rows - 1
    flat = padded.reshape(product.shape[0], rows * (count + rows))[:, : rows * width]
    return jnp.sum(flat.reshape(product.shape[0], rows, width), axis=1)


def place(total, values, first_col):
    anchor = jnp.zeros((), jnp.int32)
    current = lax.dynamic_slice(total, (anchor, first_col), values.shape)
    return lax.dynamic_update_slice(total, current + values, (anchor, first_col))


def pair_counts(mask, columns):
    blocks = mask.shape[0]
    width = C // blocks
    labels = lax.iota(jnp.int32, blocks)
    apart = labels[None, :] - labels[:, None]
    deltas = lax.iota(jnp.int32, 2 * blocks - 1) - (blocks - 1)
    per_delta = jnp.sum(
        mask[None] * (apart[None] == deltas[:, None, None]).astype(jnp.int32), axis=(1, 2)
    )
    offsets = columns - C
    intersection = jnp.maximum(0, width - jnp.abs(offsets[:, None] - width * deltas[None, :]))
    return jnp.sum(intersection * per_delta[None, :], axis=1)


def stack_scale(counts):
    return 1.0 / jnp.sqrt(NB * jnp.maximum(counts, 1).astype(jnp.float32))


def on_device(raw, mask):
    n_lag = lax.axis_size("lag")
    blk_id = lax.axis_index("blk")
    lag_id = lax.axis_index("lag")
    series = lax.all_to_all(
        raw.astype(jnp.bfloat16), ("blk", "lag"), split_axis=1, concat_axis=0, tiled=True
    ).astype(raw.dtype)
    own_chans = series.shape[1]
    band_bins = K0 + lax.iota(jnp.int32, NB)
    rows_blk = 1024
    offsets_in = lax.iota(jnp.int32, rows_blk)
    base_angle = jnp.mod(offsets_in[:, None] * band_bins[None, :], NT).astype(jnp.float32) * (
        2 * math.pi / NT
    )
    base_cos = jnp.cos(base_angle)
    base_sin = jnp.sin(base_angle)

    def transform_block(number, sums):
        start = number * rows_blk
        samples = lax.dynamic_slice_in_dim(series, start, rows_blk, 0)
        dims = (((0,), (0,)), ((), ()))
        part_cos = lax.dot_general(
            samples,
            base_cos,
            dims,
            precision=lax.Precision.HIGHEST,
            preferred_element_type=jnp.float32,
        )
        part_sin = lax.dot_general(
            samples,
            base_sin,
            dims,
            precision=lax.Precision.HIGHEST,
            preferred_element_type=jnp.float32,
        )
        shift_angle = jnp.mod(start * band_bins, NT).astype(jnp.float32) * (2 * math.pi / NT)
        shift_cos = jnp.cos(shift_angle)[None, :]
        shift_sin = jnp.sin(shift_angle)[None, :]
        real_add = part_cos * shift_cos - part_sin * shift_sin
        imag_add = part_sin * shift_cos + part_cos * shift_sin
        return (sums[0] + real_add, sums[1] - imag_add)

    empty = jnp.zeros((own_chans, NB), jnp.float32)
    real_spec, imag_spec = lax.fori_loop(0, NT // rows_blk, transform_block, (empty, empty))
    spectra = jnp.stack([real_spec, imag_spec], axis=1)
    banded = lax.all_to_all(
        spectra.astype(jnp.bfloat16), "lag", split_axis=2, concat_axis=0, tiled=True
    ).astype(spectra.dtype)
    rows = banded.shape[0]
    n_bins = banded.shape[2]
    real_band = banded[:, 0, :]
    imag_band = banded[:, 1, :]
    amplitude = jnp.sqrt(real_band * real_band + imag_band * imag_band)
    widened = padded_2(amplitude.astype(jnp.bfloat16), (("lag", 1),), SW).astype(amplitude.dtype)
    smooth = moving_mean(widened)
    first_bin = lag_id * n_bins
    weights = taper_weights(first_bin, n_bins)
    real_white = (real_band * weights[None, :] / (smooth + EPS)).astype(jnp.bfloat16)
    imag_white = (imag_band * weights[None, :] / (smooth + EPS)).astype(jnp.bfloat16)
    white = jnp.concatenate([real_white, imag_white], axis=1)
    phases = lag_phases(K0 + first_bin + lax.iota(jnp.int32, n_bins))
    rotated = rotate(real_white[::-1], imag_white[::-1], jnp.cos(phases), jnp.sin(phases))
    row_mask = lax.dynamic_index_in_dim(mask, blk_id, 0, keepdims=False)
    column_mask = jnp.repeat(row_mask, rows).astype(jnp.bfloat16)
    initial = jnp.zeros((LAGS, 2 * C), jnp.float32)
    piece = lax.all_gather(white, "blk", axis=0, tiled=True)
    start = jnp.int32(0)
    count = piece.shape[0]
    live = lax.dynamic_slice_in_dim(column_mask, start, count, 0)
    product = lax.dot_general(
        rotated, piece * live[:, None], (((1,), (1,)), ((), ())), preferred_element_type=jnp.float32
    )
    diagonal = diagonal_sums(product.reshape(LAGS, rows, count), rows)
    first_col = start - blk_id * rows + C - rows + 1
    diagonal, first_col = (diagonal, first_col)
    total = place(initial, diagonal, first_col)
    shares = lax.psum_scatter(total, ("blk", "lag"), scatter_dimension=1, tiled=True)
    n_cols = shares.shape[1]
    device = blk_id * n_lag + lag_id
    columns = device * n_cols + lax.iota(jnp.int32, n_cols)
    counts = pair_counts(mask, columns)
    return shares * stack_scale(counts)[None, :]


def solution(mesh):
    return jax.shard_map(
        on_device,
        mesh=mesh,
        in_specs=(P(("blk", "lag"), None), P()),
        out_specs=P(None, ("blk", "lag")),
        check_vma=False,
    )
```

profile of v0, /device:TPU:1, one launch (start us, length us, event | category | flops | bytes accessed | tf_op | source)
XLA Modules:
  0.0 1760.8 jit_solution(11160354922658191864)
XLA Ops:
  38.9 616.5 %while.21 = (s32[]{:T(128)}, f32[32,2048]{1,0:T(8,128)S(1)}, f32[32,2048]{1,0:T(8,128)}, f32[8192,32]{1,0:T(8,128)}, s32[2048]{0:T(1024)S(1)}, /*index=5*/s32[]{:T(128)}, s32[]{:T(128)}, s32[]{:T(128)}, s32[]{:T(128)}) while((s32[]{:T(128)}, f32[32,2048]{1,0:T(8,128)S(1)}, f32[32,2048]{1,0:T(8,128)}, ...), condition=%wide.region_1.2_spmd.clone.clone.clone, body=%wide.region_0.1_spmd.clone.clone.clone.sunk | while | flops 1670019072 | bytes 4767961 | solution.py:138
  38.9 38.2 %fusion.62 = f32[32,2048]{1,0:T(8,128)S(1)} fusion(s32[2048]{0:T(1024)S(1)} %get-tuple-element.396, f32[8192,32]{1,0:T(8,128)} %get-tuple-element.395, s32[]{:T(128)S(6)} %select_n.151), kind=kOutput, calls=%fused_computation.9.clone.1 | convolution fusion | flops 834666496 | bytes 794628 | tf_op jit(solution)/shard_map/while/body/eval_jaxpr/dot_general | solution.py:123
  77.2 38.0 %select_subtract_fusion.2 = (f32[32,2048]{1,0:T(8,128)S(1)}, f32[32,2048]{1,0:T(8,128)S(1)}) fusion(f32[32,2048]{1,0:T(8,128)S(1)} %copy-done, f32[32,2048]{1,0:T(8,128)S(1)} %fusion.62, f32[2048]{0:T(1024)S(1)} %get-tuple-element.367, f32[2048]{0:T(1024)S(1)} %get-tuple-element.368, pred[]{:T(512)S(6)} %compare.23, ...), kind=kOutput, calls=%fused_computation.18.clone.1 | convolution fusion | flops 835321856 | bytes 1859589 | tf_op jit(solution)/shard_map/while/body/eval_jaxpr/dot_general | solution.py:116
  116.0 38.2 %fusion.62 = f32[32,2048]{1,0:T(8,128)S(1)} fusion(s32[2048]{0:T(1024)S(1)} %get-tuple-element.396, f32[8192,32]{1,0:T(8,128)} %get-tuple-element.395, s32[]{:T(128)S(6)} %select_n.151), kind=kOutput, calls=%fused_computation.9.clone.1 | convolution fusion | flops 834666496 | bytes 794628 | tf_op jit(solution)/shard_map/while/body/eval_jaxpr/dot_general | solution.py:123
  154.3 38.0 %select_subtract_fusion.2 = (f32[32,2048]{1,0:T(8,128)S(1)}, f32[32,2048]{1,0:T(8,128)S(1)}) fusion(f32[32,2048]{1,0:T(8,128)S(1)} %copy-done, f32[32,2048]{1,0:T(8,128)S(1)} %fusion.62, f32[2048]{0:T(1024)S(1)} %get-tuple-element.367, f32[2048]{0:T(1024)S(1)} %get-tuple-element.368, pred[]{:T(512)S(6)} %compare.23, ...), kind=kOutput, calls=%fused_computation.18.clone.1 | convolution fusion | flops 835321856 | bytes 1859589 | tf_op jit(solution)/shard_map/while/body/eval_jaxpr/dot_general | solution.py:116
  193.0 38.2 %fusion.62 = f32[32,2048]{1,0:T(8,128)S(1)} fusion(s32[2048]{0:T(1024)S(1)} %get-tuple-element.396, f32[8192,32]{1,0:T(8,128)} %get-tuple-element.395, s32[]{:T(128)S(6)} %select_n.151), kind=kOutput, calls=%fused_computation.9.clone.1 | convolution fusion | flops 834666496 | bytes 794628 | tf_op jit(solution)/shard_map/while/body/eval_jaxpr/dot_general | solution.py:123
  231.3 38.0 %select_subtract_fusion.2 = (f32[32,2048]{1,0:T(8,128)S(1)}, f32[32,2048]{1,0:T(8,128)S(1)}) fusion(f32[32,2048]{1,0:T(8,128)S(1)} %copy-done, f32[32,2048]{1,0:T(8,128)S(1)} %fusion.62, f32[2048]{0:T(1024)S(1)} %get-tuple-element.367, f32[2048]{0:T(1024)S(1)} %get-tuple-element.368, pred[]{:T(512)S(6)} %compare.23, ...), kind=kOutput, calls=%fused_computation.18.clone.1 | convolution fusion | flops 835321856 | bytes 1859589 | tf_op jit(solution)/shard_map/while/body/eval_jaxpr/dot_general | solution.py:116
  270.1 38.2 %fusion.62 = f32[32,2048]{1,0:T(8,128)S(1)} fusion(s32[2048]{0:T(1024)S(1)} %get-tuple-element.396, f32[8192,32]{1,0:T(8,128)} %get-tuple-element.395, s32[]{:T(128)S(6)} %select_n.151), kind=kOutput, calls=%fused_computation.9.clone.1 | convolution fusion | flops 834666496 | bytes 794628 | tf_op jit(solution)/shard_map/while/body/eval_jaxpr/dot_general | solution.py:123
  308.4 38.0 %select_subtract_fusion.2 = (f32[32,2048]{1,0:T(8,128)S(1)}, f32[32,2048]{1,0:T(8,128)S(1)}) fusion(f32[32,2048]{1,0:T(8,128)S(1)} %copy-done, f32[32,2048]{1,0:T(8,128)S(1)} %fusion.62, f32[2048]{0:T(1024)S(1)} %get-tuple-element.367, f32[2048]{0:T(1024)S(1)} %get-tuple-element.368, pred[]{:T(512)S(6)} %compare.23, ...), kind=kOutput, calls=%fused_computation.18.clone.1 | convolution fusion | flops 835321856 | bytes 1859589 | tf_op jit(solution)/shard_map/while/body/eval_jaxpr/dot_general | solution.py:116
  347.2 38.2 %fusion.62 = f32[32,2048]{1,0:T(8,128)S(1)} fusion(s32[2048]{0:T(1024)S(1)} %get-tuple-element.396, f32[8192,32]{1,0:T(8,128)} %get-tuple-element.395, s32[]{:T(128)S(6)} %select_n.151), kind=kOutput, calls=%fused_computation.9.clone.1 | convolution fusion | flops 834666496 | bytes 794628 | tf_op jit(solution)/shard_map/while/body/eval_jaxpr/dot_general | solution.py:123
  385.5 38.0 %select_subtract_fusion.2 = (f32[32,2048]{1,0:T(8,128)S(1)}, f32[32,2048]{1,0:T(8,128)S(1)}) fusion(f32[32,2048]{1,0:T(8,128)S(1)} %copy-done, f32[32,2048]{1,0:T(8,128)S(1)} %fusion.62, f32[2048]{0:T(1024)S(1)} %get-tuple-element.367, f32[2048]{0:T(1024)S(1)} %get-tuple-element.368, pred[]{:T(512)S(6)} %compare.23, ...), kind=kOutput, calls=%fused_computation.18.clone.1 | convolution fusion | flops 835321856 | bytes 1859589 | tf_op jit(solution)/shard_map/while/body/eval_jaxpr/dot_general | solution.py:116
  424.2 38.2 %fusion.62 = f32[32,2048]{1,0:T(8,128)S(1)} fusion(s32[2048]{0:T(1024)S(1)} %get-tuple-element.396, f32[8192,32]{1,0:T(8,128)} %get-tuple-element.395, s32[]{:T(128)S(6)} %select_n.151), kind=kOutput, calls=%fused_computation.9.clone.1 | convolution fusion | flops 834666496 | bytes 794628 | tf_op jit(solution)/shard_map/while/body/eval_jaxpr/dot_general | solution.py:123
  462.5 38.0 %select_subtract_fusion.2 = (f32[32,2048]{1,0:T(8,128)S(1)}, f32[32,2048]{1,0:T(8,128)S(1)}) fusion(f32[32,2048]{1,0:T(8,128)S(1)} %copy-done, f32[32,2048]{1,0:T(8,128)S(1)} %fusion.62, f32[2048]{0:T(1024)S(1)} %get-tuple-element.367, f32[2048]{0:T(1024)S(1)} %get-tuple-element.368, pred[]{:T(512)S(6)} %compare.23, ...), kind=kOutput, calls=%fused_computation.18.clone.1 | convolution fusion | flops 835321856 | bytes 1859589 | tf_op jit(solution)/shard_map/while/body/eval_jaxpr/dot_general | solution.py:116
  501.3 38.2 %fusion.62 = f32[32,2048]{1,0:T(8,128)S(1)} fusion(s32[2048]{0:T(1024)S(1)} %get-tuple-element.396, f32[8192,32]{1,0:T(8,128)} %get-tuple-element.395, s32[]{:T(128)S(6)} %select_n.151), kind=kOutput, calls=%fused_computation.9.clone.1 | convolution fusion | flops 834666496 | bytes 794628 | tf_op jit(solution)/shard_map/while/body/eval_jaxpr/dot_general | solution.py:123
  539.6 38.0 %select_subtract_fusion.2 = (f32[32,2048]{1,0:T(8,128)S(1)}, f32[32,2048]{1,0:T(8,128)S(1)}) fusion(f32[32,2048]{1,0:T(8,128)S(1)} %copy-done, f32[32,2048]{1,0:T(8,128)S(1)} %fusion.62, f32[2048]{0:T(1024)S(1)} %get-tuple-element.367, f32[2048]{0:T(1024)S(1)} %get-tuple-element.368, pred[]{:T(512)S(6)} %compare.23, ...), kind=kOutput, calls=%fused_computation.18.clone.1 | convolution fusion | flops 835321856 | bytes 1859589 | tf_op jit(solution)/shard_map/while/body/eval_jaxpr/dot_general | solution.py:116
  578.4 38.2 %fusion.62 = f32[32,2048]{1,0:T(8,128)S(1)} fusion(s32[2048]{0:T(1024)S(1)} %get-tuple-element.396, f32[8192,32]{1,0:T(8,128)} %get-tuple-element.395, s32[]{:T(128)S(6)} %select_n.151), kind=kOutput, calls=%fused_computation.9.clone.1 | convolution fusion | flops 834666496 | bytes 794628 | tf_op jit(solution)/shard_map/while/body/eval_jaxpr/dot_general | solution.py:123
  616.7 38.0 %select_subtract_fusion.2 = (f32[32,2048]{1,0:T(8,128)S(1)}, f32[32,2048]{1,0:T(8,128)S(1)}) fusion(f32[32,2048]{1,0:T(8,128)S(1)} %copy-done, f32[32,2048]{1,0:T(8,128)S(1)} %fusion.62, f32[2048]{0:T(1024)S(1)} %get-tuple-element.367, f32[2048]{0:T(1024)S(1)} %get-tuple-element.368, pred[]{:T(512)S(6)} %compare.23, ...), kind=kOutput, calls=%fused_computation.18.clone.1 | convolution fusion | flops 835321856 | bytes 1859589 | tf_op jit(solution)/shard_map/while/body/eval_jaxpr/dot_general | solution.py:116
  700.4 44.3 %all-gather.2.cloned.1.call-done = bf16[4096,512]{0,1:T(8,128)(2,1)} async-done(((bf16[256,512]{0,1:T(8,128)(2,1)}), bf16[4096,512]{0,1:T(8,128)(2,1)}) %all-gather.2.cloned.1.call-update) | async-done | bytes 4194320 | tf_op jit(solution)/shard_map/all_gather | solution.py:160
  744.6 17.5 fusion.33
  774.4 38.9 %copy.78 = f32[1,8,256,4352]{3,1,2,0:T(8,128)} copy(f32[1,8,256,4352]{3,2,1,0:T(8,128)S(1)} %pad_bitcast_fusion) | data formatting | bytes 71303168
  813.3 26.2 %slice.24 = f32[8,1113856]{1,0:T(8,128)} slice(f32[8,1114112]{1,0:T(8,128)} %bitcast.57), slice={[0:8], [0:1113856]} | slice | bytes 71286784 | tf_op jit(solution)/shard_map/slice | solution.py:67
  839.4 58.8 %reshape.201 = f32[8910848]{0:T(1024)} reshape(f32[8,1113856]{1,0:T(8,128)} %slice.24) | data formatting | bytes 71286784
  907.9 192.7 %while.22 = (u32[]{:T(128)}, f32[8910848]{0:T(1024)}, f32[8,256,4351]{2,1,0:T(8,128)}, u32[]{}, u32[]{}, /*index=5*/u32[]{}, u32[]{}, u32[]{}) while((u32[]{:T(128)}, f32[8910848]{0:T(1024)}, f32[8,256,4351]{2,1,0:T(8,128)}, u32[]{}, u32[]{}, /*index=5*/u32[]{}, u32[]{}, u32[]{}) %tuple.83), condition=%wide.cond, body=%wide.body.sunk | while | flops 9 | bytes 25061936
  1116.7 635.6 %reduce-scatter.4.cloned.1.call-done = f32[64,8]{1,0:T(8,128)} async-done(((f32[8192,8]{1,0:T(8,128)}), f32[64,8]{1,0:T(8,128)}) %reduce-scatter.4.cloned.1.call-update) | async-done | bytes 2064
  (148 shorter events, 315.0 us)
Async XLA Ops:
  9.7 25.5 %all-to-all-start = ((bf16[128,2,1024]{2,1,0:T(2,128)(2,1)}), bf16[128,2,1024]{2,1,0:T(2,128)(2,1)S(1)}, u32[]{:S(2)}, u32[]{:S(2)}) async-start(bf16[128,2,1024]{2,1,0:T(2,128)(2,1)} %reshape.211), calls=%async_computation | async-start | bytes 1048576 | tf_op jit(solution)/shard_map/all_to_all | solution.py:99
  38.9 38.3 %copy-start = (f32[32,2048]{1,0:T(8,128)S(1)}, f32[32,2048]{1,0:T(8,128)}, u32[]{:S(2)}) copy-start(f32[32,2048]{1,0:T(8,128)} %get-tuple-element.385) | copy-start | bytes 786436 | tf_op jit(solution)/shard_map/while
  115.2 0.7 copy-start.1
  115.9 38.3 %copy-start = (f32[32,2048]{1,0:T(8,128)S(1)}, f32[32,2048]{1,0:T(8,128)}, u32[]{:S(2)}) copy-start(f32[32,2048]{1,0:T(8,128)} %get-tuple-element.385) | copy-start | bytes 786436 | tf_op jit(solution)/shard_map/while
  192.3 0.7 copy-start.1
  193.0 38.3 %copy-start = (f32[32,2048]{1,0:T(8,128)S(1)}, f32[32,2048]{1,0:T(8,128)}, u32[]{:S(2)}) copy-start(f32[32,2048]{1,0:T(8,128)} %get-tuple-element.385) | copy-start | bytes 786436 | tf_op jit(solution)/shard_map/while
  269.4 0.7 copy-start.1
  270.1 38.3 %copy-start = (f32[32,2048]{1,0:T(8,128)S(1)}, f32[32,2048]{1,0:T(8,128)}, u32[]{:S(2)}) copy-start(f32[32,2048]{1,0:T(8,128)} %get-tuple-element.385) | copy-start | bytes 786436 | tf_op jit(solution)/shard_map/while
  346.4 0.7 copy-start.1
  347.2 38.3 %copy-start = (f32[32,2048]{1,0:T(8,128)S(1)}, f32[32,2048]{1,0:T(8,128)}, u32[]{:S(2)}) copy-start(f32[32,2048]{1,0:T(8,128)} %get-tuple-element.385) | copy-start | bytes 786436 | tf_op jit(solution)/shard_map/while
  423.5 0.7 copy-start.1
  424.2 38.3 %copy-start = (f32[32,2048]{1,0:T(8,128)S(1)}, f32[32,2048]{1,0:T(8,128)}, u32[]{:S(2)}) copy-start(f32[32,2048]{1,0:T(8,128)} %get-tuple-element.385) | copy-start | bytes 786436 | tf_op jit(solution)/shard_map/while
  500.6 0.7 copy-start.1
  501.3 38.3 %copy-start = (f32[32,2048]{1,0:T(8,128)S(1)}, f32[32,2048]{1,0:T(8,128)}, u32[]{:S(2)}) copy-start(f32[32,2048]{1,0:T(8,128)} %get-tuple-element.385) | copy-start | bytes 786436 | tf_op jit(solution)/shard_map/while
  577.6 0.7 copy-start.1
  578.4 38.3 %copy-start = (f32[32,2048]{1,0:T(8,128)S(1)}, f32[32,2048]{1,0:T(8,128)}, u32[]{:S(2)}) copy-start(f32[32,2048]{1,0:T(8,128)} %get-tuple-element.385) | copy-start | bytes 786436 | tf_op jit(solution)/shard_map/while
  654.7 0.7 copy-start.1
  655.4 43.0 %copy-start.2 = (s32[16,16]{1,0:T(8,128)S(1)}, s32[16,16]{1,0:T(8,128)}, u32[]{:S(2)}) copy-start(s32[16,16]{1,0:T(8,128)} %param.5) | copy-start | bytes 3076
  658.9 23.7 %all-to-all-start.1 = ((bf16[8,2,8192]{2,1,0:T(2,128)(2,1)}), bf16[8,2,8192]{2,1,0:T(2,128)(2,1)S(1)}, u32[]{:S(2)}, u32[]{:S(2)}) async-start(bf16[8,2,8192]{2,1,0:T(2,128)(2,1)} %reshape.213), calls=%async_computation.1 | async-start | bytes 524288 | tf_op jit(solution)/shard_map/all_to_all | solution.py:140
  674.1 70.6 %all-gather.2.cloned.1.call-start = ((), (), s32[]{:S(2)}) async-start(), calls=%async_computation.3 | async-start | bytes 4456448 | tf_op jit(solution)/shard_map/all_gather | solution.py:160
  684.6 3.7 collective-permute-start
  687.0 6.0 collective-permute-start.1
  698.3 1054.0 %reduce-scatter.4.cloned.1.call-start = ((), (), s32[]{:S(2)}) async-start(), calls=%async_computation.4 | async-start | bytes 4227072
Sparse Core Ops, SparseCore 0:
  698.4 46.1 all-gather.1
  1116.6 635.6 reduce-scatter.3
where the time goes:
time: 1780 us; the launch traced here: 1760 us
  waiting for transfers between devices  707 us (40%)
  matrix products  628 us (35%)
  local copies, waits for them, and re-layouts  359 us (20%)
  starting transfers between devices  30.4 us (2%)
  other arithmetic  22.3 us (1%)
    unnamed x3, waiting for transfers between devices  636 us
    unnamed x58, local copies, waits for them, and re-layouts  323 us
    dot_general x8, matrix products, transform_block(): lax.dot_general(samples, base_sin, dims, precision=lax.Precision.HIGHEST,...  306 us
    dot_general x8, matrix products, transform_block(): lax.dot_general(samples, base_cos, dims, precision=lax.Precision.HIGHEST,...  304 us
    all_gather x1, waiting for transfers between devices, on_device(): piece = lax.all_gather(white, 'blk', axis=0, tiled=True)  44.3 us
  transfers between devices with their start and end apart: 6, of which 5 were waited for; matrix products, arithmetic and copies ran while one was open for 0% of the time, Pallas kernels for 0%

commit v1 on v0

v1 whole, which is shorter than its diff:
```python
import math

import jax
import jax.numpy as jnp
import numpy as np
from jax import lax
from jax.experimental import pallas as pl
from jax.experimental.pallas import tpu as pltpu
from jax.sharding import PartitionSpec as P

NT = 8192
C = 4096
NB = 2048
K0 = 16
SW = 32
TAPER = 128
LAGS = 8
LAG_STEP = 32
EPS = 1e-06

DEV = 128
ROWS = NT // DEV
BLK = 16
J2 = NB // DEV
Q = 512
FAR = 15

BF = jnp.bfloat16
F32 = jnp.float32


def split(x):
    hi = x.astype(BF)
    return hi, (x - hi.astype(F32)).astype(BF)


def np_split(x):
    hi = np.asarray(x, np.float32).astype(jnp.bfloat16)
    lo = (np.asarray(x, np.float64) - hi.astype(np.float64)).astype(jnp.bfloat16)
    return hi, lo


def cs(numer, period):
    angle = 2 * np.pi * np.mod(numer, period) / period
    return np.cos(angle), np.sin(angle)


def time_tables():
    j1, p = np.arange(DEV), np.arange(DEV)
    c, s = cs((K0 + j1)[:, None] * p[None], DEV)
    stage1 = np.concatenate([c, -s], axis=0).astype(jnp.bfloat16)
    r = np.tile(np.arange(ROWS), 2)
    c, s = cs((K0 + j1)[:, None] * r[None], NT)
    twiddle = np.stack([c, s]).astype(np.float32)
    r, j2 = np.arange(ROWS), np.arange(J2)
    c, s = cs(r[:, None] * j2[None], ROWS)
    eye = np.eye(8)
    place = lambda t: np.einsum("ab,rj->arbj", eye, t).reshape(8 * ROWS, 8 * J2)
    stage2 = np.block([[place(c), place(-s)], [place(s), place(c)]])
    return stage1, twiddle, stage2.astype(jnp.bfloat16)


def window_table():
    i, j = np.arange(DEV)[:, None], np.arange(DEV)[None]
    near = lambda d: (np.abs(d) <= SW).astype(np.float32)
    return np.concatenate([near(i - j), near(i - j - DEV), near(i - j + DEV)], axis=1).astype(
        jnp.bfloat16
    )


def taper_table():
    position = np.arange(DEV)[:, None] + DEV * np.arange(J2)[None]
    edge = np.minimum(position, NB - 1 - position)
    curve = 0.5 - 0.5 * np.cos(math.pi * (edge + 0.5) / TAPER)
    return np.tile(np.where(edge < TAPER, curve, 1.0), (1, DEV // J2)).astype(np.float32)


def channel_table():
    c, s = cs(np.arange(256)[:, None] * np.arange(Q)[None], Q)
    return np_split(np.block([[c, -s], [s, c]]))


def offset_table():
    m = np.concatenate([np.arange(256), 256 - np.arange(256)])
    c, s = cs(np.arange(Q)[:, None] * m[None], Q)
    return np_split(np.concatenate([c, s], axis=0) / Q)


def sign_table():
    table = np.zeros((32, 256), np.float32)
    for delta in range(BLK):
        for j2 in range(J2):
            table[(j2 % 2) * 16 + delta, delta * J2 + j2] = 1.0 if j2 % 4 < 2 else -1.0
    return table.astype(jnp.bfloat16)


def pack_kernel(raw_ref, out_ref, buf_ref):
    for i in range(BLK):
        x = raw_ref[:, i * 256 : (i + 1) * 256]
        rows = jnp.concatenate([x[:, :DEV], x[:, DEV:]], axis=0)
        buf_ref[pl.ds(i, DEV, stride=BLK), :] = rows.T
    out_ref[...] = buf_ref[...].astype(BF)


def dot(a, b):
    return jnp.dot(a, b, preferred_element_type=F32)


def spectra_kernel(in_ref, s1_ref, tw_ref, s2_ref, win_ref, taper_ref, out_ref, buf_ref, wide_ref):
    buf_ref[...] = in_ref[...].astype(F32)
    stage1, stage2 = s1_ref[...], s2_ref[...]
    cos, sin = tw_ref[0], tw_ref[1]
    lane = lax.broadcasted_iota(jnp.int32, (DEV, DEV), 1) % J2
    for g in range(4):
        samples = jnp.concatenate(
            [buf_ref[pl.ds(4 * g + s, DEV, stride=BLK), :] for s in range(4)], axis=1
        ).astype(BF)
        y = dot(stage1, samples)
        reals, imags = [], []
        for s in range(4):
            y_re, y_im = y[:DEV, s * DEV : (s + 1) * DEV], y[DEV:, s * DEV : (s + 1) * DEV]
            reals.append((y_re * cos + y_im * sin).astype(BF))
            imags.append((y_im * cos - y_re * sin).astype(BF))
        spec = dot(jnp.concatenate(reals + imags, axis=1), stage2)
        re, im = spec[:, :DEV], spec[:, DEV:]
        wide_ref[g] = re
        wide_ref[4 + g] = im
    for g in range(4):
        re, im = wide_ref[g], wide_ref[4 + g]
        amp = jnp.sqrt(re * re + im * im)
        after = jnp.where(lane == J2 - 1, 0.0, pltpu.roll(amp, DEV - 1, 1))
        before = jnp.where(lane == 0, 0.0, pltpu.roll(amp, 1, 1))
        total = dot(win_ref[...], jnp.concatenate([amp, after, before], axis=0).astype(BF))
        gain = taper_ref[...] / (total * (1.0 / (2 * SW + 1)) + EPS)
        buf_ref[pl.ds(g, DEV, stride=8), :] = re * gain
        buf_ref[pl.ds(4 + g, DEV, stride=8), :] = im * gain
    out_ref[...] = buf_ref[: 8 * DEV, :].astype(BF)


def stack_kernel(
    in_ref, mask_ref, rot_ref, eh_ref, el_ref, sign_ref, dh_ref, dl_ref, out_ref,
    buf_ref, f_ref, acc_ref, v_ref,
):
    buf_ref[...] = in_ref[...].astype(F32)
    pieces = [buf_ref[pl.ds(t, DEV, stride=8), :].T.astype(BF) for t in range(8)]
    rows = []
    for i in range(BLK):
        g, s = i // 4, i % 4
        tiles = [
            pieces[4 * part + g][(2 * s + h) * J2 : (2 * s + h + 1) * J2]
            for part in range(2)
            for h in range(2)
        ]
        rows.append(jnp.concatenate(tiles, axis=1))
    white = jnp.concatenate(rows, axis=0)
    f_ref[...] = dot(white, eh_ref[...]) + dot(white, el_ref[...])
    acc_ref[FAR * J2 :, :] = jnp.zeros((J2, 2 * Q), F32)

    def unit(u, carry):
        half = pl.multiple_of((u // 4) * 8, 8)
        col = pl.multiple_of((u % 4) * DEV, DEV)
        at = lambda i: pl.ds(i * J2 + half, 8)
        res, ims = pl.ds(col, DEV), pl.ds(col + Q, DEV)
        f_re = [f_ref[at(i), res] for i in range(BLK)]
        f_im = [f_ref[at(i), ims] for i in range(BLK)]
        for delta in range(FAR):
            sum_re = sum_im = jnp.zeros((8, DEV), F32)
            for i in range(BLK - delta):
                j, live = i + delta, mask_ref[i, i + delta]
                a_re, a_im = f_re[i] * live, f_im[i] * live
                sum_re = sum_re + (a_re * f_re[j] + a_im * f_im[j])
                sum_im = sum_im + (a_im * f_re[j] - a_re * f_im[j])
            acc_ref[at(delta), res] = sum_re
            acc_ref[at(delta), ims] = sum_im
        return carry

    lax.fori_loop(0, 8, unit, 0)
    hi, lo = split(acc_ref[...])
    sums = dot(sign_ref[...], hi) + dot(sign_ref[...], lo)
    far = lax.broadcasted_iota(jnp.int32, sums.shape, 0) % BLK == BLK - 1
    odd = lax.broadcasted_iota(jnp.int32, sums.shape, 1) % 2 == 1
    nearer = jnp.where(far, 0.0, pltpu.roll(sums, 2 * BLK - 1, 0))
    sums = sums + jnp.where(odd, -nearer, nearer)
    a_re, a_im, b_re, b_im = sums[:16, :Q], sums[:16, Q:], sums[16:, :Q], sums[16:, Q:]
    quarter = ((a_re - b_im, a_im + b_re), (a_re + b_im, a_im - b_re))
    for j in range(LAGS):
        g_re, g_im = quarter[0 if (2 * j - 7) % 4 == 1 else 1]
        c, s = rot_ref[0, j], rot_ref[1, j]
        v_re, v_im = c * g_re - s * g_im, c * g_im + s * g_re
        for t in range(4):
            v_ref[pl.ds(t * DEV + j, BLK, stride=LAGS), :] = v_re[:, t * DEV : (t + 1) * DEV]
            v_ref[pl.ds((4 + t) * DEV + j, BLK, stride=LAGS), :] = v_im[:, t * DEV : (t + 1) * DEV]
    v_hi, v_lo = split(jnp.concatenate([v_ref[t * DEV : (t + 1) * DEV] for t in range(8)], axis=1))
    stacked = dot(v_hi, dh_ref[...]) + dot(v_hi, dl_ref[...]) + dot(v_lo, dh_ref[...])
    for delta in range(BLK):
        for w in range(4):
            ahead = stacked[8 * delta : 8 * delta + 8, (w // 2) * DEV : (w // 2 + 1) * DEV]
            behind = stacked[8 * delta : 8 * delta + 8, 256 + (w // 2) * DEV : 256 + (w // 2 + 1) * DEV]
            to = 64 + 4 * delta + w
            out_ref[8 * to : 8 * to + 8, :] = ahead.astype(out_ref.dtype)
            to = 4 * (BLK - 1 - delta) + w
            out_ref[8 * to : 8 * to + 8, :] = behind.astype(out_ref.dtype)


def total_kernel(in_ref, place_ref, scale_ref, out_ref):
    total = jnp.sum(in_ref[...].astype(F32), axis=0)
    rolled = jnp.where(place_ref[1] == 1, pltpu.roll(total, 64, 1), total)
    flipped = jnp.concatenate([rolled[7 - j : 8 - j] for j in range(LAGS)], axis=0)
    out = jnp.where(place_ref[0] == 1, flipped, rolled)
    out_ref[...] = out[:, :64] * scale_ref[...]


def pair_counts(mask, columns):
    blocks = mask.shape[0]
    width = C // blocks
    labels = lax.iota(jnp.int32, blocks)
    apart = labels[None, :] - labels[:, None]
    deltas = lax.iota(jnp.int32, 2 * blocks - 1) - (blocks - 1)
    per_delta = jnp.sum(
        mask[None] * (apart[None] == deltas[:, None, None]).astype(jnp.int32), axis=(1, 2)
    )
    offsets = columns - C
    intersection = jnp.maximum(0, width - jnp.abs(offsets[:, None] - width * deltas[None, :]))
    return jnp.sum(intersection * per_delta[None, :], axis=1)


def stack_scale(counts):
    return 1.0 / jnp.sqrt(NB * jnp.maximum(counts, 1).astype(jnp.float32))


VM = pl.BlockSpec(memory_space=pltpu.VMEM)
SM = pl.BlockSpec(memory_space=pltpu.SMEM)


def exchange(x, rows):
    x = x.reshape(DEV, rows, DEV)
    return lax.all_to_all(x, ("blk", "lag"), split_axis=0, concat_axis=0, tiled=True)


def on_device(raw, mask):
    device = lax.axis_index("blk") * lax.axis_size("lag") + lax.axis_index("lag")
    packed = pl.pallas_call(
        pack_kernel,
        out_shape=jax.ShapeDtypeStruct((BLK * DEV, DEV), BF),
        in_specs=[VM],
        out_specs=VM,
        scratch_shapes=[pltpu.VMEM((BLK * DEV, DEV), F32)],
    )(raw)
    series = exchange(packed, BLK).reshape(BLK * DEV, DEV)
    stage1, twiddle, stage2 = time_tables()
    white = pl.pallas_call(
        spectra_kernel,
        out_shape=jax.ShapeDtypeStruct((8 * DEV, DEV), BF),
        in_specs=[VM] * 6,
        out_specs=VM,
        scratch_shapes=[pltpu.VMEM((BLK * DEV, DEV), F32), pltpu.VMEM((8, DEV, DEV), F32)],
    )(series, stage1, twiddle, stage2, window_table(), taper_table())
    banded = exchange(white, 8).reshape(8 * DEV, DEV)
    odd = 2 * lax.iota(jnp.int32, LAGS) - (LAGS - 1)
    angle = jnp.mod(odd * (K0 + device), Q).astype(F32) * (2 * math.pi / Q)
    rotation = jnp.stack([jnp.cos(angle), jnp.sin(angle)])
    parts = pl.pallas_call(
        stack_kernel,
        out_shape=jax.ShapeDtypeStruct((8 * DEV, DEV), BF),
        in_specs=[VM, SM, SM] + [VM] * 5,
        out_specs=VM,
        scratch_shapes=[
            pltpu.VMEM((8 * DEV, DEV), F32),
            pltpu.VMEM((BLK * J2, 2 * Q), F32),
            pltpu.VMEM((BLK * J2, 2 * Q), F32),
            pltpu.VMEM((8 * DEV, DEV), F32),
        ],
    )(banded, mask.astype(F32), rotation, *channel_table(), sign_table(), *offset_table())
    shares = exchange(parts, 8)
    columns = device * 64 + lax.iota(jnp.int32, 64)
    scale = stack_scale(pair_counts(mask, columns))[None, :]
    place = jnp.stack([(device < 64).astype(jnp.int32), device % 2])
    return pl.pallas_call(
        total_kernel,
        out_shape=jax.ShapeDtypeStruct((LAGS, 64), F32),
        in_specs=[VM, SM, VM],
        out_specs=VM,
    )(shares, place, scale)


def solution(mesh):
    return jax.shard_map(
        on_device,
        mesh=mesh,
        in_specs=(P(("blk", "lag"), None), P()),
        out_specs=P(None, ("blk", "lag")),
        check_vma=False,
    )
```

time: 1780 us -> 73.3 us (0.04); the launches traced: 1760 us -> 73 us
  waiting for transfers between devices: 707 us -> 33.2 us
  matrix products: 628 us -> 0 us
  local copies, waits for them, and re-layouts: 359 us -> 2.9 us
  other arithmetic: 22.3 us -> 2.66 us
    unnamed x3 -> x0, waiting for transfers between devices: 636 us -> none
    dot_general x17 -> x0, matrix products: 628 us -> none  [the longest x8 306 us: transform_block(): lax.dot_general(samples, base_sin, dims, precision=lax.Precision.HIGHEST,...]
    unnamed x58 -> x8, local copies, waits for them, and re-layouts: 323 us -> 2.9 us
    all_gather x1 -> x0, waiting for transfers between devices: 44.3 us -> none  [on_device(): piece = lax.all_gather(white, 'blk', axis=0, tiled=True)]
    slice x3 -> x0, local copies, waits for them, and re-layouts: 26.2 us -> none  [the longest x1 26.2 us: diagonal_sums(): padded.reshape(product.shape[0], rows * (count + rows))[:, :rows * width]]
  transfers between devices with their start and end apart: 6 -> 3, of which waited for: 5 -> 3; matrix products, arithmetic and copies ran while one was open for 0% -> 4% of each run, Pallas kernels for 0% -> 0%
where the time goes in v1:
time: 73.3 us; the launch traced here: 73 us
  waiting for transfers between devices  33.2 us (45%)
  starting transfers between devices  19.7 us (27%)
  Pallas kernels  14.4 us (20%)
  local copies, waits for them, and re-layouts  2.9 us (4%)
  other arithmetic  2.66 us (4%)
    all_to_all x3, waiting for transfers between devices, exchange(): lax.all_to_all(x, ('blk', 'lag'), split_axis=0, concat_axis=0, tiled=True)  33.2 us
    all_to_all x3, starting transfers between devices, exchange(): lax.all_to_all(x, ('blk', 'lag'), split_axis=0, concat_axis=0, tiled=True)  19.7 us
    pallas_call x1, Pallas kernels, on_device(): pl.pallas_call(stack_kernel, out_shape=jax.ShapeDtypeStruct((8 * DEV, DEV...  6.82 us
    pallas_call x1, Pallas kernels, on_device(): pl.pallas_call(spectra_kernel, out_shape=jax.ShapeDtypeStruct((8 * DEV, D...  3.38 us
    unnamed x8, local copies, waits for them, and re-layouts  2.9 us
    pallas_call x1, Pallas kernels, on_device(): pl.pallas_call(pack_kernel, out_shape=jax.ShapeDtypeStruct((BLK * DEV, DE...  2.47 us
    pallas_call x1, Pallas kernels, on_device(): pl.pallas_call(total_kernel, out_shape=jax.ShapeDtypeStruct((LAGS, 64), F...  1.76 us
  transfers between devices with their start and end apart: 3, of which 3 were waited for; matrix products, arithmetic and copies ran while one was open for 4% of the time, Pallas kernels for 0%

profile of v1, /device:TPU:1, one launch (start us, length us, event | category | flops | bytes accessed | tf_op | source)
XLA Modules:
  0.0 73.0 jit_solution(8326274600839703230)
XLA Ops:
  0.0 2.5 %shard_map.118 = bf16[2048,128]{1,0:T(8,128)(2,1)} custom-call(f32[64,4096]{1,0:T(8,128)} %raw_ref.1), custom_call_target="tpu_custom_call" | custom-call | tf_op jit(solution)/shard_map/pallas_call | solution.py:242
  2.5 11.5 %all-to-all-start = ((bf16[128,16,128]{2,1,0:T(8,128)(2,1)}), bf16[128,16,128]{2,1,0:T(8,128)(2,1)S(1)}, u32[]{:S(2)}, u32[]{:S(2)}) async-start(bf16[128,16,128]{2,1,0:T(8,128)(2,1)} %bitcast.10), calls=%async_computation | async-start | bytes 1048576 | tf_op jit(solution)/shard_map/all_to_all | solution.py:237
  14.0 0.1 fusion.3
  14.1 0.6 pad_maximum_fusion.rot_ref
  14.6 13.4 %all-to-all-done = bf16[128,16,128]{2,1,0:T(8,128)(2,1)S(1)} async-done(((bf16[128,16,128]{2,1,0:T(8,128)(2,1)}), bf16[128,16,128]{2,1,0:T(8,128)(2,1)S(1)}, u32[]{:S(2)}, u32[]{:S(2)}) %all-to-all-start) | async-done | bytes 524320 | tf_op jit(solution)/shard_map/all_to_all | solution.py:237
  28.0 0.0 copy-start
  28.0 0.8 %copy-done = bf16[128,16,128]{2,1,0:T(8,128)(2,1)} copy-done((bf16[128,16,128]{2,1,0:T(8,128)(2,1)}, bf16[128,16,128]{2,1,0:T(8,128)(2,1)S(1)}, u32[]{:S(2)}) %copy-start) | copy-done | bytes 524312
  28.8 3.4 %shard_map.119 = bf16[1024,128]{1,0:T(8,128)(2,1)} custom-call(bf16[2048,128]{1,0:T(8,128)(2,1)} %bitcast.9, bf16[256,128]{1,0:T(8,128)(2,1)} %constant.84.clone.s1_ref, f32[2,128,128]{2,1,0:T(8,128)} %constant.85.clone.tw_ref, bf16[1024,256]{1,0:T(8,128)(2,1)} %constant.86.clone.s2_ref, bf16[128,384]{1,0:T(8,128)(2,1)} %constant.87.clone.win_ref, ...), custom_call_target="tpu_custom_call" | custom-call | tf_op jit(solution)/shard_map/pallas_call | solution.py:251
  32.2 4.0 %all-to-all-start.1 = ((bf16[128,8,128]{2,1,0:T(8,128)(2,1)}), bf16[128,8,128]{2,1,0:T(8,128)(2,1)S(1)}, u32[]{:S(2)}, u32[]{:S(2)}) async-start(bf16[128,8,128]{2,1,0:T(8,128)(2,1)} %bitcast.11), calls=%async_computation.1 | async-start | bytes 524288 | tf_op jit(solution)/shard_map/all_to_all | solution.py:237
  36.2 0.0 copy-start.3
  36.3 0.7 copy-done.3
  36.9 0.6 convert_element_type.30.mask_ref
  37.5 0.1 select_reduce_fusion
  37.7 0.1 multiply_reduce_fusion
  37.8 9.7 %all-to-all-done.1 = bf16[128,8,128]{2,1,0:T(8,128)(2,1)S(1)} async-done(((bf16[128,8,128]{2,1,0:T(8,128)(2,1)}), bf16[128,8,128]{2,1,0:T(8,128)(2,1)S(1)}, u32[]{:S(2)}, u32[]{:S(2)}) %all-to-all-start.1) | async-done | bytes 262176 | tf_op jit(solution)/shard_map/all_to_all | solution.py:237
  47.5 0.0 copy-start.2
  47.5 0.7 copy-done.2
  48.2 6.8 %shard_map.120 = bf16[1024,128]{1,0:T(8,128)(2,1)} custom-call(bf16[1024,128]{1,0:T(8,128)(2,1)} %bitcast.12, f32[16,16]{1,0:T(8,128)} %convert_element_type.30.mask_ref, f32[2,8]{1,0:T(2,128)} %pad_maximum_fusion.rot_ref, bf16[512,1024]{1,0:T(8,128)(2,1)} %constant.89.clone.eh_ref, bf16[512,1024]{1,0:T(8,128)(2,1)} %constant.90.clone.el_ref, ...), custom_call_target="tpu_custom_call" | custom-call | tf_op jit(solution)/shard_map/pallas_call | solution.py:262
  55.0 4.2 %all-to-all-start.2 = ((bf16[128,8,128]{2,1,0:T(8,128)(2,1)}), bf16[128,8,128]{2,1,0:T(8,128)(2,1)S(1)}, u32[]{:S(2)}, u32[]{:S(2)}) async-start(bf16[128,8,128]{2,1,0:T(8,128)(2,1)} %bitcast.13), calls=%async_computation.2 | async-start | bytes 524288 | tf_op jit(solution)/shard_map/all_to_all | solution.py:237
  59.2 0.7 pad_add_fusion.place_ref
  59.9 0.5 rsqrt_bitcast_fusion.scale_ref
  60.4 10.1 %all-to-all-done.2.in_ref = bf16[128,8,128]{2,1,0:T(8,128)(2,1)S(1)} async-done(((bf16[128,8,128]{2,1,0:T(8,128)(2,1)}), bf16[128,8,128]{2,1,0:T(8,128)(2,1)S(1)}, u32[]{:S(2)}, u32[]{:S(2)}) %all-to-all-start.2) | async-done | bytes 262176 | tf_op jit(solution)/shard_map/all_to_all | solution.py:237
  70.5 0.7 copy-done.1
  71.2 1.8 %shard_map.121 = f32[8,64]{1,0:T(8,128)} custom-call(bf16[128,8,128]{2,1,0:T(8,128)(2,1)} %copy-done.1, s32[2]{0:T(128)} %pad_add_fusion.place_ref, f32[1,64]{1,0:T(1,128)} %rsqrt_bitcast_fusion.scale_ref), custom_call_target="tpu_custom_call" | custom-call | tf_op jit(solution)/shard_map/pallas_call | solution.py:278
  (5 shorter events, 0.0 us)
Async XLA Ops:
  2.5 25.5 %all-to-all-start = ((bf16[128,16,128]{2,1,0:T(8,128)(2,1)}), bf16[128,16,128]{2,1,0:T(8,128)(2,1)S(1)}, u32[]{:S(2)}, u32[]{:S(2)}) async-start(bf16[128,16,128]{2,1,0:T(8,128)(2,1)} %bitcast.10), calls=%async_computation | async-start | bytes 1048576 | tf_op jit(solution)/shard_map/all_to_all | solution.py:237
  28.0 0.8 %copy-start = (bf16[128,16,128]{2,1,0:T(8,128)(2,1)}, bf16[128,16,128]{2,1,0:T(8,128)(2,1)S(1)}, u32[]{:S(2)}) copy-start(bf16[128,16,128]{2,1,0:T(8,128)(2,1)S(1)} %all-to-all-done) | copy-start | bytes 1572868
  32.2 15.3 %all-to-all-start.1 = ((bf16[128,8,128]{2,1,0:T(8,128)(2,1)}), bf16[128,8,128]{2,1,0:T(8,128)(2,1)S(1)}, u32[]{:S(2)}, u32[]{:S(2)}) async-start(bf16[128,8,128]{2,1,0:T(8,128)(2,1)} %bitcast.11), calls=%async_computation.1 | async-start | bytes 524288 | tf_op jit(solution)/shard_map/all_to_all | solution.py:237
  36.2 0.7 copy-start.3
  47.5 0.7 copy-start.2
  55.0 15.4 %all-to-all-start.2 = ((bf16[128,8,128]{2,1,0:T(8,128)(2,1)}), bf16[128,8,128]{2,1,0:T(8,128)(2,1)S(1)}, u32[]{:S(2)}, u32[]{:S(2)}) async-start(bf16[128,8,128]{2,1,0:T(8,128)(2,1)} %bitcast.13), calls=%async_computation.2 | async-start | bytes 524288 | tf_op jit(solution)/shard_map/all_to_all | solution.py:237
  70.5 0.7 copy-start.1

commit v2 on v1

--- a/solution.py
+++ b/solution.py
@@ -94,9 +94,20 @@
     return table.astype(jnp.bfloat16)
 
 
-def pack_kernel(raw_ref, out_ref, buf_ref):
+def pack_kernel(raw_ref, out_ref, raw_buf, buf_ref, sems):
+    wide = C // 4
+    copies = [
+        pltpu.make_async_copy(
+            raw_ref.at[:, pl.ds(k * wide, wide)], raw_buf.at[:, pl.ds(k * wide, wide)], sems.at[k]
+        )
+        for k in range(4)
+    ]
+    for copy in copies:
+        copy.start()
     for i in range(BLK):
-        x = raw_ref[:, i * 256 : (i + 1) * 256]
+        if i % 4 == 0:
+            copies[i // 4].wait()
+        x = raw_buf[:, i * 256 : (i + 1) * 256]
         rows = jnp.concatenate([x[:, :DEV], x[:, DEV:]], axis=0)
         buf_ref[pl.ds(i, DEV, stride=BLK), :] = rows.T
     out_ref[...] = buf_ref[...].astype(BF)
@@ -138,9 +149,15 @@
 
 
 def stack_kernel(
-    in_ref, mask_ref, rot_ref, eh_ref, el_ref, sign_ref, dh_ref, dl_ref, out_ref,
-    buf_ref, f_ref, acc_ref, v_ref,
+    in_ref, mask_ref, rot_ref, eh_ref, el_ref, sign_ref, dh_far, dl_far, out_ref,
+    buf_ref, f_ref, acc_ref, v_ref, dh_ref, dl_ref, sems,
 ):
+    tables = (
+        pltpu.make_async_copy(dh_far, dh_ref, sems.at[0]),
+        pltpu.make_async_copy(dl_far, dl_ref, sems.at[1]),
+    )
+    for table in tables:
+        table.start()
     buf_ref[...] = in_ref[...].astype(F32)
     pieces = [buf_ref[pl.ds(t, DEV, stride=8), :].T.astype(BF) for t in range(8)]
     rows = []
@@ -191,23 +208,27 @@
             v_ref[pl.ds(t * DEV + j, BLK, stride=LAGS), :] = v_re[:, t * DEV : (t + 1) * DEV]
             v_ref[pl.ds((4 + t) * DEV + j, BLK, stride=LAGS), :] = v_im[:, t * DEV : (t + 1) * DEV]
     v_hi, v_lo = split(jnp.concatenate([v_ref[t * DEV : (t + 1) * DEV] for t in range(8)], axis=1))
+    for table in tables:
+        table.wait()
     stacked = dot(v_hi, dh_ref[...]) + dot(v_hi, dl_ref[...]) + dot(v_lo, dh_ref[...])
+    row = lax.broadcasted_iota(jnp.int32, (8, DEV), 0) < 4
+    low = lax.broadcasted_iota(jnp.int32, (8, DEV), 1) < 64
     for delta in range(BLK):
-        for w in range(4):
-            ahead = stacked[8 * delta : 8 * delta + 8, (w // 2) * DEV : (w // 2 + 1) * DEV]
-            behind = stacked[8 * delta : 8 * delta + 8, 256 + (w // 2) * DEV : 256 + (w // 2 + 1) * DEV]
-            to = 64 + 4 * delta + w
-            out_ref[8 * to : 8 * to + 8, :] = ahead.astype(out_ref.dtype)
-            to = 4 * (BLK - 1 - delta) + w
-            out_ref[8 * to : 8 * to + 8, :] = behind.astype(out_ref.dtype)
+        for t in range(4):
+            tile = stacked[8 * delta : 8 * delta + 8, t * DEV : (t + 1) * DEV]
+            pair = jnp.where(row == low, tile, pltpu.roll(pltpu.roll(tile, 4, 0), 64, 1))
+            to = 64 + 4 * delta if t < 2 else 4 * (BLK - 1 - delta)
+            at = 4 * (to + 2 * (t % 2))
+            out_ref[at : at + 8, :] = pair.astype(BF)
 
 
 def total_kernel(in_ref, place_ref, scale_ref, out_ref):
-    total = jnp.sum(in_ref[...].astype(F32), axis=0)
-    rolled = jnp.where(place_ref[1] == 1, pltpu.roll(total, 64, 1), total)
-    flipped = jnp.concatenate([rolled[7 - j : 8 - j] for j in range(LAGS)], axis=0)
-    out = jnp.where(place_ref[0] == 1, flipped, rolled)
-    out_ref[...] = out[:, :64] * scale_ref[...]
+    total = jnp.sum(in_ref[...].astype(F32).reshape(DEV // 2, 8, DEV), axis=0)
+    total = total + pltpu.roll(total, 4, 0)
+    low = lax.broadcasted_iota(jnp.int32, (8, DEV), 0) < 4
+    lags = jnp.where(low, total, pltpu.roll(total, 64, 1))[:, :64]
+    flipped = jnp.concatenate([lags[7 - j : 8 - j] for j in range(LAGS)], axis=0)
+    out_ref[...] = jnp.where(place_ref[0] == 1, flipped, lags) * scale_ref[...]
 
 
 def pair_counts(mask, columns):
@@ -230,6 +251,7 @@
 
 VM = pl.BlockSpec(memory_space=pltpu.VMEM)
 SM = pl.BlockSpec(memory_space=pltpu.SMEM)
+LIMIT = pltpu.CompilerParams(vmem_limit_bytes=24 * 1024 * 1024)
 
 
 def exchange(x, rows):
@@ -242,9 +264,14 @@
     packed = pl.pallas_call(
         pack_kernel,
         out_shape=jax.ShapeDtypeStruct((BLK * DEV, DEV), BF),
-        in_specs=[VM],
+        in_specs=[pl.BlockSpec(memory_space=pltpu.HBM)],
         out_specs=VM,
-        scratch_shapes=[pltpu.VMEM((BLK * DEV, DEV), F32)],
+        compiler_params=LIMIT,
+        scratch_shapes=[
+            pltpu.VMEM((ROWS, C), F32),
+            pltpu.VMEM((BLK * DEV, DEV), F32),
+            pltpu.SemaphoreType.DMA((4,)),
+        ],
     )(raw)
     series = exchange(packed, BLK).reshape(BLK * DEV, DEV)
     stage1, twiddle, stage2 = time_tables()
@@ -253,6 +280,7 @@
         out_shape=jax.ShapeDtypeStruct((8 * DEV, DEV), BF),
         in_specs=[VM] * 6,
         out_specs=VM,
+        compiler_params=LIMIT,
         scratch_shapes=[pltpu.VMEM((BLK * DEV, DEV), F32), pltpu.VMEM((8, DEV, DEV), F32)],
     )(series, stage1, twiddle, stage2, window_table(), taper_table())
     banded = exchange(white, 8).reshape(8 * DEV, DEV)
@@ -261,25 +289,30 @@
     rotation = jnp.stack([jnp.cos(angle), jnp.sin(angle)])
     parts = pl.pallas_call(
         stack_kernel,
-        out_shape=jax.ShapeDtypeStruct((8 * DEV, DEV), BF),
-        in_specs=[VM, SM, SM] + [VM] * 5,
+        out_shape=jax.ShapeDtypeStruct((4 * DEV, DEV), BF),
+        in_specs=[VM, SM, SM] + [VM] * 3 + [pl.BlockSpec(memory_space=pltpu.HBM)] * 2,
         out_specs=VM,
+        compiler_params=LIMIT,
         scratch_shapes=[
             pltpu.VMEM((8 * DEV, DEV), F32),
             pltpu.VMEM((BLK * J2, 2 * Q), F32),
             pltpu.VMEM((BLK * J2, 2 * Q), F32),
             pltpu.VMEM((8 * DEV, DEV), F32),
+            pltpu.VMEM((2 * Q, Q), BF),
+            pltpu.VMEM((2 * Q, Q), BF),
+            pltpu.SemaphoreType.DMA((2,)),
         ],
     )(banded, mask.astype(F32), rotation, *channel_table(), sign_table(), *offset_table())
-    shares = exchange(parts, 8)
+    shares = exchange(parts, 4).reshape(4 * DEV, DEV)
     columns = device * 64 + lax.iota(jnp.int32, 64)
     scale = stack_scale(pair_counts(mask, columns))[None, :]
-    place = jnp.stack([(device < 64).astype(jnp.int32), device % 2])
+    place = (device < 64).astype(jnp.int32)[None]
     return pl.pallas_call(
         total_kernel,
         out_shape=jax.ShapeDtypeStruct((LAGS, 64), F32),
         in_specs=[VM, SM, VM],
         out_specs=VM,
+        compiler_params=LIMIT,
     )(shares, place, scale)
 
 

time: 73.3 us -> 69.1 us (0.943)
  Pallas kernels: 14.4 us -> 9.85 us
  other arithmetic: 2.66 us -> 0.34 us
  waiting for transfers between devices: 33.2 us -> 34.9 us
  local copies, waits for them, and re-layouts: 2.9 us -> 3.73 us
    all_to_all x3, waiting for transfers between devices: 33.2 us -> 34.9 us  [exchange(): lax.all_to_all(x, ('blk', 'lag'), split_axis=0, concat_axis=0, tiled=True)]
    pallas_call x1, Pallas kernels: 6.82 us -> 5.5 us  [on_device(): pl.pallas_call(stack_kernel, out_shape=jax.ShapeDtypeStruct((4 * DEV, DEV...]
    pallas_call x1, Pallas kernels: 3.38 us -> 2.08 us  [on_device(): pl.pallas_call(spectra_kernel, out_shape=jax.ShapeDtypeStruct((8 * DEV, D...]
    pallas_call x1, Pallas kernels: 1.76 us -> 0.74 us  [on_device(): pl.pallas_call(total_kernel, out_shape=jax.ShapeDtypeStruct((LAGS, 64), F...]
    pallas_call x1, Pallas kernels: 2.47 us -> 1.54 us  [on_device(): pl.pallas_call(pack_kernel, out_shape=jax.ShapeDtypeStruct((BLK * DEV, DE...]
    unnamed x8 -> x24, local copies, waits for them, and re-layouts: 2.9 us -> 3.73 us
  transfers between devices with their start and end apart: 3 -> 3, of which waited for: 3 -> 3; matrix products, arithmetic and copies ran while one was open for 4% -> 0% of each run, Pallas kernels for 0% -> 0%
where the time goes in v2:
time: 69.1 us; the launch traced here: 68.7 us
  waiting for transfers between devices  34.9 us (51%)
  starting transfers between devices  19.7 us (29%)
  Pallas kernels  9.85 us (14%)
  local copies, waits for them, and re-layouts  3.73 us (5%)
    all_to_all x3, waiting for transfers between devices, exchange(): lax.all_to_all(x, ('blk', 'lag'), split_axis=0, concat_axis=0, tiled=True)  34.9 us
    all_to_all x3, starting transfers between devices, exchange(): lax.all_to_all(x, ('blk', 'lag'), split_axis=0, concat_axis=0, tiled=True)  19.7 us
    pallas_call x1, Pallas kernels, on_device(): pl.pallas_call(stack_kernel, out_shape=jax.ShapeDtypeStruct((4 * DEV, DEV...  5.5 us
    unnamed x24, local copies, waits for them, and re-layouts  3.73 us
    pallas_call x1, Pallas kernels, on_device(): pl.pallas_call(spectra_kernel, out_shape=jax.ShapeDtypeStruct((8 * DEV, D...  2.08 us
    pallas_call x1, Pallas kernels, on_device(): pl.pallas_call(pack_kernel, out_shape=jax.ShapeDtypeStruct((BLK * DEV, DE...  1.54 us
  transfers between devices with their start and end apart: 3, of which 3 were waited for; matrix products, arithmetic and copies ran while one was open for 0% of the time, Pallas kernels for 0%

profile of v2, /device:TPU:1, one launch (start us, length us, event | category | flops | bytes accessed | tf_op | source)
XLA Modules:
  0.0 68.7 jit_solution(6913987356816917681)
XLA Ops:
  0.0 1.2 %copy-done.4 = f32[64,4096]{1,0:T(8,128)S(1)} copy-done((f32[64,4096]{1,0:T(8,128)S(1)}, f32[64,4096]{1,0:T(8,128)}, u32[]{:S(2)}) %copy-start.4) | copy-done | bytes 1048600
  1.2 1.5 %shard_map.118 = bf16[2048,128]{1,0:T(8,128)(2,1)} custom-call(f32[64,4096]{1,0:T(8,128)S(1)} %copy-done.4), custom_call_target="tpu_custom_call" | custom-call | tf_op jit(solution)/shard_map/pallas_call | solution.py:264
  2.8 0.0 copy-start.5
  2.8 0.0 copy-start.6
  2.8 0.0 copy-start.7
  2.8 0.0 copy-start.8
  2.8 0.0 copy-start.9
  2.8 11.5 %all-to-all-start = ((bf16[128,16,128]{2,1,0:T(8,128)(2,1)}), bf16[128,16,128]{2,1,0:T(8,128)(2,1)S(1)}, u32[]{:S(2)}, u32[]{:S(2)}) async-start(bf16[128,16,128]{2,1,0:T(8,128)(2,1)} %bitcast), calls=%async_computation | async-start | bytes 1048576 | tf_op jit(solution)/shard_map/all_to_all | solution.py:259
  14.4 0.1 fusion.3
  14.5 13.9 %all-to-all-done = bf16[128,16,128]{2,1,0:T(8,128)(2,1)S(1)} async-done(((bf16[128,16,128]{2,1,0:T(8,128)(2,1)}), bf16[128,16,128]{2,1,0:T(8,128)(2,1)S(1)}, u32[]{:S(2)}, u32[]{:S(2)}) %all-to-all-start) | async-done | bytes 524320 | tf_op jit(solution)/shard_map/all_to_all | solution.py:259
  28.4 0.0 copy-start
  28.4 2.1 %shard_map.119 = bf16[1024,128]{1,0:T(8,128)(2,1)} custom-call(bf16[2048,128]{1,0:T(8,128)(2,1)S(1)} %bitcast.9, bf16[256,128]{1,0:T(8,128)(2,1)S(1)} %copy-done.8, f32[2,128,128]{2,1,0:T(8,128)S(1)} %copy-done.6, bf16[1024,256]{1,0:T(8,128)(2,1)S(1)} %copy-done.5, bf16[128,384]{1,0:T(8,128)(2,1)S(1)} %copy-done.7, f32[128,128]{1,0:T(8,128)S(1)} %copy-done.9), custom_call_target="tpu_custom_call" | custom-call | tf_op jit(solution)/shard_map/pallas_call | solution.py:278
  30.5 4.0 %all-to-all-start.1 = ((bf16[128,8,128]{2,1,0:T(8,128)(2,1)}), bf16[128,8,128]{2,1,0:T(8,128)(2,1)S(1)}, u32[]{:S(2)}, u32[]{:S(2)}) async-start(bf16[128,8,128]{2,1,0:T(8,128)(2,1)} %bitcast.2), calls=%async_computation.1 | async-start | bytes 524288 | tf_op jit(solution)/shard_map/all_to_all | solution.py:259
  34.6 0.0 copy-start.10
  34.6 0.1 select_reduce_fusion
  34.7 0.1 multiply_reduce_fusion
  34.8 11.0 %all-to-all-done.1 = bf16[128,8,128]{2,1,0:T(8,128)(2,1)S(1)} async-done(((bf16[128,8,128]{2,1,0:T(8,128)(2,1)}), bf16[128,8,128]{2,1,0:T(8,128)(2,1)S(1)}, u32[]{:S(2)}, u32[]{:S(2)}) %all-to-all-start.1) | async-done | bytes 262176 | tf_op jit(solution)/shard_map/all_to_all | solution.py:259
  45.8 0.0 copy-start.2
  45.8 1.2 %copy-done.2 = bf16[1024,512]{1,0:T(8,128)(2,1)S(1)} copy-done((bf16[1024,512]{1,0:T(8,128)(2,1)S(1)}, bf16[1024,512]{1,0:T(8,128)(2,1)}, u32[]{:S(2)}) %copy-start.2) | copy-done | bytes 1048600
  47.1 1.2 %copy-done.3 = bf16[1024,512]{1,0:T(8,128)(2,1)S(1)} copy-done((bf16[1024,512]{1,0:T(8,128)(2,1)S(1)}, bf16[1024,512]{1,0:T(8,128)(2,1)}, u32[]{:S(2)}) %copy-start.3) | copy-done | bytes 1048600
  48.3 5.5 %shard_map.120 = bf16[512,128]{1,0:T(8,128)(2,1)} custom-call(bf16[1024,128]{1,0:T(8,128)(2,1)S(1)} %bitcast.10, f32[16,16]{1,0:T(8,128)S(1)} %convert_element_type.30.mask_ref, f32[2,8]{1,0:T(2,128)S(1)} %pad_maximum_fusion.rot_ref, bf16[512,1024]{1,0:T(8,128)(2,1)S(1)} %copy-done, bf16[512,1024]{1,0:T(8,128)(2,1)S(1)} %copy-done.1, ...), custom_call_target="tpu_custom_call" | custom-call | tf_op jit(solution)/shard_map/pallas_call | solution.py:290
  53.8 4.2 %all-to-all-start.2 = ((bf16[128,4,128]{2,1,0:T(4,128)(2,1)}), bf16[128,4,128]{2,1,0:T(4,128)(2,1)S(1)}, u32[]{:S(2)}, u32[]{:S(2)}) async-start(bf16[128,4,128]{2,1,0:T(4,128)(2,1)} %bitcast.4), calls=%async_computation.2 | async-start | bytes 262144 | tf_op jit(solution)/shard_map/all_to_all | solution.py:259
  58.0 10.0 %all-to-all-done.2 = bf16[128,4,128]{2,1,0:T(4,128)(2,1)S(1)} async-done(((bf16[128,4,128]{2,1,0:T(4,128)(2,1)}), bf16[128,4,128]{2,1,0:T(4,128)(2,1)S(1)}, u32[]{:S(2)}, u32[]{:S(2)}) %all-to-all-start.2) | async-done | bytes 131104 | tf_op jit(solution)/shard_map/all_to_all | solution.py:259
  68.0 0.7 %shard_map.121 = f32[8,64]{1,0:T(8,128)} custom-call(bf16[512,128]{1,0:T(8,128)(2,1)S(1)} %bitcast.11, s32[1]{0:T(128)} %bitcast.6.place_ref, f32[1,64]{1,0:T(1,128)S(1)} %rsqrt_bitcast_fusion.scale_ref), custom_call_target="tpu_custom_call" | custom-call | tf_op jit(solution)/shard_map/pallas_call | solution.py:310
  (20 shorter events, 0.1 us)
Async XLA Ops:
  0.0 1.2 %copy-start.4 = (f32[64,4096]{1,0:T(8,128)S(1)}, f32[64,4096]{1,0:T(8,128)}, u32[]{:S(2)}) copy-start(f32[64,4096]{1,0:T(8,128)} %raw_ref.1) | copy-start | bytes 3145732
  2.8 25.6 %copy-start.5 = (bf16[1024,256]{1,0:T(8,128)(2,1)S(1)}, bf16[1024,256]{1,0:T(8,128)(2,1)}, u32[]{:S(2)}) copy-start(bf16[1024,256]{1,0:T(8,128)(2,1)} %constant.76.clone.s2_ref) | copy-start | bytes 1572868
  2.8 25.6 %copy-start.6 = (f32[2,128,128]{2,1,0:T(8,128)S(1)}, f32[2,128,128]{2,1,0:T(8,128)}, u32[]{:S(2)}) copy-start(f32[2,128,128]{2,1,0:T(8,128)} %constant.75.clone.tw_ref) | copy-start | bytes 393220
  2.8 25.6 %copy-start.7 = (bf16[128,384]{1,0:T(8,128)(2,1)S(1)}, bf16[128,384]{1,0:T(8,128)(2,1)}, u32[]{:S(2)}) copy-start(bf16[128,384]{1,0:T(8,128)(2,1)} %constant.77.clone.win_ref) | copy-start | bytes 294916
  2.8 25.6 %copy-start.8 = (bf16[256,128]{1,0:T(8,128)(2,1)S(1)}, bf16[256,128]{1,0:T(8,128)(2,1)}, u32[]{:S(2)}) copy-start(bf16[256,128]{1,0:T(8,128)(2,1)} %constant.74.clone.s1_ref) | copy-start | bytes 196612
  2.8 25.6 %copy-start.9 = (f32[128,128]{1,0:T(8,128)S(1)}, f32[128,128]{1,0:T(8,128)}, u32[]{:S(2)}) copy-start(f32[128,128]{1,0:T(8,128)} %constant.78.clone.taper_ref) | copy-start | bytes 196612
  2.8 25.5 %all-to-all-start = ((bf16[128,16,128]{2,1,0:T(8,128)(2,1)}), bf16[128,16,128]{2,1,0:T(8,128)(2,1)S(1)}, u32[]{:S(2)}, u32[]{:S(2)}) async-start(bf16[128,16,128]{2,1,0:T(8,128)(2,1)} %bitcast), calls=%async_computation | async-start | bytes 1048576 | tf_op jit(solution)/shard_map/all_to_all | solution.py:259
  28.4 17.4 %copy-start = (bf16[512,1024]{1,0:T(8,128)(2,1)S(1)}, bf16[512,1024]{1,0:T(8,128)(2,1)}, u32[]{:S(2)}) copy-start(bf16[512,1024]{1,0:T(8,128)(2,1)} %constant.79.clone.eh_ref) | copy-start | bytes 3145732
  28.4 17.4 %copy-start.1 = (bf16[512,1024]{1,0:T(8,128)(2,1)S(1)}, bf16[512,1024]{1,0:T(8,128)(2,1)}, u32[]{:S(2)}) copy-start(bf16[512,1024]{1,0:T(8,128)(2,1)} %constant.80.clone.el_ref) | copy-start | bytes 3145732
  30.5 4.1 %copy-start.11 = (s32[16,16]{1,0:T(8,128)S(1)}, s32[16,16]{1,0:T(8,128)}, u32[]{:S(2)}) copy-start(s32[16,16]{1,0:T(8,128)} %param.13) | copy-start | bytes 3076
  30.5 15.3 %all-to-all-start.1 = ((bf16[128,8,128]{2,1,0:T(8,128)(2,1)}), bf16[128,8,128]{2,1,0:T(8,128)(2,1)S(1)}, u32[]{:S(2)}, u32[]{:S(2)}) async-start(bf16[128,8,128]{2,1,0:T(8,128)(2,1)} %bitcast.2), calls=%async_computation.1 | async-start | bytes 524288 | tf_op jit(solution)/shard_map/all_to_all | solution.py:259
  34.6 11.3 %copy-start.10 = (bf16[32,256]{1,0:T(8,128)(2,1)S(1)}, bf16[32,256]{1,0:T(8,128)(2,1)}, u32[]{:S(2)}) copy-start(bf16[32,256]{1,0:T(8,128)(2,1)} %constant.81.clone.sign_ref) | copy-start | bytes 49156
  45.8 1.2 %copy-start.2 = (bf16[1024,512]{1,0:T(8,128)(2,1)S(1)}, bf16[1024,512]{1,0:T(8,128)(2,1)}, u32[]{:S(2)}) copy-start(bf16[1024,512]{1,0:T(8,128)(2,1)} %constant.82.clone.dh_far) | copy-start | bytes 3145732
  47.1 1.2 %copy-start.3 = (bf16[1024,512]{1,0:T(8,128)(2,1)S(1)}, bf16[1024,512]{1,0:T(8,128)(2,1)}, u32[]{:S(2)}) copy-start(bf16[1024,512]{1,0:T(8,128)(2,1)} %constant.83.clone.dl_far) | copy-start | bytes 3145732
  53.8 14.2 %all-to-all-start.2 = ((bf16[128,4,128]{2,1,0:T(4,128)(2,1)}), bf16[128,4,128]{2,1,0:T(4,128)(2,1)S(1)}, u32[]{:S(2)}, u32[]{:S(2)}) async-start(bf16[128,4,128]{2,1,0:T(4,128)(2,1)} %bitcast.4), calls=%async_computation.2 | async-start | bytes 262144 | tf_op jit(solution)/shard_map/all_to_all | solution.py:259

commit v3 on v2

--- a/solution.py
+++ b/solution.py
@@ -77,21 +77,12 @@
 
 def channel_table():
     c, s = cs(np.arange(256)[:, None] * np.arange(Q)[None], Q)
-    return np_split(np.block([[c, -s], [s, c]]))
+    return np_split(np.concatenate([c, s], axis=1))
 
 
 def offset_table():
-    m = np.concatenate([np.arange(256), 256 - np.arange(256)])
-    c, s = cs(np.arange(Q)[:, None] * m[None], Q)
+    c, s = cs(np.arange(Q)[:, None] * np.arange(256)[None], Q)
     return np_split(np.concatenate([c, s], axis=0) / Q)
-
-
-def sign_table():
-    table = np.zeros((32, 256), np.float32)
-    for delta in range(BLK):
-        for j2 in range(J2):
-            table[(j2 % 2) * 16 + delta, delta * J2 + j2] = 1.0 if j2 % 4 < 2 else -1.0
-    return table.astype(jnp.bfloat16)
 
 
 def pack_kernel(raw_ref, out_ref, raw_buf, buf_ref, sems):
@@ -149,76 +140,94 @@
 
 
 def stack_kernel(
-    in_ref, mask_ref, rot_ref, eh_ref, el_ref, sign_ref, dh_far, dl_far, out_ref,
-    buf_ref, f_ref, acc_ref, v_ref, dh_ref, dl_ref, sems,
+    in_ref, mask_ref, rot_ref, eh_ref, el_ref, dh_ref, dl_ref, out_ref,
+    buf_ref, f_ref, acc_ref, v_ref,
 ):
-    tables = (
-        pltpu.make_async_copy(dh_far, dh_ref, sems.at[0]),
-        pltpu.make_async_copy(dl_far, dl_ref, sems.at[1]),
-    )
-    for table in tables:
-        table.start()
     buf_ref[...] = in_ref[...].astype(F32)
     pieces = [buf_ref[pl.ds(t, DEV, stride=8), :].T.astype(BF) for t in range(8)]
     rows = []
-    for i in range(BLK):
-        g, s = i // 4, i % 4
-        tiles = [
-            pieces[4 * part + g][(2 * s + h) * J2 : (2 * s + h + 1) * J2]
-            for part in range(2)
-            for h in range(2)
-        ]
-        rows.append(jnp.concatenate(tiles, axis=1))
+    for part in range(2):
+        for i in range(BLK):
+            g, s = i // 4, i % 4
+            tiles = [
+                pieces[4 * part + g][(2 * s + h) * J2 : (2 * s + h + 1) * J2] for h in range(2)
+            ]
+            rows.append(jnp.concatenate(tiles, axis=1))
     white = jnp.concatenate(rows, axis=0)
-    f_ref[...] = dot(white, eh_ref[...]) + dot(white, el_ref[...])
-    acc_ref[FAR * J2 :, :] = jnp.zeros((J2, 2 * Q), F32)
+    product = dot(white, eh_ref[...]) + dot(white, el_ref[...])
+    half = BLK * J2
+    f_re = product[:half, :Q] + product[half:, Q:]
+    f_im = product[half:, :Q] - product[:half, Q:]
+    for part, value in enumerate((f_re, f_im)):
+        for k in range(2 * BLK):
+            for t in range(4):
+                f_ref[pl.ds(part * 1024 + 32 * k + t, 8, stride=4), :] = value[
+                    8 * k : 8 * k + 8, t * DEV : (t + 1) * DEV
+                ]
+    acc_ref[...] = jnp.zeros_like(acc_ref)
 
     def unit(u, carry):
-        half = pl.multiple_of((u // 4) * 8, 8)
-        col = pl.multiple_of((u % 4) * DEV, DEV)
-        at = lambda i: pl.ds(i * J2 + half, 8)
-        res, ims = pl.ds(col, DEV), pl.ds(col + Q, DEV)
-        f_re = [f_ref[at(i), res] for i in range(BLK)]
-        f_im = [f_ref[at(i), ims] for i in range(BLK)]
+        at = lambda i, part: pl.ds(pl.multiple_of(part * 1024 + i * 64 + u * 8, 8), 8)
+        re = [f_ref[at(i, 0), :] for i in range(BLK)]
+        im = [f_ref[at(i, 1), :] for i in range(BLK)]
         for delta in range(FAR):
-            sum_re = sum_im = jnp.zeros((8, DEV), F32)
+            sum_re = sum_im = None
             for i in range(BLK - delta):
-                j, live = i + delta, mask_ref[i, i + delta]
-                a_re, a_im = f_re[i] * live, f_im[i] * live
-                sum_re = sum_re + (a_re * f_re[j] + a_im * f_im[j])
-                sum_im = sum_im + (a_im * f_re[j] - a_re * f_im[j])
-            acc_ref[at(delta), res] = sum_re
-            acc_ref[at(delta), ims] = sum_im
+                j = i + delta
+                live = mask_ref[pl.ds(i * BLK + j, 8, stride=0), :]
+                a_re, a_im = re[i] * live, im[i] * live
+                term = a_re * re[j] + a_im * im[j]
+                sum_re = term if sum_re is None else sum_re + term
+                if delta:
+                    term = a_im * re[j] - a_re * im[j]
+                    sum_im = term if sum_im is None else sum_im + term
+            acc_ref[2 * delta] = sum_re - acc_ref[2 * delta]
+            if delta:
+                acc_ref[2 * delta + 1] = sum_im - acc_ref[2 * delta + 1]
         return carry
 
-    lax.fori_loop(0, 8, unit, 0)
-    hi, lo = split(acc_ref[...])
-    sums = dot(sign_ref[...], hi) + dot(sign_ref[...], lo)
-    far = lax.broadcasted_iota(jnp.int32, sums.shape, 0) % BLK == BLK - 1
-    odd = lax.broadcasted_iota(jnp.int32, sums.shape, 1) % 2 == 1
-    nearer = jnp.where(far, 0.0, pltpu.roll(sums, 2 * BLK - 1, 0))
-    sums = sums + jnp.where(odd, -nearer, nearer)
-    a_re, a_im, b_re, b_im = sums[:16, :Q], sums[:16, Q:], sums[16:, :Q], sums[16:, Q:]
-    quarter = ((a_re - b_im, a_im + b_re), (a_re + b_im, a_im - b_re))
-    for j in range(LAGS):
-        g_re, g_im = quarter[0 if (2 * j - 7) % 4 == 1 else 1]
-        c, s = rot_ref[0, j], rot_ref[1, j]
-        v_re, v_im = c * g_re - s * g_im, c * g_im + s * g_re
-        for t in range(4):
-            v_ref[pl.ds(t * DEV + j, BLK, stride=LAGS), :] = v_re[:, t * DEV : (t + 1) * DEV]
-            v_ref[pl.ds((4 + t) * DEV + j, BLK, stride=LAGS), :] = v_im[:, t * DEV : (t + 1) * DEV]
-    v_hi, v_lo = split(jnp.concatenate([v_ref[t * DEV : (t + 1) * DEV] for t in range(8)], axis=1))
-    for table in tables:
-        table.wait()
+    lax.fori_loop(0, J2 // 2, unit, 0)
+    first = lax.broadcasted_iota(jnp.int32, (8, DEV), 0) < 4
+    lane = lax.broadcasted_iota(jnp.int32, (8, DEV), 1)
+    parity = jnp.where(lane % 2 == 1, -1.0, 1.0)
+    turn = jnp.where(first, -1.0, 1.0)
+    for delta in range(BLK):
+        if delta < FAR:
+            x_re, x_im = acc_ref[2 * delta], acc_ref[2 * delta + 1]
+            if delta + 1 < FAR:
+                x_re = x_re + parity * acc_ref[2 * delta + 2]
+                x_im = x_im + parity * acc_ref[2 * delta + 3]
+            s_re, s_im = pltpu.roll(x_re, 4, 0), pltpu.roll(x_im, 4, 0)
+            g_re = jnp.where(first, x_re, s_re) + turn * jnp.where(first, s_im, x_im)
+            g_im = jnp.where(first, x_im, s_im) - turn * jnp.where(first, s_re, x_re)
+        for u in range(4):
+            at = pl.ds((delta * 4 + u) * 8, 8)
+            to = pl.ds(512 + (delta * 4 + u) * 8, 8)
+            if delta < FAR:
+                c, s = rot_ref[0, u], rot_ref[1, u]
+                v_ref[at, :] = s * g_im - c * g_re
+                v_ref[to, :] = -(c * g_im) - s * g_re
+            else:
+                v_ref[at, :] = jnp.zeros((8, DEV), F32)
+                v_ref[to, :] = jnp.zeros((8, DEV), F32)
+    shifted = [v_ref[pl.ds(512 * c + t, DEV, stride=4), :] for c in range(2) for t in range(4)]
+    v_hi, v_lo = split(jnp.concatenate(shifted, axis=1))
     stacked = dot(v_hi, dh_ref[...]) + dot(v_hi, dl_ref[...]) + dot(v_lo, dh_ref[...])
-    row = lax.broadcasted_iota(jnp.int32, (8, DEV), 0) < 4
-    low = lax.broadcasted_iota(jnp.int32, (8, DEV), 1) < 64
+    left, right = stacked[:, :DEV], stacked[:, DEV:]
+    last = lax.broadcasted_iota(jnp.int32, (DEV, DEV), 1) == DEV - 1
+    left1, right1 = pltpu.roll(left, DEV - 1, 1), pltpu.roll(right, DEV - 1, 1)
+    beyond = jnp.concatenate([left1[8:], jnp.zeros((8, DEV), F32)], axis=0)
+    behind = (jnp.where(last, right1, left1), jnp.where(last, beyond, right1))
+    same = first == (lane < 64)
     for delta in range(BLK):
-        for t in range(4):
-            tile = stacked[8 * delta : 8 * delta + 8, t * DEV : (t + 1) * DEV]
-            pair = jnp.where(row == low, tile, pltpu.roll(pltpu.roll(tile, 4, 0), 64, 1))
-            to = 64 + 4 * delta if t < 2 else 4 * (BLK - 1 - delta)
-            at = 4 * (to + 2 * (t % 2))
+        for t in range(2):
+            tile = (left, right)[t][8 * delta : 8 * delta + 8]
+            pair = jnp.where(same, tile, pltpu.roll(pltpu.roll(tile, 4, 0), 64, 1))
+            at = 4 * (64 + 4 * delta + 2 * t)
+            out_ref[at : at + 8, :] = pair.astype(BF)
+            tile = behind[t][8 * delta : 8 * delta + 8]
+            pair = jnp.where(same, pltpu.roll(tile, 64, 1), pltpu.roll(tile, 4, 0))
+            at = 4 * (4 * (BLK - 1 - delta) + 2 - 2 * t)
             out_ref[at : at + 8, :] = pair.astype(BF)
 
 
@@ -226,9 +235,12 @@
     total = jnp.sum(in_ref[...].astype(F32).reshape(DEV // 2, 8, DEV), axis=0)
     total = total + pltpu.roll(total, 4, 0)
     low = lax.broadcasted_iota(jnp.int32, (8, DEV), 0) < 4
-    lags = jnp.where(low, total, pltpu.roll(total, 64, 1))[:, :64]
+    lags = jnp.where(low, total, pltpu.roll(total, 64, 1))
+    lane = lax.broadcasted_iota(jnp.int32, (8, DEV), 1)
     flipped = jnp.concatenate([lags[7 - j : 8 - j] for j in range(LAGS)], axis=0)
-    out_ref[...] = jnp.where(place_ref[0] == 1, flipped, lags) * scale_ref[...]
+    flipped = jnp.take_along_axis(flipped, (63 - lane) & 127, axis=1)
+    out = jnp.where(place_ref[0] == 1, flipped, lags)
+    out_ref[...] = out[:, :64] * scale_ref[...]
 
 
 def pair_counts(mask, columns):
@@ -266,7 +278,6 @@
         out_shape=jax.ShapeDtypeStruct((BLK * DEV, DEV), BF),
         in_specs=[pl.BlockSpec(memory_space=pltpu.HBM)],
         out_specs=VM,
-        compiler_params=LIMIT,
         scratch_shapes=[
             pltpu.VMEM((ROWS, C), F32),
             pltpu.VMEM((BLK * DEV, DEV), F32),
@@ -286,23 +297,22 @@
     banded = exchange(white, 8).reshape(8 * DEV, DEV)
     odd = 2 * lax.iota(jnp.int32, LAGS) - (LAGS - 1)
     angle = jnp.mod(odd * (K0 + device), Q).astype(F32) * (2 * math.pi / Q)
-    rotation = jnp.stack([jnp.cos(angle), jnp.sin(angle)])
+    spread = lambda x: jnp.broadcast_to(x.reshape(4, 2, 1, 1), (4, 2, 4, DEV)).reshape(4, 8, DEV)
+    rotation = jnp.stack([spread(jnp.cos(angle)), spread(jnp.sin(angle))])
+    live = jnp.broadcast_to(mask.astype(F32).reshape(BLK * BLK, 1), (BLK * BLK, DEV))
     parts = pl.pallas_call(
         stack_kernel,
         out_shape=jax.ShapeDtypeStruct((4 * DEV, DEV), BF),
-        in_specs=[VM, SM, SM] + [VM] * 3 + [pl.BlockSpec(memory_space=pltpu.HBM)] * 2,
+        in_specs=[VM] * 7,
         out_specs=VM,
         compiler_params=LIMIT,
         scratch_shapes=[
             pltpu.VMEM((8 * DEV, DEV), F32),
-            pltpu.VMEM((BLK * J2, 2 * Q), F32),
-            pltpu.VMEM((BLK * J2, 2 * Q), F32),
+            pltpu.VMEM((2048, DEV), F32),
+            pltpu.VMEM((2 * FAR, 8, DEV), F32),
             pltpu.VMEM((8 * DEV, DEV), F32),
-            pltpu.VMEM((2 * Q, Q), BF),
-            pltpu.VMEM((2 * Q, Q), BF),
-            pltpu.SemaphoreType.DMA((2,)),
         ],
-    )(banded, mask.astype(F32), rotation, *channel_table(), sign_table(), *offset_table())
+    )(banded, live, rotation, *channel_table(), *offset_table())
     shares = exchange(parts, 4).reshape(4 * DEV, DEV)
     columns = device * 64 + lax.iota(jnp.int32, 64)
     scale = stack_scale(pair_counts(mask, columns))[None, :]

time: 69.1 us -> 64.7 us (0.936)
  local copies, waits for them, and re-layouts: 3.73 us -> 0.68 us
  Pallas kernels: 9.85 us -> 9.14 us
    unnamed x24 -> x20, local copies, waits for them, and re-layouts: 3.73 us -> 0.06 us
    pallas_call x1, Pallas kernels: 5.5 us -> 3.84 us  [on_device(): pl.pallas_call(stack_kernel, out_shape=jax.ShapeDtypeStruct((4 * DEV, DEV...]
    pallas_call x1, Pallas kernels: 1.54 us -> 2.41 us  [on_device(): pl.pallas_call(pack_kernel, out_shape=jax.ShapeDtypeStruct((BLK * DEV, DE...]
  transfers between devices with their start and end apart: 3 -> 3, of which waited for: 3 -> 3; matrix products, arithmetic and copies ran while one was open for 0% -> 1% of each run, Pallas kernels for 0% -> 0%
where the time goes in v3:
time: 64.7 us; the launch traced here: 64.4 us
  waiting for transfers between devices  34.4 us (53%)
  starting transfers between devices  19.7 us (30%)
  Pallas kernels  9.14 us (14%)
  local copies, waits for them, and re-layouts  0.68 us (1%)
    all_to_all x3, waiting for transfers between devices, exchange(): lax.all_to_all(x, ('blk', 'lag'), split_axis=0, concat_axis=0, tiled=True)  34.4 us
    all_to_all x3, starting transfers between devices, exchange(): lax.all_to_all(x, ('blk', 'lag'), split_axis=0, concat_axis=0, tiled=True)  19.7 us
    pallas_call x1, Pallas kernels, on_device(): pl.pallas_call(stack_kernel, out_shape=jax.ShapeDtypeStruct((4 * DEV, DEV...  3.84 us
    pallas_call x1, Pallas kernels, on_device(): pl.pallas_call(pack_kernel, out_shape=jax.ShapeDtypeStruct((BLK * DEV, DE...  2.41 us
    pallas_call x1, Pallas kernels, on_device(): pl.pallas_call(spectra_kernel, out_shape=jax.ShapeDtypeStruct((8 * DEV, D...  2.09 us
  transfers between devices with their start and end apart: 3, of which 3 were waited for; matrix products, arithmetic and copies ran while one was open for 1% of the time, Pallas kernels for 0%

profile of v3, /device:TPU:1, one launch (start us, length us, event | category | flops | bytes accessed | tf_op | source)
XLA Modules:
  0.0 64.4 jit_solution(13842119119980390504)
XLA Ops:
  0.0 2.4 %shard_map.109 = bf16[2048,128]{1,0:T(8,128)(2,1)} custom-call(f32[64,4096]{1,0:T(8,128)} %raw_ref.1), custom_call_target="tpu_custom_call" | custom-call | tf_op jit(solution)/shard_map/pallas_call | solution.py:276
  2.4 0.0 copy-start
  2.4 0.0 copy-start.6
  2.4 0.0 copy-start.7
  2.5 11.5 %all-to-all-start = ((bf16[128,16,128]{2,1,0:T(8,128)(2,1)}), bf16[128,16,128]{2,1,0:T(8,128)(2,1)S(1)}, u32[]{:S(2)}, u32[]{:S(2)}) async-start(bf16[128,16,128]{2,1,0:T(8,128)(2,1)} %bitcast.12), calls=%async_computation | async-start | bytes 1048576 | tf_op jit(solution)/shard_map/all_to_all | solution.py:271
  14.0 0.1 fusion.3
  14.1 0.1 broadcast_in_dim.44
  14.1 0.1 broadcast_in_dim.45
  14.2 0.1 broadcast_in_dim.41
  14.3 0.1 broadcast_in_dim.42
  14.4 0.1 broadcast_in_dim.46
  14.5 0.1 broadcast_in_dim.43
  14.5 13.5 %all-to-all-done = bf16[128,16,128]{2,1,0:T(8,128)(2,1)S(1)} async-done(((bf16[128,16,128]{2,1,0:T(8,128)(2,1)}), bf16[128,16,128]{2,1,0:T(8,128)(2,1)S(1)}, u32[]{:S(2)}, u32[]{:S(2)}) %all-to-all-start) | async-done | bytes 524320 | tf_op jit(solution)/shard_map/all_to_all | solution.py:271
  28.1 2.1 %shard_map.110 = bf16[1024,128]{1,0:T(8,128)(2,1)} custom-call(bf16[2048,128]{1,0:T(8,128)(2,1)S(1)} %bitcast.9, bf16[256,128]{1,0:T(8,128)(2,1)S(1)} %copy-done.7, f32[2,128,128]{2,1,0:T(8,128)S(1)} %copy-done.5, bf16[1024,256]{1,0:T(8,128)(2,1)S(1)} %copy-done, bf16[128,384]{1,0:T(8,128)(2,1)S(1)} %copy-done.6, f32[128,128]{1,0:T(8,128)S(1)} %copy-done.8), custom_call_target="tpu_custom_call" | custom-call | tf_op jit(solution)/shard_map/pallas_call | solution.py:289
  30.2 4.0 %all-to-all-start.1 = ((bf16[128,8,128]{2,1,0:T(8,128)(2,1)}), bf16[128,8,128]{2,1,0:T(8,128)(2,1)S(1)}, u32[]{:S(2)}, u32[]{:S(2)}) async-start(bf16[128,8,128]{2,1,0:T(8,128)(2,1)} %bitcast.2), calls=%async_computation.1 | async-start | bytes 524288 | tf_op jit(solution)/shard_map/all_to_all | solution.py:271
  34.2 0.1 broadcast_in_dim.39
  34.3 0.1 select_reduce_fusion
  34.5 0.1 multiply_reduce_fusion
  34.6 10.9 %all-to-all-done.1 = bf16[128,8,128]{2,1,0:T(8,128)(2,1)S(1)} async-done(((bf16[128,8,128]{2,1,0:T(8,128)(2,1)}), bf16[128,8,128]{2,1,0:T(8,128)(2,1)S(1)}, u32[]{:S(2)}, u32[]{:S(2)}) %all-to-all-start.1) | async-done | bytes 262176 | tf_op jit(solution)/shard_map/all_to_all | solution.py:271
  45.5 0.1 broadcast_in_dim.40.mask_ref
  45.6 3.8 %shard_map.111 = bf16[512,128]{1,0:T(8,128)(2,1)} custom-call(bf16[1024,128]{1,0:T(8,128)(2,1)S(1)} %bitcast.10, f32[256,128]{1,0:T(8,128)S(1)} %broadcast_in_dim.40.mask_ref, f32[2,4,8,128]{3,2,1,0:T(8,128)S(1)} %pad_maximum_fusion.rot_ref, bf16[256,1024]{1,0:T(8,128)(2,1)S(1)} %copy-done.1, bf16[256,1024]{1,0:T(8,128)(2,1)S(1)} %copy-done.2, ...), custom_call_target="tpu_custom_call" | custom-call | tf_op jit(solution)/shard_map/pallas_call | solution.py:303
  49.5 4.2 %all-to-all-start.2 = ((bf16[128,4,128]{2,1,0:T(4,128)(2,1)}), bf16[128,4,128]{2,1,0:T(4,128)(2,1)S(1)}, u32[]{:S(2)}, u32[]{:S(2)}) async-start(bf16[128,4,128]{2,1,0:T(4,128)(2,1)} %bitcast.4), calls=%async_computation.2 | async-start | bytes 262144 | tf_op jit(solution)/shard_map/all_to_all | solution.py:271
  53.6 10.0 %all-to-all-done.2 = bf16[128,4,128]{2,1,0:T(4,128)(2,1)S(1)} async-done(((bf16[128,4,128]{2,1,0:T(4,128)(2,1)}), bf16[128,4,128]{2,1,0:T(4,128)(2,1)S(1)}, u32[]{:S(2)}, u32[]{:S(2)}) %all-to-all-start.2) | async-done | bytes 131104 | tf_op jit(solution)/shard_map/all_to_all | solution.py:271
  63.6 0.8 %shard_map.112 = f32[8,64]{1,0:T(8,128)} custom-call(bf16[512,128]{1,0:T(8,128)(2,1)S(1)} %bitcast.11, s32[1]{0:T(128)} %bitcast.6.place_ref, f32[1,64]{1,0:T(1,128)S(1)} %rsqrt_bitcast_fusion.scale_ref), custom_call_target="tpu_custom_call" | custom-call | tf_op jit(solution)/shard_map/pallas_call | solution.py:320
  (24 shorter events, 0.1 us)
Async XLA Ops:
  2.4 25.6 %copy-start = (bf16[1024,256]{1,0:T(8,128)(2,1)S(1)}, bf16[1024,256]{1,0:T(8,128)(2,1)}, u32[]{:S(2)}) copy-start(bf16[1024,256]{1,0:T(8,128)(2,1)} %constant.76.clone.s2_ref) | copy-start | bytes 1572868
  2.4 25.6 %copy-start.6 = (bf16[128,384]{1,0:T(8,128)(2,1)S(1)}, bf16[128,384]{1,0:T(8,128)(2,1)}, u32[]{:S(2)}) copy-start(bf16[128,384]{1,0:T(8,128)(2,1)} %constant.77.clone.win_ref) | copy-start | bytes 294916
  2.4 25.6 %copy-start.7 = (bf16[256,128]{1,0:T(8,128)(2,1)S(1)}, bf16[256,128]{1,0:T(8,128)(2,1)}, u32[]{:S(2)}) copy-start(bf16[256,128]{1,0:T(8,128)(2,1)} %constant.74.clone.s1_ref) | copy-start | bytes 196612
  2.5 25.6 %copy-start.8 = (f32[128,128]{1,0:T(8,128)S(1)}, f32[128,128]{1,0:T(8,128)}, u32[]{:S(2)}) copy-start(f32[128,128]{1,0:T(8,128)} %constant.78.clone.taper_ref) | copy-start | bytes 196612
  2.5 25.5 %all-to-all-start = ((bf16[128,16,128]{2,1,0:T(8,128)(2,1)}), bf16[128,16,128]{2,1,0:T(8,128)(2,1)S(1)}, u32[]{:S(2)}, u32[]{:S(2)}) async-start(bf16[128,16,128]{2,1,0:T(8,128)(2,1)} %bitcast.12), calls=%async_computation | async-start | bytes 1048576 | tf_op jit(solution)/shard_map/all_to_all | solution.py:271
  14.0 14.1 %copy-start.5 = (f32[2,128,128]{2,1,0:T(8,128)S(1)}, f32[2,128,128]{2,1,0:T(8,128)}, u32[]{:S(2)}) copy-start(f32[2,128,128]{2,1,0:T(8,128)} %constant.75.clone.tw_ref) | copy-start | bytes 393220
  28.0 6.2 %copy-start.9 = (s32[16,16]{1,0:T(8,128)S(1)}, s32[16,16]{1,0:T(8,128)}, u32[]{:S(2)}) copy-start(s32[16,16]{1,0:T(8,128)} %param.12) | copy-start | bytes 3076
  28.0 17.5 %copy-start.2 = (bf16[256,1024]{1,0:T(8,128)(2,1)S(1)}, bf16[256,1024]{1,0:T(8,128)(2,1)}, u32[]{:S(2)}) copy-start(bf16[256,1024]{1,0:T(8,128)(2,1)} %constant.80.clone.el_ref) | copy-start | bytes 1572868
  28.1 17.5 %copy-start.3 = (bf16[1024,256]{1,0:T(8,128)(2,1)S(1)}, bf16[1024,256]{1,0:T(8,128)(2,1)}, u32[]{:S(2)}) copy-start(bf16[1024,256]{1,0:T(8,128)(2,1)} %constant.81.clone.dh_ref) | copy-start | bytes 1572868
  28.1 17.5 %copy-start.4 = (bf16[1024,256]{1,0:T(8,128)(2,1)S(1)}, bf16[1024,256]{1,0:T(8,128)(2,1)}, u32[]{:S(2)}) copy-start(bf16[1024,256]{1,0:T(8,128)(2,1)} %constant.82.clone.dl_ref) | copy-start | bytes 1572868
  30.2 15.4 %copy-start.1 = (bf16[256,1024]{1,0:T(8,128)(2,1)S(1)}, bf16[256,1024]{1,0:T(8,128)(2,1)}, u32[]{:S(2)}) copy-start(bf16[256,1024]{1,0:T(8,128)(2,1)} %constant.79.clone.eh_ref) | copy-start | bytes 1572868
  30.2 15.3 %all-to-all-start.1 = ((bf16[128,8,128]{2,1,0:T(8,128)(2,1)}), bf16[128,8,128]{2,1,0:T(8,128)(2,1)S(1)}, u32[]{:S(2)}, u32[]{:S(2)}) async-start(bf16[128,8,128]{2,1,0:T(8,128)(2,1)} %bitcast.2), calls=%async_computation.1 | async-start | bytes 524288 | tf_op jit(solution)/shard_map/all_to_all | solution.py:271
  49.5 14.2 %all-to-all-start.2 = ((bf16[128,4,128]{2,1,0:T(4,128)(2,1)}), bf16[128,4,128]{2,1,0:T(4,128)(2,1)S(1)}, u32[]{:S(2)}, u32[]{:S(2)}) async-start(bf16[128,4,128]{2,1,0:T(4,128)(2,1)} %bitcast.4), calls=%async_computation.2 | async-start | bytes 262144 | tf_op jit(solution)/shard_map/all_to_all | solution.py:271

commit v4 on v3

--- a/solution.py
+++ b/solution.py
@@ -76,59 +76,75 @@
 
 
 def channel_table():
-    c, s = cs(np.arange(256)[:, None] * np.arange(Q)[None], Q)
+    c, s = cs(np.arange(256)[:, None] * (2 * np.arange(256) + 1)[None], 2 * Q)
     return np_split(np.concatenate([c, s], axis=1))
 
 
 def offset_table():
-    c, s = cs(np.arange(Q)[:, None] * np.arange(256)[None], Q)
+    c, s = cs((2 * np.arange(256) + 1)[:, None] * np.arange(256)[None], 2 * Q)
     return np_split(np.concatenate([c, s], axis=0) / Q)
 
 
-def pack_kernel(raw_ref, out_ref, raw_buf, buf_ref, sems):
-    wide = C // 4
-    copies = [
+def pack_kernel(raw_ref, out_ref, raw_buf, buf_ref, out_buf, in_sems, out_sems):
+    wide = C // 8
+    takes = [
         pltpu.make_async_copy(
-            raw_ref.at[:, pl.ds(k * wide, wide)], raw_buf.at[:, pl.ds(k * wide, wide)], sems.at[k]
+            raw_ref.at[:, pl.ds(k * wide, wide)], raw_buf.at[:, pl.ds(k * wide, wide)], in_sems.at[k]
         )
-        for k in range(4)
+        for k in range(8)
     ]
-    for copy in copies:
-        copy.start()
-    for i in range(BLK):
-        if i % 4 == 0:
-            copies[i // 4].wait()
-        x = raw_buf[:, i * 256 : (i + 1) * 256]
-        rows = jnp.concatenate([x[:, :DEV], x[:, DEV:]], axis=0)
-        buf_ref[pl.ds(i, DEV, stride=BLK), :] = rows.T
-    out_ref[...] = buf_ref[...].astype(BF)
+    for take in takes:
+        take.start()
+    gives = []
+    for k in range(2):
+        for i in range(8):
+            if i % 2 == 0:
+                takes[4 * k + i // 2].wait()
+            at = (8 * k + i) * 256
+            rows = jnp.concatenate([raw_buf[:, at : at + DEV], raw_buf[:, at + DEV : at + 256]], axis=0)
+            buf_ref[pl.ds(1024 * k + i, DEV, stride=8), :] = rows.T
+        out_buf[k] = buf_ref[1024 * k : 1024 * (k + 1), :].reshape(DEV, 8, DEV).astype(BF)
+        give = pltpu.make_async_copy(
+            out_buf.at[k], out_ref.at[:, pl.ds(8 * k, 8), :], out_sems.at[k]
+        )
+        give.start()
+        gives.append(give)
+    for give in gives:
+        give.wait()
 
 
 def dot(a, b):
     return jnp.dot(a, b, preferred_element_type=F32)
 
 
-def spectra_kernel(in_ref, s1_ref, tw_ref, s2_ref, win_ref, taper_ref, out_ref, buf_ref, wide_ref):
-    buf_ref[...] = in_ref[...].astype(F32)
-    stage1, stage2 = s1_ref[...], s2_ref[...]
-    cos, sin = tw_ref[0], tw_ref[1]
+def spectra_kernel(
+    in_ref, s1_ref, tw_ref, s2_ref, win_ref, taper_ref, out_ref, buf_ref, z_ref, spec_ref
+):
+    series = in_ref[...].astype(F32).reshape(DEV, 2, 8, DEV)
+    for k in range(2):
+        buf_ref[1024 * k : 1024 * (k + 1), :] = series[:, k].reshape(1024, DEV)
+    stage1 = s1_ref[...]
+    for g in range(4):
+        samples = jnp.concatenate(
+            [
+                buf_ref[pl.ds(1024 * (g // 2) + (4 * g + s) % 8, DEV, stride=8), :]
+                for s in range(4)
+            ],
+            axis=1,
+        ).astype(BF)
+        y = dot(stage1, samples)
+        for s in range(4):
+            y_re, y_im = y[:DEV, s * DEV : (s + 1) * DEV], y[DEV:, s * DEV : (s + 1) * DEV]
+            z_ref[g * DEV : (g + 1) * DEV, s * DEV : (s + 1) * DEV] = (
+                y_re * tw_ref[0] + y_im * tw_ref[1]
+            ).astype(BF)
+            z_ref[g * DEV : (g + 1) * DEV, (4 + s) * DEV : (5 + s) * DEV] = (
+                y_im * tw_ref[0] - y_re * tw_ref[1]
+            ).astype(BF)
+    spec_ref[...] = dot(z_ref[...], s2_ref[...])
     lane = lax.broadcasted_iota(jnp.int32, (DEV, DEV), 1) % J2
     for g in range(4):
-        samples = jnp.concatenate(
-            [buf_ref[pl.ds(4 * g + s, DEV, stride=BLK), :] for s in range(4)], axis=1
-        ).astype(BF)
-        y = dot(stage1, samples)
-        reals, imags = [], []
-        for s in range(4):
-            y_re, y_im = y[:DEV, s * DEV : (s + 1) * DEV], y[DEV:, s * DEV : (s + 1) * DEV]
-            reals.append((y_re * cos + y_im * sin).astype(BF))
-            imags.append((y_im * cos - y_re * sin).astype(BF))
-        spec = dot(jnp.concatenate(reals + imags, axis=1), stage2)
-        re, im = spec[:, :DEV], spec[:, DEV:]
-        wide_ref[g] = re
-        wide_ref[4 + g] = im
-    for g in range(4):
-        re, im = wide_ref[g], wide_ref[4 + g]
+        re, im = spec_ref[g * DEV : (g + 1) * DEV, :DEV], spec_ref[g * DEV : (g + 1) * DEV, DEV:]
         amp = jnp.sqrt(re * re + im * im)
         after = jnp.where(lane == J2 - 1, 0.0, pltpu.roll(amp, DEV - 1, 1))
         before = jnp.where(lane == 0, 0.0, pltpu.roll(amp, 1, 1))
@@ -156,13 +172,16 @@
     white = jnp.concatenate(rows, axis=0)
     product = dot(white, eh_ref[...]) + dot(white, el_ref[...])
     half = BLK * J2
-    f_re = product[:half, :Q] + product[half:, Q:]
-    f_im = product[half:, :Q] - product[:half, Q:]
-    for part, value in enumerate((f_re, f_im)):
-        for k in range(2 * BLK):
-            for t in range(4):
-                f_ref[pl.ds(part * 1024 + 32 * k + t, 8, stride=4), :] = value[
-                    8 * k : 8 * k + 8, t * DEV : (t + 1) * DEV
+    for t in range(2):
+        at = slice(t * DEV, (t + 1) * DEV)
+        to = slice(256 + t * DEV, 256 + (t + 1) * DEV)
+        rc, rs, ic, ims = product[:half, at], product[:half, to], product[half:, at], product[half:, to]
+        for part, sign, value in (
+            (0, 0, rc + ims), (0, 1, rc - ims), (1, 0, ic - rs), (1, 1, ic + rs)
+        ):
+            for k in range(2 * BLK):
+                f_ref[pl.ds(part * 1024 + 32 * k + 2 * sign + t, 8, stride=4), :] = value[
+                    8 * k : 8 * k + 8
                 ]
     acc_ref[...] = jnp.zeros_like(acc_ref)
 
@@ -170,33 +189,38 @@
         at = lambda i, part: pl.ds(pl.multiple_of(part * 1024 + i * 64 + u * 8, 8), 8)
         re = [f_ref[at(i, 0), :] for i in range(BLK)]
         im = [f_ref[at(i, 1), :] for i in range(BLK)]
+        both = [re[i] + im[i] for i in range(BLK)]
+        less = [re[i] - im[i] for i in range(BLK)]
         for delta in range(FAR):
-            sum_re = sum_im = None
+            sums = [None, None, None]
             for i in range(BLK - delta):
                 j = i + delta
                 live = mask_ref[pl.ds(i * BLK + j, 8, stride=0), :]
                 a_re, a_im = re[i] * live, im[i] * live
-                term = a_re * re[j] + a_im * im[j]
-                sum_re = term if sum_re is None else sum_re + term
-                if delta:
-                    term = a_im * re[j] - a_re * im[j]
-                    sum_im = term if sum_im is None else sum_im + term
-            acc_ref[2 * delta] = sum_re - acc_ref[2 * delta]
-            if delta:
-                acc_ref[2 * delta + 1] = sum_im - acc_ref[2 * delta + 1]
+                if delta == 0:
+                    terms = [a_re * re[j] + a_im * im[j]]
+                else:
+                    terms = [(a_re + a_im) * re[j], a_im * less[j], a_re * both[j]]
+                sums = [t if s is None else s + t for s, t in zip(sums, terms)]
+            if delta == 0:
+                acc_ref[0] = sums[0] - acc_ref[0]
+            else:
+                acc_ref[2 * delta] = sums[0] - sums[1] - acc_ref[2 * delta]
+                acc_ref[2 * delta + 1] = sums[0] - sums[2] - acc_ref[2 * delta + 1]
         return carry
 
     lax.fori_loop(0, J2 // 2, unit, 0)
     first = lax.broadcasted_iota(jnp.int32, (8, DEV), 0) < 4
     lane = lax.broadcasted_iota(jnp.int32, (8, DEV), 1)
-    parity = jnp.where(lane % 2 == 1, -1.0, 1.0)
+    row = lax.broadcasted_iota(jnp.int32, (8, DEV), 0)
+    beside = jnp.where((lane % 2 == 1) == (row % 4 < 2), -1.0, 1.0)
     turn = jnp.where(first, -1.0, 1.0)
     for delta in range(BLK):
         if delta < FAR:
             x_re, x_im = acc_ref[2 * delta], acc_ref[2 * delta + 1]
             if delta + 1 < FAR:
-                x_re = x_re + parity * acc_ref[2 * delta + 2]
-                x_im = x_im + parity * acc_ref[2 * delta + 3]
+                x_re = x_re - beside * acc_ref[2 * delta + 3]
+                x_im = x_im + beside * acc_ref[2 * delta + 2]
             s_re, s_im = pltpu.roll(x_re, 4, 0), pltpu.roll(x_im, 4, 0)
             g_re = jnp.where(first, x_re, s_re) + turn * jnp.where(first, s_im, x_im)
             g_im = jnp.where(first, x_im, s_im) - turn * jnp.where(first, s_re, x_re)
@@ -210,9 +234,12 @@
             else:
                 v_ref[at, :] = jnp.zeros((8, DEV), F32)
                 v_ref[to, :] = jnp.zeros((8, DEV), F32)
-    shifted = [v_ref[pl.ds(512 * c + t, DEV, stride=4), :] for c in range(2) for t in range(4)]
-    v_hi, v_lo = split(jnp.concatenate(shifted, axis=1))
-    stacked = dot(v_hi, dh_ref[...]) + dot(v_hi, dl_ref[...]) + dot(v_lo, dh_ref[...])
+    load = lambda c, t: v_ref[pl.ds(512 * c + t, DEV, stride=4), :]
+    folded = [load(0, 0) + load(0, 2), load(0, 1) + load(0, 3)]
+    folded += [load(1, 0) - load(1, 2), load(1, 1) - load(1, 3)]
+    v_hi, v_lo = split(jnp.concatenate(folded, axis=1))
+    fine = dot(jnp.concatenate([v_hi, v_lo], axis=0), dh_ref[...])
+    stacked = fine[:DEV] + fine[DEV:] + dot(v_hi, dl_ref[...])
     left, right = stacked[:, :DEV], stacked[:, DEV:]
     last = lax.broadcasted_iota(jnp.int32, (DEV, DEV), 1) == DEV - 1
     left1, right1 = pltpu.roll(left, DEV - 1, 1), pltpu.roll(right, DEV - 1, 1)
@@ -275,13 +302,15 @@
     device = lax.axis_index("blk") * lax.axis_size("lag") + lax.axis_index("lag")
     packed = pl.pallas_call(
         pack_kernel,
-        out_shape=jax.ShapeDtypeStruct((BLK * DEV, DEV), BF),
+        out_shape=jax.ShapeDtypeStruct((DEV, BLK, DEV), BF),
         in_specs=[pl.BlockSpec(memory_space=pltpu.HBM)],
-        out_specs=VM,
+        out_specs=pl.BlockSpec(memory_space=pltpu.HBM),
         scratch_shapes=[
             pltpu.VMEM((ROWS, C), F32),
             pltpu.VMEM((BLK * DEV, DEV), F32),
-            pltpu.SemaphoreType.DMA((4,)),
+            pltpu.VMEM((2, DEV, 8, DEV), BF),
+            pltpu.SemaphoreType.DMA((8,)),
+            pltpu.SemaphoreType.DMA((2,)),
         ],
     )(raw)
     series = exchange(packed, BLK).reshape(BLK * DEV, DEV)
@@ -292,7 +321,11 @@
         in_specs=[VM] * 6,
         out_specs=VM,
         compiler_params=LIMIT,
-        scratch_shapes=[pltpu.VMEM((BLK * DEV, DEV), F32), pltpu.VMEM((8, DEV, DEV), F32)],
+        scratch_shapes=[
+            pltpu.VMEM((BLK * DEV, DEV), F32),
+            pltpu.VMEM((4 * DEV, 8 * DEV), BF),
+            pltpu.VMEM((4 * DEV, 2 * DEV), F32),
+        ],
     )(series, stage1, twiddle, stage2, window_table(), taper_table())
     banded = exchange(white, 8).reshape(8 * DEV, DEV)
     odd = 2 * lax.iota(jnp.int32, LAGS) - (LAGS - 1)

time: 64.7 us -> 64.2 us (level)
  no operation moved by 1% of the time
where the time goes in v4:
time: 64.2 us; the launch traced here: 64 us
  waiting for transfers between devices  34.4 us (54%)
  starting transfers between devices  19.7 us (31%)
  Pallas kernels  8.69 us (14%)
  local copies, waits for them, and re-layouts  0.68 us (1%)
    all_to_all x3, waiting for transfers between devices, exchange(): lax.all_to_all(x, ('blk', 'lag'), split_axis=0, concat_axis=0, tiled=True)  34.4 us
    all_to_all x3, starting transfers between devices, exchange(): lax.all_to_all(x, ('blk', 'lag'), split_axis=0, concat_axis=0, tiled=True)  19.7 us
    pallas_call x1, Pallas kernels, on_device(): pl.pallas_call(stack_kernel, out_shape=jax.ShapeDtypeStruct((4 * DEV, DEV...  3.21 us
    pallas_call x1, Pallas kernels, on_device(): pl.pallas_call(pack_kernel, out_shape=jax.ShapeDtypeStruct((DEV, BLK, DEV...  2.57 us
    pallas_call x1, Pallas kernels, on_device(): pl.pallas_call(spectra_kernel, out_shape=jax.ShapeDtypeStruct((8 * DEV, D...  2.1 us
  transfers between devices with their start and end apart: 3, of which 3 were waited for; matrix products, arithmetic and copies ran while one was open for 1% of the time, Pallas kernels for 0%

profile of v4, /device:TPU:1, one launch (start us, length us, event | category | flops | bytes accessed | tf_op | source)
XLA Modules:
  0.0 64.0 jit_solution(17171235151821317068)
XLA Ops:
  0.0 2.6 %shard_map.109 = bf16[128,16,128]{2,1,0:T(8,128)(2,1)} custom-call(f32[64,4096]{1,0:T(8,128)} %raw_ref.1), custom_call_target="tpu_custom_call" | custom-call | tf_op jit(solution)/shard_map/pallas_call | solution.py:303
  2.6 0.0 copy-start
  2.6 0.0 copy-start.6
  2.6 0.0 copy-start.7
  2.6 11.5 %all-to-all-start = ((bf16[128,16,128]{2,1,0:T(8,128)(2,1)}), bf16[128,16,128]{2,1,0:T(8,128)(2,1)S(1)}, u32[]{:S(2)}, u32[]{:S(2)}) async-start(bf16[128,16,128]{2,1,0:T(8,128)(2,1)} %shard_map.109), calls=%async_computation | async-start | bytes 1048576 | tf_op jit(solution)/shard_map/all_to_all | solution.py:298
  14.2 0.1 fusion.3
  14.2 0.1 broadcast_in_dim.44
  14.3 0.1 broadcast_in_dim.45
  14.4 0.1 broadcast_in_dim.41
  14.4 0.1 broadcast_in_dim.42
  14.6 0.1 broadcast_in_dim.46
  14.6 0.1 broadcast_in_dim.43
  14.7 13.5 %all-to-all-done = bf16[128,16,128]{2,1,0:T(8,128)(2,1)S(1)} async-done(((bf16[128,16,128]{2,1,0:T(8,128)(2,1)}), bf16[128,16,128]{2,1,0:T(8,128)(2,1)S(1)}, u32[]{:S(2)}, u32[]{:S(2)}) %all-to-all-start) | async-done | bytes 524320 | tf_op jit(solution)/shard_map/all_to_all | solution.py:298
  28.2 2.1 %shard_map.110 = bf16[1024,128]{1,0:T(8,128)(2,1)} custom-call(bf16[2048,128]{1,0:T(8,128)(2,1)S(1)} %bitcast.8, bf16[256,128]{1,0:T(8,128)(2,1)S(1)} %copy-done.7, f32[2,128,128]{2,1,0:T(8,128)S(1)} %copy-done.5, bf16[1024,256]{1,0:T(8,128)(2,1)S(1)} %copy-done, bf16[128,384]{1,0:T(8,128)(2,1)S(1)} %copy-done.6, f32[128,128]{1,0:T(8,128)S(1)} %copy-done.8), custom_call_target="tpu_custom_call" | custom-call | tf_op jit(solution)/shard_map/pallas_call | solution.py:318
  30.3 4.0 %all-to-all-start.1 = ((bf16[128,8,128]{2,1,0:T(8,128)(2,1)}), bf16[128,8,128]{2,1,0:T(8,128)(2,1)S(1)}, u32[]{:S(2)}, u32[]{:S(2)}) async-start(bf16[128,8,128]{2,1,0:T(8,128)(2,1)} %bitcast.1), calls=%async_computation.1 | async-start | bytes 524288 | tf_op jit(solution)/shard_map/all_to_all | solution.py:298
  34.4 0.1 broadcast_in_dim.39
  34.5 0.1 select_reduce_fusion
  34.6 0.1 multiply_reduce_fusion
  34.7 10.9 %all-to-all-done.1 = bf16[128,8,128]{2,1,0:T(8,128)(2,1)S(1)} async-done(((bf16[128,8,128]{2,1,0:T(8,128)(2,1)}), bf16[128,8,128]{2,1,0:T(8,128)(2,1)S(1)}, u32[]{:S(2)}, u32[]{:S(2)}) %all-to-all-start.1) | async-done | bytes 262176 | tf_op jit(solution)/shard_map/all_to_all | solution.py:298
  45.7 0.1 broadcast_in_dim.40.mask_ref
  45.8 3.2 %shard_map.111 = bf16[512,128]{1,0:T(8,128)(2,1)} custom-call(bf16[1024,128]{1,0:T(8,128)(2,1)S(1)} %bitcast.9, f32[256,128]{1,0:T(8,128)S(1)} %broadcast_in_dim.40.mask_ref, f32[2,4,8,128]{3,2,1,0:T(8,128)S(1)} %pad_maximum_fusion.rot_ref, bf16[256,512]{1,0:T(8,128)(2,1)S(1)} %copy-done.1, bf16[256,512]{1,0:T(8,128)(2,1)S(1)} %copy-done.2, ...), custom_call_target="tpu_custom_call" | custom-call | tf_op jit(solution)/shard_map/pallas_call | solution.py:336
  49.0 4.2 %all-to-all-start.2 = ((bf16[128,4,128]{2,1,0:T(4,128)(2,1)}), bf16[128,4,128]{2,1,0:T(4,128)(2,1)S(1)}, u32[]{:S(2)}, u32[]{:S(2)}) async-start(bf16[128,4,128]{2,1,0:T(4,128)(2,1)} %bitcast.3), calls=%async_computation.2 | async-start | bytes 262144 | tf_op jit(solution)/shard_map/all_to_all | solution.py:298
  53.2 10.0 %all-to-all-done.2 = bf16[128,4,128]{2,1,0:T(4,128)(2,1)S(1)} async-done(((bf16[128,4,128]{2,1,0:T(4,128)(2,1)}), bf16[128,4,128]{2,1,0:T(4,128)(2,1)S(1)}, u32[]{:S(2)}, u32[]{:S(2)}) %all-to-all-start.2) | async-done | bytes 131104 | tf_op jit(solution)/shard_map/all_to_all | solution.py:298
  63.2 0.8 %shard_map.112 = f32[8,64]{1,0:T(8,128)} custom-call(bf16[512,128]{1,0:T(8,128)(2,1)S(1)} %bitcast.10, s32[1]{0:T(128)} %bitcast.5.place_ref, f32[1,64]{1,0:T(1,128)S(1)} %rsqrt_bitcast_fusion.scale_ref), custom_call_target="tpu_custom_call" | custom-call | tf_op jit(solution)/shard_map/pallas_call | solution.py:353
  (24 shorter events, 0.1 us)
Async XLA Ops:
  2.6 25.6 %copy-start = (bf16[1024,256]{1,0:T(8,128)(2,1)S(1)}, bf16[1024,256]{1,0:T(8,128)(2,1)}, u32[]{:S(2)}) copy-start(bf16[1024,256]{1,0:T(8,128)(2,1)} %constant.76.clone.s2_ref) | copy-start | bytes 1572868
  2.6 25.6 %copy-start.6 = (bf16[128,384]{1,0:T(8,128)(2,1)S(1)}, bf16[128,384]{1,0:T(8,128)(2,1)}, u32[]{:S(2)}) copy-start(bf16[128,384]{1,0:T(8,128)(2,1)} %constant.77.clone.win_ref) | copy-start | bytes 294916
  2.6 25.6 %copy-start.7 = (bf16[256,128]{1,0:T(8,128)(2,1)S(1)}, bf16[256,128]{1,0:T(8,128)(2,1)}, u32[]{:S(2)}) copy-start(bf16[256,128]{1,0:T(8,128)(2,1)} %constant.74.clone.s1_ref) | copy-start | bytes 196612
  2.6 25.6 %copy-start.8 = (f32[128,128]{1,0:T(8,128)S(1)}, f32[128,128]{1,0:T(8,128)}, u32[]{:S(2)}) copy-start(f32[128,128]{1,0:T(8,128)} %constant.78.clone.taper_ref) | copy-start | bytes 196612
  2.6 25.5 %all-to-all-start = ((bf16[128,16,128]{2,1,0:T(8,128)(2,1)}), bf16[128,16,128]{2,1,0:T(8,128)(2,1)S(1)}, u32[]{:S(2)}, u32[]{:S(2)}) async-start(bf16[128,16,128]{2,1,0:T(8,128)(2,1)} %shard_map.109), calls=%async_computation | async-start | bytes 1048576 | tf_op jit(solution)/shard_map/all_to_all | solution.py:298
  14.1 14.1 %copy-start.5 = (f32[2,128,128]{2,1,0:T(8,128)S(1)}, f32[2,128,128]{2,1,0:T(8,128)}, u32[]{:S(2)}) copy-start(f32[2,128,128]{2,1,0:T(8,128)} %constant.75.clone.tw_ref) | copy-start | bytes 393220
  28.2 6.2 %copy-start.9 = (s32[16,16]{1,0:T(8,128)S(1)}, s32[16,16]{1,0:T(8,128)}, u32[]{:S(2)}) copy-start(s32[16,16]{1,0:T(8,128)} %param.12) | copy-start | bytes 3076
  28.2 17.5 %copy-start.3 = (bf16[512,256]{1,0:T(8,128)(2,1)S(1)}, bf16[512,256]{1,0:T(8,128)(2,1)}, u32[]{:S(2)}) copy-start(bf16[512,256]{1,0:T(8,128)(2,1)} %constant.81.clone.dh_ref) | copy-start | bytes 786436
  28.2 17.5 %copy-start.4 = (bf16[512,256]{1,0:T(8,128)(2,1)S(1)}, bf16[512,256]{1,0:T(8,128)(2,1)}, u32[]{:S(2)}) copy-start(bf16[512,256]{1,0:T(8,128)(2,1)} %constant.82.clone.dl_ref) | copy-start | bytes 786436
  30.3 15.4 %copy-start.1 = (bf16[256,512]{1,0:T(8,128)(2,1)S(1)}, bf16[256,512]{1,0:T(8,128)(2,1)}, u32[]{:S(2)}) copy-start(bf16[256,512]{1,0:T(8,128)(2,1)} %constant.79.clone.eh_ref) | copy-start | bytes 786436
  30.3 15.4 %copy-start.2 = (bf16[256,512]{1,0:T(8,128)(2,1)S(1)}, bf16[256,512]{1,0:T(8,128)(2,1)}, u32[]{:S(2)}) copy-start(bf16[256,512]{1,0:T(8,128)(2,1)} %constant.80.clone.el_ref) | copy-start | bytes 786436
  30.3 15.3 %all-to-all-start.1 = ((bf16[128,8,128]{2,1,0:T(8,128)(2,1)}), bf16[128,8,128]{2,1,0:T(8,128)(2,1)S(1)}, u32[]{:S(2)}, u32[]{:S(2)}) async-start(bf16[128,8,128]{2,1,0:T(8,128)(2,1)} %bitcast.1), calls=%async_computation.1 | async-start | bytes 524288 | tf_op jit(solution)/shard_map/all_to_all | solution.py:298
  49.0 14.2 %all-to-all-start.2 = ((bf16[128,4,128]{2,1,0:T(4,128)(2,1)}), bf16[128,4,128]{2,1,0:T(4,128)(2,1)S(1)}, u32[]{:S(2)}, u32[]{:S(2)}) async-start(bf16[128,4,128]{2,1,0:T(4,128)(2,1)} %bitcast.3), calls=%async_computation.2 | async-start | bytes 262144 | tf_op jit(solution)/shard_map/all_to_all | solution.py:298

commit v5 on v4

--- a/solution.py
+++ b/solution.py
@@ -45,34 +45,53 @@
     return np.cos(angle), np.sin(angle)
 
 
+def first_bins():
+    n = np.arange(64)
+    residue = np.concatenate([n, (DEV - n) % DEV])
+    residue[64] = 64
+    return np.where(residue < K0, residue + DEV, residue)
+
+
+def first_bin(row):
+    residue = jnp.where(row <= 64, row, 192 - row)
+    return jnp.where(residue < K0, residue + DEV, residue)
+
+
 def time_tables():
-    j1, p = np.arange(DEV), np.arange(DEV)
-    c, s = cs((K0 + j1)[:, None] * p[None], DEV)
-    stage1 = np.concatenate([c, -s], axis=0).astype(jnp.bfloat16)
+    n, p = np.arange(64), np.arange(DEV)
+    c, s = cs(n[:, None] * p[None], DEV)
+    stage1 = np.concatenate([c, -s], axis=0)
+    stage1[64] = np.cos(np.pi * p)
     r = np.tile(np.arange(ROWS), 2)
-    c, s = cs((K0 + j1)[:, None] * r[None], NT)
-    twiddle = np.stack([c, s]).astype(np.float32)
+    c, s = cs(first_bins()[:, None] * r[None], NT)
+    mirror = np.where(np.arange(DEV) < 64, 1.0, -1.0)[:, None]
+    twiddle = np.stack([c, mirror * s, mirror * c, s]).astype(np.float32)
     r, j2 = np.arange(ROWS), np.arange(J2)
     c, s = cs(r[:, None] * j2[None], ROWS)
     eye = np.eye(8)
     place = lambda t: np.einsum("ab,rj->arbj", eye, t).reshape(8 * ROWS, 8 * J2)
     stage2 = np.block([[place(c), place(-s)], [place(s), place(c)]])
-    return stage1, twiddle, stage2.astype(jnp.bfloat16)
+    return stage1.astype(jnp.bfloat16), twiddle, stage2.astype(jnp.bfloat16)
+
+
+AFTER, BEFORE = slice(16, 48), (slice(0, 16), slice(64, 96))
 
 
 def window_table():
-    i, j = np.arange(DEV)[:, None], np.arange(DEV)[None]
+    bins = first_bins()
+    gap = bins[:, None] - bins[None]
     near = lambda d: (np.abs(d) <= SW).astype(np.float32)
-    return np.concatenate([near(i - j), near(i - j - DEV), near(i - j + DEV)], axis=1).astype(
-        jnp.bfloat16
-    )
+    after, before = near(gap - DEV), near(gap + DEV)
+    return np.concatenate(
+        [near(gap), after[:, AFTER]] + [before[:, rows] for rows in BEFORE], axis=1
+    ).astype(jnp.bfloat16)
 
 
 def taper_table():
-    position = np.arange(DEV)[:, None] + DEV * np.arange(J2)[None]
+    position = (first_bins() - K0)[:, None] + DEV * np.arange(J2)[None]
     edge = np.minimum(position, NB - 1 - position)
     curve = 0.5 - 0.5 * np.cos(math.pi * (edge + 0.5) / TAPER)
-    return np.tile(np.where(edge < TAPER, curve, 1.0), (1, DEV // J2)).astype(np.float32)
+    return np.tile(np.where(edge < TAPER, curve, 1.0), (1, 2 * DEV // J2)).astype(np.float32)
 
 
 def channel_table():
@@ -86,20 +105,19 @@
 
 
 def pack_kernel(raw_ref, out_ref, raw_buf, buf_ref, out_buf, in_sems, out_sems):
-    wide = C // 8
+    wide = C // 2
     takes = [
         pltpu.make_async_copy(
             raw_ref.at[:, pl.ds(k * wide, wide)], raw_buf.at[:, pl.ds(k * wide, wide)], in_sems.at[k]
         )
-        for k in range(8)
+        for k in range(2)
     ]
     for take in takes:
         take.start()
     gives = []
     for k in range(2):
+        takes[k].wait()
         for i in range(8):
-            if i % 2 == 0:
-                takes[4 * k + i // 2].wait()
             at = (8 * k + i) * 256
             rows = jnp.concatenate([raw_buf[:, at : at + DEV], raw_buf[:, at + DEV : at + 256]], axis=0)
             buf_ref[pl.ds(1024 * k + i, DEV, stride=8), :] = rows.T
@@ -118,41 +136,62 @@
 
 
 def spectra_kernel(
-    in_ref, s1_ref, tw_ref, s2_ref, win_ref, taper_ref, out_ref, buf_ref, z_ref, spec_ref
+    in_ref, s1_ref, tw_ref, s2_ref, win_ref, taper_ref, out_ref, buf_ref, z_ref, white_ref
 ):
     series = in_ref[...].astype(F32).reshape(DEV, 2, 8, DEV)
     for k in range(2):
         buf_ref[1024 * k : 1024 * (k + 1), :] = series[:, k].reshape(1024, DEV)
-    stage1 = s1_ref[...]
-    for g in range(4):
-        samples = jnp.concatenate(
-            [
-                buf_ref[pl.ds(1024 * (g // 2) + (4 * g + s) % 8, DEV, stride=8), :]
-                for s in range(4)
-            ],
-            axis=1,
-        ).astype(BF)
-        y = dot(stage1, samples)
-        for s in range(4):
-            y_re, y_im = y[:DEV, s * DEV : (s + 1) * DEV], y[DEV:, s * DEV : (s + 1) * DEV]
-            z_ref[g * DEV : (g + 1) * DEV, s * DEV : (s + 1) * DEV] = (
-                y_re * tw_ref[0] + y_im * tw_ref[1]
-            ).astype(BF)
-            z_ref[g * DEV : (g + 1) * DEV, (4 + s) * DEV : (5 + s) * DEV] = (
-                y_im * tw_ref[0] - y_re * tw_ref[1]
-            ).astype(BF)
-    spec_ref[...] = dot(z_ref[...], s2_ref[...])
-    lane = lax.broadcasted_iota(jnp.int32, (DEV, DEV), 1) % J2
-    for g in range(4):
-        re, im = spec_ref[g * DEV : (g + 1) * DEV, :DEV], spec_ref[g * DEV : (g + 1) * DEV, DEV:]
-        amp = jnp.sqrt(re * re + im * im)
-        after = jnp.where(lane == J2 - 1, 0.0, pltpu.roll(amp, DEV - 1, 1))
-        before = jnp.where(lane == 0, 0.0, pltpu.roll(amp, 1, 1))
-        total = dot(win_ref[...], jnp.concatenate([amp, after, before], axis=0).astype(BF))
+    top_row = lax.broadcasted_iota(jnp.int32, (8, DEV), 0) == 0
+    lane = lax.broadcasted_iota(jnp.int32, (1, DEV), 1) % J2
+
+    def turn(g, w):
+        rows = [
+            buf_ref[pl.ds(1024 * (g // 2) + (4 * g + 2 * w + s) % 8, DEV, stride=8), :]
+            for s in range(2)
+        ]
+        y = dot(s1_ref[...], jnp.concatenate(rows, axis=1).astype(BF))
+        for s in range(2):
+            re, im = y[:64, s * DEV : (s + 1) * DEV], y[64:, s * DEV : (s + 1) * DEV]
+            no_im = jnp.concatenate([jnp.where(top_row, 0.0, im[:8]), im[8:]], axis=0)
+            re_64 = jnp.concatenate([jnp.where(top_row, im[:8], re[:8]), re[8:]], axis=0)
+            for half, real in enumerate((re, re_64)):
+                at = slice(half * 64, half * 64 + 64)
+                to = slice(g * DEV + half * 64, g * DEV + half * 64 + 64)
+                col = 2 * w + s
+                z_ref[to, col * DEV : (col + 1) * DEV] = (
+                    real * tw_ref[0, at] + no_im * tw_ref[1, at]
+                ).astype(BF)
+                z_ref[to, (4 + col) * DEV : (5 + col) * DEV] = (
+                    no_im * tw_ref[2, at] - real * tw_ref[3, at]
+                ).astype(BF)
+
+    def shifted(x, by, edge):
+        tiles = [pltpu.roll(x[:, s * DEV : (s + 1) * DEV], by, 1) for s in range(2)]
+        return jnp.concatenate([jnp.where(lane == edge, 0.0, t) for t in tiles], axis=1)
+
+    def whiten(h, spec):
+        re, im = (
+            jnp.concatenate([spec[:DEV, at : at + DEV], spec[DEV:, at : at + DEV]], axis=1)
+            for at in (0, DEV)
+        )
+        power = re * re + im * im
+        amp = power * lax.rsqrt(jnp.maximum(power, 1e-30))
+        near = [amp, shifted(amp[AFTER], DEV - 1, J2 - 1)]
+        near += [shifted(amp[rows], 1, 0) for rows in BEFORE]
+        total = dot(win_ref[...], jnp.concatenate(near, axis=0).astype(BF))
         gain = taper_ref[...] / (total * (1.0 / (2 * SW + 1)) + EPS)
-        buf_ref[pl.ds(g, DEV, stride=8), :] = re * gain
-        buf_ref[pl.ds(4 + g, DEV, stride=8), :] = im * gain
-    out_ref[...] = buf_ref[: 8 * DEV, :].astype(BF)
+        for part, value in enumerate((re * gain, im * gain)):
+            for s in range(2):
+                white_ref[pl.ds(4 * part + 2 * h + s, DEV, stride=8), :] = value[
+                    :, s * DEV : (s + 1) * DEV
+                ]
+
+    for h in range(2):
+        for g in (2 * h, 2 * h + 1):
+            for w in range(2):
+                turn(g, w)
+        whiten(h, dot(z_ref[2 * h * DEV : 2 * (h + 1) * DEV, :], s2_ref[...]))
+    out_ref[...] = white_ref[...].astype(BF)
 
 
 def stack_kernel(
@@ -309,7 +348,7 @@
             pltpu.VMEM((ROWS, C), F32),
             pltpu.VMEM((BLK * DEV, DEV), F32),
             pltpu.VMEM((2, DEV, 8, DEV), BF),
-            pltpu.SemaphoreType.DMA((8,)),
+            pltpu.SemaphoreType.DMA((2,)),
             pltpu.SemaphoreType.DMA((2,)),
         ],
     )(raw)
@@ -324,12 +363,12 @@
         scratch_shapes=[
             pltpu.VMEM((BLK * DEV, DEV), F32),
             pltpu.VMEM((4 * DEV, 8 * DEV), BF),
-            pltpu.VMEM((4 * DEV, 2 * DEV), F32),
+            pltpu.VMEM((8 * DEV, DEV), F32),
         ],
     )(series, stage1, twiddle, stage2, window_table(), taper_table())
     banded = exchange(white, 8).reshape(8 * DEV, DEV)
     odd = 2 * lax.iota(jnp.int32, LAGS) - (LAGS - 1)
-    angle = jnp.mod(odd * (K0 + device), Q).astype(F32) * (2 * math.pi / Q)
+    angle = jnp.mod(odd * first_bin(device), Q).astype(F32) * (2 * math.pi / Q)
     spread = lambda x: jnp.broadcast_to(x.reshape(4, 2, 1, 1), (4, 2, 4, DEV)).reshape(4, 8, DEV)
     rotation = jnp.stack([spread(jnp.cos(angle)), spread(jnp.sin(angle))])
     live = jnp.broadcast_to(mask.astype(F32).reshape(BLK * BLK, 1), (BLK * BLK, DEV))

time: 64.2 us -> 64.1 us (level)
  no operation moved by 1% of the time
where the time goes in v5:
time: 64.1 us; the launch traced here: 63.9 us
  waiting for transfers between devices  34.4 us (54%)
  starting transfers between devices  19.7 us (31%)
  Pallas kernels  8.63 us (13%)
  local copies, waits for them, and re-layouts  0.68 us (1%)
    all_to_all x3, waiting for transfers between devices, exchange(): lax.all_to_all(x, ('blk', 'lag'), split_axis=0, concat_axis=0, tiled=True)  34.4 us
    all_to_all x3, starting transfers between devices, exchange(): lax.all_to_all(x, ('blk', 'lag'), split_axis=0, concat_axis=0, tiled=True)  19.7 us
    pallas_call x1, Pallas kernels, on_device(): pl.pallas_call(stack_kernel, out_shape=jax.ShapeDtypeStruct((4 * DEV, DEV...  3.21 us
    pallas_call x1, Pallas kernels, on_device(): pl.pallas_call(spectra_kernel, out_shape=jax.ShapeDtypeStruct((8 * DEV, D...  2.37 us
    pallas_call x1, Pallas kernels, on_device(): pl.pallas_call(pack_kernel, out_shape=jax.ShapeDtypeStruct((DEV, BLK, DEV...  2.25 us
  transfers between devices with their start and end apart: 3, of which 3 were waited for; matrix products, arithmetic and copies ran while one was open for 1% of the time, Pallas kernels for 0%

profile of v5, /device:TPU:1, one launch (start us, length us, event | category | flops | bytes accessed | tf_op | source)
XLA Modules:
  0.0 63.9 jit_solution(357904697245722501)
XLA Ops:
  0.0 2.2 %shard_map.109 = bf16[128,16,128]{2,1,0:T(8,128)(2,1)} custom-call(f32[64,4096]{1,0:T(8,128)} %raw_ref.1), custom_call_target="tpu_custom_call" | custom-call | tf_op jit(solution)/shard_map/pallas_call | solution.py:342
  2.3 0.0 copy-start
  2.3 0.0 copy-start.5
  2.3 0.0 copy-start.7
  2.3 11.5 %all-to-all-start = ((bf16[128,16,128]{2,1,0:T(8,128)(2,1)}), bf16[128,16,128]{2,1,0:T(8,128)(2,1)S(1)}, u32[]{:S(2)}, u32[]{:S(2)}) async-start(bf16[128,16,128]{2,1,0:T(8,128)(2,1)} %shard_map.109), calls=%async_computation | async-start | bytes 1048576 | tf_op jit(solution)/shard_map/all_to_all | solution.py:337
  13.8 0.1 fusion.3
  13.9 0.1 broadcast_in_dim.44
  14.0 0.1 broadcast_in_dim.45
  14.0 0.1 broadcast_in_dim.41
  14.1 0.1 broadcast_in_dim.42
  14.2 0.1 broadcast_in_dim.46
  14.3 0.1 broadcast_in_dim.43
  14.4 13.5 %all-to-all-done = bf16[128,16,128]{2,1,0:T(8,128)(2,1)S(1)} async-done(((bf16[128,16,128]{2,1,0:T(8,128)(2,1)}), bf16[128,16,128]{2,1,0:T(8,128)(2,1)S(1)}, u32[]{:S(2)}, u32[]{:S(2)}) %all-to-all-start) | async-done | bytes 524320 | tf_op jit(solution)/shard_map/all_to_all | solution.py:337
  27.9 2.4 %shard_map.110 = bf16[1024,128]{1,0:T(8,128)(2,1)} custom-call(bf16[2048,128]{1,0:T(8,128)(2,1)S(1)} %bitcast.8, bf16[128,128]{1,0:T(8,128)(2,1)S(1)} %copy-done.8, f32[4,128,128]{2,1,0:T(8,128)S(1)} %copy-done.5, bf16[1024,256]{1,0:T(8,128)(2,1)S(1)} %copy-done, bf16[128,208]{1,0:T(8,128)(2,1)S(1)} %copy-done.7, f32[128,256]{1,0:T(8,128)S(1)} %copy-done.6), custom_call_target="tpu_custom_call" | custom-call | tf_op jit(solution)/shard_map/pallas_call | solution.py:357
  30.3 4.0 %all-to-all-start.1 = ((bf16[128,8,128]{2,1,0:T(8,128)(2,1)}), bf16[128,8,128]{2,1,0:T(8,128)(2,1)S(1)}, u32[]{:S(2)}, u32[]{:S(2)}) async-start(bf16[128,8,128]{2,1,0:T(8,128)(2,1)} %bitcast.1), calls=%async_computation.1 | async-start | bytes 524288 | tf_op jit(solution)/shard_map/all_to_all | solution.py:337
  34.3 0.1 broadcast_in_dim.39
  34.4 0.1 select_reduce_fusion
  34.6 0.1 multiply_reduce_fusion
  34.7 10.9 %all-to-all-done.1 = bf16[128,8,128]{2,1,0:T(8,128)(2,1)S(1)} async-done(((bf16[128,8,128]{2,1,0:T(8,128)(2,1)}), bf16[128,8,128]{2,1,0:T(8,128)(2,1)S(1)}, u32[]{:S(2)}, u32[]{:S(2)}) %all-to-all-start.1) | async-done | bytes 262176 | tf_op jit(solution)/shard_map/all_to_all | solution.py:337
  45.6 0.1 broadcast_in_dim.40.mask_ref
  45.7 3.2 %shard_map.111 = bf16[512,128]{1,0:T(8,128)(2,1)} custom-call(bf16[1024,128]{1,0:T(8,128)(2,1)S(1)} %bitcast.9, f32[256,128]{1,0:T(8,128)S(1)} %broadcast_in_dim.40.mask_ref, f32[2,4,8,128]{3,2,1,0:T(8,128)S(1)} %pad_maximum_fusion.rot_ref, bf16[256,512]{1,0:T(8,128)(2,1)S(1)} %copy-done.1, bf16[256,512]{1,0:T(8,128)(2,1)S(1)} %copy-done.2, ...), custom_call_target="tpu_custom_call" | custom-call | tf_op jit(solution)/shard_map/pallas_call | solution.py:375
  48.9 4.2 %all-to-all-start.2 = ((bf16[128,4,128]{2,1,0:T(4,128)(2,1)}), bf16[128,4,128]{2,1,0:T(4,128)(2,1)S(1)}, u32[]{:S(2)}, u32[]{:S(2)}) async-start(bf16[128,4,128]{2,1,0:T(4,128)(2,1)} %bitcast.3), calls=%async_computation.2 | async-start | bytes 262144 | tf_op jit(solution)/shard_map/all_to_all | solution.py:337
  53.1 10.0 %all-to-all-done.2 = bf16[128,4,128]{2,1,0:T(4,128)(2,1)S(1)} async-done(((bf16[128,4,128]{2,1,0:T(4,128)(2,1)}), bf16[128,4,128]{2,1,0:T(4,128)(2,1)S(1)}, u32[]{:S(2)}, u32[]{:S(2)}) %all-to-all-start.2) | async-done | bytes 131104 | tf_op jit(solution)/shard_map/all_to_all | solution.py:337
  63.1 0.8 %shard_map.112 = f32[8,64]{1,0:T(8,128)} custom-call(bf16[512,128]{1,0:T(8,128)(2,1)S(1)} %bitcast.10, s32[1]{0:T(128)} %bitcast.5.place_ref, f32[1,64]{1,0:T(1,128)S(1)} %rsqrt_bitcast_fusion.scale_ref), custom_call_target="tpu_custom_call" | custom-call | tf_op jit(solution)/shard_map/pallas_call | solution.py:392
  (24 shorter events, 0.1 us)
Async XLA Ops:
  2.3 25.6 %copy-start = (bf16[1024,256]{1,0:T(8,128)(2,1)S(1)}, bf16[1024,256]{1,0:T(8,128)(2,1)}, u32[]{:S(2)}) copy-start(bf16[1024,256]{1,0:T(8,128)(2,1)} %constant.80.clone.s2_ref) | copy-start | bytes 1572868
  2.3 25.6 %copy-start.5 = (f32[4,128,128]{2,1,0:T(8,128)S(1)}, f32[4,128,128]{2,1,0:T(8,128)}, u32[]{:S(2)}) copy-start(f32[4,128,128]{2,1,0:T(8,128)} %constant.79.clone.tw_ref) | copy-start | bytes 786436
  2.3 25.6 %copy-start.7 = (bf16[128,208]{1,0:T(8,128)(2,1)S(1)}, bf16[128,208]{1,0:T(8,128)(2,1)}, u32[]{:S(2)}) copy-start(bf16[128,208]{1,0:T(8,128)(2,1)} %constant.81.clone.win_ref) | copy-start | bytes 159748
  2.3 25.5 %all-to-all-start = ((bf16[128,16,128]{2,1,0:T(8,128)(2,1)}), bf16[128,16,128]{2,1,0:T(8,128)(2,1)S(1)}, u32[]{:S(2)}, u32[]{:S(2)}) async-start(bf16[128,16,128]{2,1,0:T(8,128)(2,1)} %shard_map.109), calls=%async_computation | async-start | bytes 1048576 | tf_op jit(solution)/shard_map/all_to_all | solution.py:337
  13.8 14.0 %copy-start.6 = (f32[128,256]{1,0:T(8,128)S(1)}, f32[128,256]{1,0:T(8,128)}, u32[]{:S(2)}) copy-start(f32[128,256]{1,0:T(8,128)} %constant.82.clone.taper_ref) | copy-start | bytes 393220
  14.4 13.5 %copy-start.8 = (bf16[128,128]{1,0:T(8,128)(2,1)S(1)}, bf16[128,128]{1,0:T(8,128)(2,1)}, u32[]{:S(2)}) copy-start(bf16[128,128]{1,0:T(8,128)(2,1)} %constant.78.clone.s1_ref) | copy-start | bytes 98308
  27.9 6.5 %copy-start.9 = (s32[16,16]{1,0:T(8,128)S(1)}, s32[16,16]{1,0:T(8,128)}, u32[]{:S(2)}) copy-start(s32[16,16]{1,0:T(8,128)} %param.12) | copy-start | bytes 3076
  27.9 17.8 %copy-start.3 = (bf16[512,256]{1,0:T(8,128)(2,1)S(1)}, bf16[512,256]{1,0:T(8,128)(2,1)}, u32[]{:S(2)}) copy-start(bf16[512,256]{1,0:T(8,128)(2,1)} %constant.85.clone.dh_ref) | copy-start | bytes 786436
  27.9 17.8 %copy-start.4 = (bf16[512,256]{1,0:T(8,128)(2,1)S(1)}, bf16[512,256]{1,0:T(8,128)(2,1)}, u32[]{:S(2)}) copy-start(bf16[512,256]{1,0:T(8,128)(2,1)} %constant.86.clone.dl_ref) | copy-start | bytes 786436
  30.3 15.4 %copy-start.1 = (bf16[256,512]{1,0:T(8,128)(2,1)S(1)}, bf16[256,512]{1,0:T(8,128)(2,1)}, u32[]{:S(2)}) copy-start(bf16[256,512]{1,0:T(8,128)(2,1)} %constant.83.clone.eh_ref) | copy-start | bytes 786436
  30.3 15.4 %copy-start.2 = (bf16[256,512]{1,0:T(8,128)(2,1)S(1)}, bf16[256,512]{1,0:T(8,128)(2,1)}, u32[]{:S(2)}) copy-start(bf16[256,512]{1,0:T(8,128)(2,1)} %constant.84.clone.el_ref) | copy-start | bytes 786436
  30.3 15.3 %all-to-all-start.1 = ((bf16[128,8,128]{2,1,0:T(8,128)(2,1)}), bf16[128,8,128]{2,1,0:T(8,128)(2,1)S(1)}, u32[]{:S(2)}, u32[]{:S(2)}) async-start(bf16[128,8,128]{2,1,0:T(8,128)(2,1)} %bitcast.1), calls=%async_computation.1 | async-start | bytes 524288 | tf_op jit(solution)/shard_map/all_to_all | solution.py:337
  48.9 14.2 %all-to-all-start.2 = ((bf16[128,4,128]{2,1,0:T(4,128)(2,1)}), bf16[128,4,128]{2,1,0:T(4,128)(2,1)S(1)}, u32[]{:S(2)}, u32[]{:S(2)}) async-start(bf16[128,4,128]{2,1,0:T(4,128)(2,1)} %bitcast.3), calls=%async_computation.2 | async-start | bytes 262144 | tf_op jit(solution)/shard_map/all_to_all | solution.py:337

commit v6 on v5

--- a/solution.py
+++ b/solution.py
@@ -144,20 +144,20 @@
     top_row = lax.broadcasted_iota(jnp.int32, (8, DEV), 0) == 0
     lane = lax.broadcasted_iota(jnp.int32, (1, DEV), 1) % J2
 
-    def turn(g, w):
+    def turn(g, w=0):
         rows = [
-            buf_ref[pl.ds(1024 * (g // 2) + (4 * g + 2 * w + s) % 8, DEV, stride=8), :]
-            for s in range(2)
+            buf_ref[pl.ds(1024 * (g // 2) + (4 * g + s) % 8, DEV, stride=8), :]
+            for s in range(4)
         ]
         y = dot(s1_ref[...], jnp.concatenate(rows, axis=1).astype(BF))
-        for s in range(2):
+        for s in range(4):
             re, im = y[:64, s * DEV : (s + 1) * DEV], y[64:, s * DEV : (s + 1) * DEV]
             no_im = jnp.concatenate([jnp.where(top_row, 0.0, im[:8]), im[8:]], axis=0)
             re_64 = jnp.concatenate([jnp.where(top_row, im[:8], re[:8]), re[8:]], axis=0)
             for half, real in enumerate((re, re_64)):
                 at = slice(half * 64, half * 64 + 64)
                 to = slice(g * DEV + half * 64, g * DEV + half * 64 + 64)
-                col = 2 * w + s
+                col = s
                 z_ref[to, col * DEV : (col + 1) * DEV] = (
                     real * tw_ref[0, at] + no_im * tw_ref[1, at]
                 ).astype(BF)
@@ -186,11 +186,11 @@
                     :, s * DEV : (s + 1) * DEV
                 ]
 
+    for g in range(4):
+        turn(g)
+    spec = dot(z_ref[...], s2_ref[...])
     for h in range(2):
-        for g in (2 * h, 2 * h + 1):
-            for w in range(2):
-                turn(g, w)
-        whiten(h, dot(z_ref[2 * h * DEV : 2 * (h + 1) * DEV, :], s2_ref[...]))
+        whiten(h, spec[2 * h * DEV : 2 * (h + 1) * DEV])
     out_ref[...] = white_ref[...].astype(BF)
 
 

time: 64.1 us -> 63.7 us (level)
  no operation moved by 1% of the time
where the time goes in v6:
time: 63.7 us; the launch traced here: 63.5 us
  waiting for transfers between devices  34.4 us (54%)
  starting transfers between devices  19.7 us (31%)
  Pallas kernels  8.19 us (13%)
  local copies, waits for them, and re-layouts  0.68 us (1%)
    all_to_all x3, waiting for transfers between devices, exchange(): lax.all_to_all(x, ('blk', 'lag'), split_axis=0, concat_axis=0, tiled=True)  34.4 us
    all_to_all x3, starting transfers between devices, exchange(): lax.all_to_all(x, ('blk', 'lag'), split_axis=0, concat_axis=0, tiled=True)  19.7 us
    pallas_call x1, Pallas kernels, on_device(): pl.pallas_call(stack_kernel, out_shape=jax.ShapeDtypeStruct((4 * DEV, DEV...  3.21 us
    pallas_call x1, Pallas kernels, on_device(): pl.pallas_call(pack_kernel, out_shape=jax.ShapeDtypeStruct((DEV, BLK, DEV...  2.25 us
    pallas_call x1, Pallas kernels, on_device(): pl.pallas_call(spectra_kernel, out_shape=jax.ShapeDtypeStruct((8 * DEV, D...  1.93 us
  transfers between devices with their start and end apart: 3, of which 3 were waited for; matrix products, arithmetic and copies ran while one was open for 1% of the time, Pallas kernels for 0%

profile of v6, /device:TPU:1, one launch (start us, length us, event | category | flops | bytes accessed | tf_op | source)
XLA Modules:
  0.0 63.5 jit_solution(13783941800184856597)
XLA Ops:
  0.0 2.2 %shard_map.109 = bf16[128,16,128]{2,1,0:T(8,128)(2,1)} custom-call(f32[64,4096]{1,0:T(8,128)} %raw_ref.1), custom_call_target="tpu_custom_call" | custom-call | tf_op jit(solution)/shard_map/pallas_call | solution.py:342
  2.3 0.0 copy-start
  2.3 0.0 copy-start.5
  2.3 0.0 copy-start.7
  2.3 11.5 %all-to-all-start = ((bf16[128,16,128]{2,1,0:T(8,128)(2,1)}), bf16[128,16,128]{2,1,0:T(8,128)(2,1)S(1)}, u32[]{:S(2)}, u32[]{:S(2)}) async-start(bf16[128,16,128]{2,1,0:T(8,128)(2,1)} %shard_map.109), calls=%async_computation | async-start | bytes 1048576 | tf_op jit(solution)/shard_map/all_to_all | solution.py:337
  13.8 0.1 fusion.3
  13.9 0.1 broadcast_in_dim.44
  14.0 0.1 broadcast_in_dim.45
  14.0 0.1 broadcast_in_dim.41
  14.1 0.1 broadcast_in_dim.42
  14.2 0.1 broadcast_in_dim.46
  14.3 0.1 broadcast_in_dim.43
  14.4 13.5 %all-to-all-done = bf16[128,16,128]{2,1,0:T(8,128)(2,1)S(1)} async-done(((bf16[128,16,128]{2,1,0:T(8,128)(2,1)}), bf16[128,16,128]{2,1,0:T(8,128)(2,1)S(1)}, u32[]{:S(2)}, u32[]{:S(2)}) %all-to-all-start) | async-done | bytes 524320 | tf_op jit(solution)/shard_map/all_to_all | solution.py:337
  27.9 1.9 %shard_map.110 = bf16[1024,128]{1,0:T(8,128)(2,1)} custom-call(bf16[2048,128]{1,0:T(8,128)(2,1)S(1)} %bitcast.8, bf16[128,128]{1,0:T(8,128)(2,1)S(1)} %copy-done.8, f32[4,128,128]{2,1,0:T(8,128)S(1)} %copy-done.5, bf16[1024,256]{1,0:T(8,128)(2,1)S(1)} %copy-done, bf16[128,208]{1,0:T(8,128)(2,1)S(1)} %copy-done.7, f32[128,256]{1,0:T(8,128)S(1)} %copy-done.6), custom_call_target="tpu_custom_call" | custom-call | tf_op jit(solution)/shard_map/pallas_call | solution.py:357
  29.8 4.0 %all-to-all-start.1 = ((bf16[128,8,128]{2,1,0:T(8,128)(2,1)}), bf16[128,8,128]{2,1,0:T(8,128)(2,1)S(1)}, u32[]{:S(2)}, u32[]{:S(2)}) async-start(bf16[128,8,128]{2,1,0:T(8,128)(2,1)} %bitcast.1), calls=%async_computation.1 | async-start | bytes 524288 | tf_op jit(solution)/shard_map/all_to_all | solution.py:337
  33.9 0.1 broadcast_in_dim.39
  34.0 0.1 select_reduce_fusion
  34.1 0.1 multiply_reduce_fusion
  34.2 10.9 %all-to-all-done.1 = bf16[128,8,128]{2,1,0:T(8,128)(2,1)S(1)} async-done(((bf16[128,8,128]{2,1,0:T(8,128)(2,1)}), bf16[128,8,128]{2,1,0:T(8,128)(2,1)S(1)}, u32[]{:S(2)}, u32[]{:S(2)}) %all-to-all-start.1) | async-done | bytes 262176 | tf_op jit(solution)/shard_map/all_to_all | solution.py:337
  45.2 0.1 broadcast_in_dim.40.mask_ref
  45.3 3.2 %shard_map.111 = bf16[512,128]{1,0:T(8,128)(2,1)} custom-call(bf16[1024,128]{1,0:T(8,128)(2,1)S(1)} %bitcast.9, f32[256,128]{1,0:T(8,128)S(1)} %broadcast_in_dim.40.mask_ref, f32[2,4,8,128]{3,2,1,0:T(8,128)S(1)} %pad_maximum_fusion.rot_ref, bf16[256,512]{1,0:T(8,128)(2,1)S(1)} %copy-done.1, bf16[256,512]{1,0:T(8,128)(2,1)S(1)} %copy-done.2, ...), custom_call_target="tpu_custom_call" | custom-call | tf_op jit(solution)/shard_map/pallas_call | solution.py:375
  48.5 4.2 %all-to-all-start.2 = ((bf16[128,4,128]{2,1,0:T(4,128)(2,1)}), bf16[128,4,128]{2,1,0:T(4,128)(2,1)S(1)}, u32[]{:S(2)}, u32[]{:S(2)}) async-start(bf16[128,4,128]{2,1,0:T(4,128)(2,1)} %bitcast.3), calls=%async_computation.2 | async-start | bytes 262144 | tf_op jit(solution)/shard_map/all_to_all | solution.py:337
  52.7 10.0 %all-to-all-done.2 = bf16[128,4,128]{2,1,0:T(4,128)(2,1)S(1)} async-done(((bf16[128,4,128]{2,1,0:T(4,128)(2,1)}), bf16[128,4,128]{2,1,0:T(4,128)(2,1)S(1)}, u32[]{:S(2)}, u32[]{:S(2)}) %all-to-all-start.2) | async-done | bytes 131104 | tf_op jit(solution)/shard_map/all_to_all | solution.py:337
  62.6 0.8 %shard_map.112 = f32[8,64]{1,0:T(8,128)} custom-call(bf16[512,128]{1,0:T(8,128)(2,1)S(1)} %bitcast.10, s32[1]{0:T(128)} %bitcast.5.place_ref, f32[1,64]{1,0:T(1,128)S(1)} %rsqrt_bitcast_fusion.scale_ref), custom_call_target="tpu_custom_call" | custom-call | tf_op jit(solution)/shard_map/pallas_call | solution.py:392
  (24 shorter events, 0.1 us)
Async XLA Ops:
  2.3 25.6 %copy-start = (bf16[1024,256]{1,0:T(8,128)(2,1)S(1)}, bf16[1024,256]{1,0:T(8,128)(2,1)}, u32[]{:S(2)}) copy-start(bf16[1024,256]{1,0:T(8,128)(2,1)} %constant.80.clone.s2_ref) | copy-start | bytes 1572868
  2.3 25.6 %copy-start.5 = (f32[4,128,128]{2,1,0:T(8,128)S(1)}, f32[4,128,128]{2,1,0:T(8,128)}, u32[]{:S(2)}) copy-start(f32[4,128,128]{2,1,0:T(8,128)} %constant.79.clone.tw_ref) | copy-start | bytes 786436
  2.3 25.6 %copy-start.7 = (bf16[128,208]{1,0:T(8,128)(2,1)S(1)}, bf16[128,208]{1,0:T(8,128)(2,1)}, u32[]{:S(2)}) copy-start(bf16[128,208]{1,0:T(8,128)(2,1)} %constant.81.clone.win_ref) | copy-start | bytes 159748
  2.3 25.5 %all-to-all-start = ((bf16[128,16,128]{2,1,0:T(8,128)(2,1)}), bf16[128,16,128]{2,1,0:T(8,128)(2,1)S(1)}, u32[]{:S(2)}, u32[]{:S(2)}) async-start(bf16[128,16,128]{2,1,0:T(8,128)(2,1)} %shard_map.109), calls=%async_computation | async-start | bytes 1048576 | tf_op jit(solution)/shard_map/all_to_all | solution.py:337
  13.8 14.0 %copy-start.6 = (f32[128,256]{1,0:T(8,128)S(1)}, f32[128,256]{1,0:T(8,128)}, u32[]{:S(2)}) copy-start(f32[128,256]{1,0:T(8,128)} %constant.82.clone.taper_ref) | copy-start | bytes 393220
  14.4 13.5 %copy-start.8 = (bf16[128,128]{1,0:T(8,128)(2,1)S(1)}, bf16[128,128]{1,0:T(8,128)(2,1)}, u32[]{:S(2)}) copy-start(bf16[128,128]{1,0:T(8,128)(2,1)} %constant.78.clone.s1_ref) | copy-start | bytes 98308
  27.9 6.0 %copy-start.9 = (s32[16,16]{1,0:T(8,128)S(1)}, s32[16,16]{1,0:T(8,128)}, u32[]{:S(2)}) copy-start(s32[16,16]{1,0:T(8,128)} %param.12) | copy-start | bytes 3076
  27.9 17.4 %copy-start.3 = (bf16[512,256]{1,0:T(8,128)(2,1)S(1)}, bf16[512,256]{1,0:T(8,128)(2,1)}, u32[]{:S(2)}) copy-start(bf16[512,256]{1,0:T(8,128)(2,1)} %constant.85.clone.dh_ref) | copy-start | bytes 786436
  27.9 17.4 %copy-start.4 = (bf16[512,256]{1,0:T(8,128)(2,1)S(1)}, bf16[512,256]{1,0:T(8,128)(2,1)}, u32[]{:S(2)}) copy-start(bf16[512,256]{1,0:T(8,128)(2,1)} %constant.86.clone.dl_ref) | copy-start | bytes 786436
  29.8 15.4 %copy-start.1 = (bf16[256,512]{1,0:T(8,128)(2,1)S(1)}, bf16[256,512]{1,0:T(8,128)(2,1)}, u32[]{:S(2)}) copy-start(bf16[256,512]{1,0:T(8,128)(2,1)} %constant.83.clone.eh_ref) | copy-start | bytes 786436
  29.8 15.4 %copy-start.2 = (bf16[256,512]{1,0:T(8,128)(2,1)S(1)}, bf16[256,512]{1,0:T(8,128)(2,1)}, u32[]{:S(2)}) copy-start(bf16[256,512]{1,0:T(8,128)(2,1)} %constant.84.clone.el_ref) | copy-start | bytes 786436
  29.8 15.3 %all-to-all-start.1 = ((bf16[128,8,128]{2,1,0:T(8,128)(2,1)}), bf16[128,8,128]{2,1,0:T(8,128)(2,1)S(1)}, u32[]{:S(2)}, u32[]{:S(2)}) async-start(bf16[128,8,128]{2,1,0:T(8,128)(2,1)} %bitcast.1), calls=%async_computation.1 | async-start | bytes 524288 | tf_op jit(solution)/shard_map/all_to_all | solution.py:337
  48.5 14.2 %all-to-all-start.2 = ((bf16[128,4,128]{2,1,0:T(4,128)(2,1)}), bf16[128,4,128]{2,1,0:T(4,128)(2,1)S(1)}, u32[]{:S(2)}, u32[]{:S(2)}) async-start(bf16[128,4,128]{2,1,0:T(4,128)(2,1)} %bitcast.3), calls=%async_computation.2 | async-start | bytes 262144 | tf_op jit(solution)/shard_map/all_to_all | solution.py:337

commit v7 on v6

--- a/solution.py
+++ b/solution.py
@@ -136,8 +136,12 @@
 
 
 def spectra_kernel(
-    in_ref, s1_ref, tw_ref, s2_ref, win_ref, taper_ref, out_ref, buf_ref, z_ref, white_ref
+    in_ref, s1_ref, tw_ref, s2_ref, win_ref, taper_ref, mask_ref, out_ref, live_ref,
+    buf_ref, z_ref, white_ref,
 ):
+    mask = mask_ref[...].astype(F32)
+    for i in range(BLK):
+        live_ref[i * BLK : (i + 1) * BLK, :] = jnp.broadcast_to(mask[:, i : i + 1], (BLK, DEV))
     series = in_ref[...].astype(F32).reshape(DEV, 2, 8, DEV)
     for k in range(2):
         buf_ref[1024 * k : 1024 * (k + 1), :] = series[:, k].reshape(1024, DEV)
@@ -248,7 +252,7 @@
                 acc_ref[2 * delta + 1] = sums[0] - sums[2] - acc_ref[2 * delta + 1]
         return carry
 
-    lax.fori_loop(0, J2 // 2, unit, 0)
+    lax.fori_loop(0, J2 // 2, unit, 0, unroll=2)
     first = lax.broadcasted_iota(jnp.int32, (8, DEV), 0) < 4
     lane = lax.broadcasted_iota(jnp.int32, (8, DEV), 1)
     row = lax.broadcasted_iota(jnp.int32, (8, DEV), 0)
@@ -354,24 +358,26 @@
     )(raw)
     series = exchange(packed, BLK).reshape(BLK * DEV, DEV)
     stage1, twiddle, stage2 = time_tables()
-    white = pl.pallas_call(
+    white, live = pl.pallas_call(
         spectra_kernel,
-        out_shape=jax.ShapeDtypeStruct((8 * DEV, DEV), BF),
-        in_specs=[VM] * 6,
-        out_specs=VM,
+        out_shape=(
+            jax.ShapeDtypeStruct((8 * DEV, DEV), BF),
+            jax.ShapeDtypeStruct((BLK * BLK, DEV), F32),
+        ),
+        in_specs=[VM] * 7,
+        out_specs=(VM, VM),
         compiler_params=LIMIT,
         scratch_shapes=[
             pltpu.VMEM((BLK * DEV, DEV), F32),
             pltpu.VMEM((4 * DEV, 8 * DEV), BF),
             pltpu.VMEM((8 * DEV, DEV), F32),
         ],
-    )(series, stage1, twiddle, stage2, window_table(), taper_table())
+    )(series, stage1, twiddle, stage2, window_table(), taper_table(), mask)
     banded = exchange(white, 8).reshape(8 * DEV, DEV)
     odd = 2 * lax.iota(jnp.int32, LAGS) - (LAGS - 1)
     angle = jnp.mod(odd * first_bin(device), Q).astype(F32) * (2 * math.pi / Q)
     spread = lambda x: jnp.broadcast_to(x.reshape(4, 2, 1, 1), (4, 2, 4, DEV)).reshape(4, 8, DEV)
     rotation = jnp.stack([spread(jnp.cos(angle)), spread(jnp.sin(angle))])
-    live = jnp.broadcast_to(mask.astype(F32).reshape(BLK * BLK, 1), (BLK * BLK, DEV))
     parts = pl.pallas_call(
         stack_kernel,
         out_shape=jax.ShapeDtypeStruct((4 * DEV, DEV), BF),

time: 63.7 us -> 63.5 us (level)
  no operation moved by 1% of the time
where the time goes in v7:
time: 63.5 us; the launch traced here: 63.3 us
  waiting for transfers between devices  34.5 us (54%)
  starting transfers between devices  19.7 us (31%)
  Pallas kernels  8.15 us (13%)
    all_to_all x3, waiting for transfers between devices, exchange(): lax.all_to_all(x, ('blk', 'lag'), split_axis=0, concat_axis=0, tiled=True)  34.5 us
    all_to_all x3, starting transfers between devices, exchange(): lax.all_to_all(x, ('blk', 'lag'), split_axis=0, concat_axis=0, tiled=True)  19.7 us
    pallas_call x1, Pallas kernels, on_device(): pl.pallas_call(stack_kernel, out_shape=jax.ShapeDtypeStruct((4 * DEV, DEV...  3.17 us
    pallas_call x1, Pallas kernels, on_device(): pl.pallas_call(pack_kernel, out_shape=jax.ShapeDtypeStruct((DEV, BLK, DEV...  2.25 us
    pallas_call x1, Pallas kernels, on_device(): pl.pallas_call(spectra_kernel, out_shape=(jax.ShapeDtypeStruct((8 * DEV,...  1.93 us
  transfers between devices with their start and end apart: 3, of which 3 were waited for; matrix products, arithmetic and copies ran while one was open for 1% of the time, Pallas kernels for 0%

profile of v7, /device:TPU:1, one launch (start us, length us, event | category | flops | bytes accessed | tf_op | source)
XLA Modules:
  0.0 63.3 jit_solution(10391047267481357766)
XLA Ops:
  0.0 2.2 %shard_map.109 = bf16[128,16,128]{2,1,0:T(8,128)(2,1)} custom-call(f32[64,4096]{1,0:T(8,128)} %raw_ref.1), custom_call_target="tpu_custom_call" | custom-call | tf_op jit(solution)/shard_map/pallas_call | solution.py:346
  2.3 0.0 copy-start
  2.3 0.0 copy-start.7
  2.3 11.5 %all-to-all-start = ((bf16[128,16,128]{2,1,0:T(8,128)(2,1)}), bf16[128,16,128]{2,1,0:T(8,128)(2,1)S(1)}, u32[]{:S(2)}, u32[]{:S(2)}) async-start(bf16[128,16,128]{2,1,0:T(8,128)(2,1)} %shard_map.109), calls=%async_computation | async-start | bytes 1048576 | tf_op jit(solution)/shard_map/all_to_all | solution.py:341
  13.8 0.0 copy-start.6
  13.8 0.1 fusion.3
  13.9 0.1 broadcast_in_dim.35
  14.0 0.1 broadcast_in_dim.36
  14.0 0.1 broadcast_in_dim.32
  14.1 0.1 broadcast_in_dim.33
  14.2 0.1 broadcast_in_dim.37
  14.3 0.1 broadcast_in_dim.34
  14.4 13.5 %all-to-all-done = bf16[128,16,128]{2,1,0:T(8,128)(2,1)S(1)} async-done(((bf16[128,16,128]{2,1,0:T(8,128)(2,1)}), bf16[128,16,128]{2,1,0:T(8,128)(2,1)S(1)}, u32[]{:S(2)}, u32[]{:S(2)}) %all-to-all-start) | async-done | bytes 524320 | tf_op jit(solution)/shard_map/all_to_all | solution.py:341
  27.9 0.0 copy-start.3
  27.9 0.0 copy-start.4
  27.9 1.9 %shard_map.110 = (bf16[1024,128]{1,0:T(8,128)(2,1)}, f32[256,128]{1,0:T(8,128)S(1)}) custom-call(bf16[2048,128]{1,0:T(8,128)(2,1)S(1)} %bitcast.8, bf16[128,128]{1,0:T(8,128)(2,1)S(1)} %copy-done.9, f32[4,128,128]{2,1,0:T(8,128)S(1)} %copy-done.5, bf16[1024,256]{1,0:T(8,128)(2,1)S(1)} %copy-done, bf16[128,208]{1,0:T(8,128)(2,1)S(1)} %copy-done.7, ...), custom_call_target="tpu_custom_call" | custom-call | tf_op jit(solution)/shard_map/pallas_call | solution.py:361
  29.8 4.0 %all-to-all-start.1 = ((bf16[128,8,128]{2,1,0:T(8,128)(2,1)}), bf16[128,8,128]{2,1,0:T(8,128)(2,1)S(1)}, u32[]{:S(2)}, u32[]{:S(2)}) async-start(bf16[128,8,128]{2,1,0:T(8,128)(2,1)} %bitcast.1), calls=%async_computation.1 | async-start | bytes 524288 | tf_op jit(solution)/shard_map/all_to_all | solution.py:341
  33.9 0.1 select_reduce_fusion
  34.0 0.1 multiply_reduce_fusion
  34.1 11.0 %all-to-all-done.1 = bf16[128,8,128]{2,1,0:T(8,128)(2,1)S(1)} async-done(((bf16[128,8,128]{2,1,0:T(8,128)(2,1)}), bf16[128,8,128]{2,1,0:T(8,128)(2,1)S(1)}, u32[]{:S(2)}, u32[]{:S(2)}) %all-to-all-start.1) | async-done | bytes 262176 | tf_op jit(solution)/shard_map/all_to_all | solution.py:341
  45.2 3.2 %shard_map.111 = bf16[512,128]{1,0:T(8,128)(2,1)} custom-call(bf16[1024,128]{1,0:T(8,128)(2,1)S(1)} %bitcast.9, f32[256,128]{1,0:T(8,128)S(1)} %get-tuple-element.8.mask_ref, f32[2,4,8,128]{3,2,1,0:T(8,128)S(1)} %pad_maximum_fusion.rot_ref, bf16[256,512]{1,0:T(8,128)(2,1)S(1)} %copy-done.1, bf16[256,512]{1,0:T(8,128)(2,1)S(1)} %copy-done.2, ...), custom_call_target="tpu_custom_call" | custom-call | tf_op jit(solution)/shard_map/pallas_call | solution.py:381
  48.3 4.2 %all-to-all-start.2 = ((bf16[128,4,128]{2,1,0:T(4,128)(2,1)}), bf16[128,4,128]{2,1,0:T(4,128)(2,1)S(1)}, u32[]{:S(2)}, u32[]{:S(2)}) async-start(bf16[128,4,128]{2,1,0:T(4,128)(2,1)} %bitcast.3), calls=%async_computation.2 | async-start | bytes 262144 | tf_op jit(solution)/shard_map/all_to_all | solution.py:341
  52.5 10.0 %all-to-all-done.2 = bf16[128,4,128]{2,1,0:T(4,128)(2,1)S(1)} async-done(((bf16[128,4,128]{2,1,0:T(4,128)(2,1)}), bf16[128,4,128]{2,1,0:T(4,128)(2,1)S(1)}, u32[]{:S(2)}, u32[]{:S(2)}) %all-to-all-start.2) | async-done | bytes 131104 | tf_op jit(solution)/shard_map/all_to_all | solution.py:341
  62.5 0.8 %shard_map.112 = f32[8,64]{1,0:T(8,128)} custom-call(bf16[512,128]{1,0:T(8,128)(2,1)S(1)} %bitcast.10, s32[1]{0:T(128)} %bitcast.5.place_ref, f32[1,64]{1,0:T(1,128)S(1)} %rsqrt_bitcast_fusion.scale_ref), custom_call_target="tpu_custom_call" | custom-call | tf_op jit(solution)/shard_map/pallas_call | solution.py:398
  (21 shorter events, 0.1 us)
Async XLA Ops:
  2.3 25.6 %copy-start = (bf16[1024,256]{1,0:T(8,128)(2,1)S(1)}, bf16[1024,256]{1,0:T(8,128)(2,1)}, u32[]{:S(2)}) copy-start(bf16[1024,256]{1,0:T(8,128)(2,1)} %constant.80.clone.s2_ref) | copy-start | bytes 1572868
  2.3 25.6 %copy-start.5 = (f32[4,128,128]{2,1,0:T(8,128)S(1)}, f32[4,128,128]{2,1,0:T(8,128)}, u32[]{:S(2)}) copy-start(f32[4,128,128]{2,1,0:T(8,128)} %constant.79.clone.tw_ref) | copy-start | bytes 786436
  2.3 25.6 %copy-start.7 = (bf16[128,208]{1,0:T(8,128)(2,1)S(1)}, bf16[128,208]{1,0:T(8,128)(2,1)}, u32[]{:S(2)}) copy-start(bf16[128,208]{1,0:T(8,128)(2,1)} %constant.81.clone.win_ref) | copy-start | bytes 159748
  2.3 25.5 %all-to-all-start = ((bf16[128,16,128]{2,1,0:T(8,128)(2,1)}), bf16[128,16,128]{2,1,0:T(8,128)(2,1)S(1)}, u32[]{:S(2)}, u32[]{:S(2)}) async-start(bf16[128,16,128]{2,1,0:T(8,128)(2,1)} %shard_map.109), calls=%async_computation | async-start | bytes 1048576 | tf_op jit(solution)/shard_map/all_to_all | solution.py:341
  13.8 14.0 %copy-start.6 = (f32[128,256]{1,0:T(8,128)S(1)}, f32[128,256]{1,0:T(8,128)}, u32[]{:S(2)}) copy-start(f32[128,256]{1,0:T(8,128)} %constant.82.clone.taper_ref) | copy-start | bytes 393220
  14.4 13.5 %copy-start.8 = (s32[16,16]{1,0:T(8,128)S(1)}, s32[16,16]{1,0:T(8,128)}, u32[]{:S(2)}) copy-start(s32[16,16]{1,0:T(8,128)} %mask_ref.1) | copy-start | bytes 3076
  14.4 13.5 %copy-start.9 = (bf16[128,128]{1,0:T(8,128)(2,1)S(1)}, bf16[128,128]{1,0:T(8,128)(2,1)}, u32[]{:S(2)}) copy-start(bf16[128,128]{1,0:T(8,128)(2,1)} %constant.78.clone.s1_ref) | copy-start | bytes 98308
  27.9 17.3 %copy-start.3 = (bf16[512,256]{1,0:T(8,128)(2,1)S(1)}, bf16[512,256]{1,0:T(8,128)(2,1)}, u32[]{:S(2)}) copy-start(bf16[512,256]{1,0:T(8,128)(2,1)} %constant.85.clone.dh_ref) | copy-start | bytes 786436
  27.9 17.3 %copy-start.4 = (bf16[512,256]{1,0:T(8,128)(2,1)S(1)}, bf16[512,256]{1,0:T(8,128)(2,1)}, u32[]{:S(2)}) copy-start(bf16[512,256]{1,0:T(8,128)(2,1)} %constant.86.clone.dl_ref) | copy-start | bytes 786436
  29.8 15.3 %copy-start.1 = (bf16[256,512]{1,0:T(8,128)(2,1)S(1)}, bf16[256,512]{1,0:T(8,128)(2,1)}, u32[]{:S(2)}) copy-start(bf16[256,512]{1,0:T(8,128)(2,1)} %constant.83.clone.eh_ref) | copy-start | bytes 786436
  29.8 15.3 %copy-start.2 = (bf16[256,512]{1,0:T(8,128)(2,1)S(1)}, bf16[256,512]{1,0:T(8,128)(2,1)}, u32[]{:S(2)}) copy-start(bf16[256,512]{1,0:T(8,128)(2,1)} %constant.84.clone.el_ref) | copy-start | bytes 786436
  29.8 15.3 %all-to-all-start.1 = ((bf16[128,8,128]{2,1,0:T(8,128)(2,1)}), bf16[128,8,128]{2,1,0:T(8,128)(2,1)S(1)}, u32[]{:S(2)}, u32[]{:S(2)}) async-start(bf16[128,8,128]{2,1,0:T(8,128)(2,1)} %bitcast.1), calls=%async_computation.1 | async-start | bytes 524288 | tf_op jit(solution)/shard_map/all_to_all | solution.py:341
  48.3 14.2 %all-to-all-start.2 = ((bf16[128,4,128]{2,1,0:T(4,128)(2,1)}), bf16[128,4,128]{2,1,0:T(4,128)(2,1)S(1)}, u32[]{:S(2)}, u32[]{:S(2)}) async-start(bf16[128,4,128]{2,1,0:T(4,128)(2,1)} %bitcast.3), calls=%async_computation.2 | async-start | bytes 262144 | tf_op jit(solution)/shard_map/all_to_all | solution.py:341

commit v8 on v7

--- a/solution.py
+++ b/solution.py
@@ -301,7 +301,7 @@
             out_ref[at : at + 8, :] = pair.astype(BF)
 
 
-def total_kernel(in_ref, place_ref, scale_ref, out_ref):
+def total_kernel(in_ref, scale_ref, out_ref):
     total = jnp.sum(in_ref[...].astype(F32).reshape(DEV // 2, 8, DEV), axis=0)
     total = total + pltpu.roll(total, 4, 0)
     low = lax.broadcasted_iota(jnp.int32, (8, DEV), 0) < 4
@@ -309,8 +309,10 @@
     lane = lax.broadcasted_iota(jnp.int32, (8, DEV), 1)
     flipped = jnp.concatenate([lags[7 - j : 8 - j] for j in range(LAGS)], axis=0)
     flipped = jnp.take_along_axis(flipped, (63 - lane) & 127, axis=1)
-    out = jnp.where(place_ref[0] == 1, flipped, lags)
-    out_ref[...] = out[:, :64] * scale_ref[...]
+    ahead, mirrored = scale_ref[0:1, :], scale_ref[1:2, :]
+    out_ref[...] = jnp.where(
+        mirrored > 0.0, flipped[:, :64] * mirrored, lags[:, :64] * ahead
+    )
 
 
 def pair_counts(mask, columns):
@@ -393,15 +395,15 @@
     )(banded, live, rotation, *channel_table(), *offset_table())
     shares = exchange(parts, 4).reshape(4 * DEV, DEV)
     columns = device * 64 + lax.iota(jnp.int32, 64)
-    scale = stack_scale(pair_counts(mask, columns))[None, :]
-    place = (device < 64).astype(jnp.int32)[None]
+    scale = stack_scale(pair_counts(mask, columns))
+    scales = jnp.stack([scale, jnp.where(device < 64, scale, 0.0)])
     return pl.pallas_call(
         total_kernel,
         out_shape=jax.ShapeDtypeStruct((LAGS, 64), F32),
-        in_specs=[VM, SM, VM],
+        in_specs=[VM, VM],
         out_specs=VM,
         compiler_params=LIMIT,
-    )(shares, place, scale)
+    )(shares, scales)
 
 
 def solution(mesh):

time: 63.5 us -> 63.6 us (level)
  waiting for transfers between devices: 34.5 us -> 33.8 us
where the time goes in v8:
time: 63.6 us; the launch traced here: 63.3 us
  waiting for transfers between devices  33.8 us (53%)
  starting transfers between devices  19.7 us (31%)
  Pallas kernels  8.15 us (13%)
  local copies, waits for them, and re-layouts  1.11 us (2%)
    all_to_all x3, waiting for transfers between devices, exchange(): lax.all_to_all(x, ('blk', 'lag'), split_axis=0, concat_axis=0, tiled=True)  33.8 us
    all_to_all x3, starting transfers between devices, exchange(): lax.all_to_all(x, ('blk', 'lag'), split_axis=0, concat_axis=0, tiled=True)  19.7 us
    pallas_call x1, Pallas kernels, on_device(): pl.pallas_call(stack_kernel, out_shape=jax.ShapeDtypeStruct((4 * DEV, DEV...  3.17 us
    pallas_call x1, Pallas kernels, on_device(): pl.pallas_call(pack_kernel, out_shape=jax.ShapeDtypeStruct((DEV, BLK, DEV...  2.25 us
    pallas_call x1, Pallas kernels, on_device(): pl.pallas_call(spectra_kernel, out_shape=(jax.ShapeDtypeStruct((8 * DEV,...  1.93 us
  transfers between devices with their start and end apart: 3, of which 3 were waited for; matrix products, arithmetic and copies ran while one was open for 1% of the time, Pallas kernels for 0%

profile of v8, /device:TPU:1, one launch (start us, length us, event | category | flops | bytes accessed | tf_op | source)
XLA Modules:
  0.0 63.3 jit_solution(5794928466167109933)
XLA Ops:
  0.0 2.2 %shard_map.109 = bf16[128,16,128]{2,1,0:T(8,128)(2,1)} custom-call(f32[64,4096]{1,0:T(8,128)} %raw_ref.1), custom_call_target="tpu_custom_call" | custom-call | tf_op jit(solution)/shard_map/pallas_call | solution.py:348
  2.3 0.0 copy-start
  2.3 0.0 copy-start.6
  2.3 0.0 copy-start.9
  2.3 11.5 %all-to-all-start = ((bf16[128,16,128]{2,1,0:T(8,128)(2,1)}), bf16[128,16,128]{2,1,0:T(8,128)(2,1)S(1)}, u32[]{:S(2)}, u32[]{:S(2)}) async-start(bf16[128,16,128]{2,1,0:T(8,128)(2,1)} %shard_map.109), calls=%async_computation | async-start | bytes 1048576 | tf_op jit(solution)/shard_map/all_to_all | solution.py:343
  13.8 0.0 copy-start.7
  13.9 0.1 fusion.3
  13.9 0.1 broadcast_in_dim.33
  14.0 0.1 broadcast_in_dim.34
  14.1 0.1 broadcast_in_dim.30
  14.1 0.1 broadcast_in_dim.31
  14.2 0.6 copy-done.8
  14.8 0.1 select_reduce_fusion
  15.0 0.1 multiply_reduce_fusion
  15.1 12.8 %all-to-all-done = bf16[128,16,128]{2,1,0:T(8,128)(2,1)S(1)} async-done(((bf16[128,16,128]{2,1,0:T(8,128)(2,1)}), bf16[128,16,128]{2,1,0:T(8,128)(2,1)S(1)}, u32[]{:S(2)}, u32[]{:S(2)}) %all-to-all-start) | async-done | bytes 524320 | tf_op jit(solution)/shard_map/all_to_all | solution.py:343
  27.9 1.9 %shard_map.110 = (bf16[1024,128]{1,0:T(8,128)(2,1)}, f32[256,128]{1,0:T(8,128)S(1)}) custom-call(bf16[2048,128]{1,0:T(8,128)(2,1)S(1)} %bitcast.9, bf16[128,128]{1,0:T(8,128)(2,1)S(1)} %copy-done.9, f32[4,128,128]{2,1,0:T(8,128)S(1)} %copy-done.5, bf16[1024,256]{1,0:T(8,128)(2,1)S(1)} %copy-done, bf16[128,208]{1,0:T(8,128)(2,1)S(1)} %copy-done.7, ...), custom_call_target="tpu_custom_call" | custom-call | tf_op jit(solution)/shard_map/pallas_call | solution.py:363
  29.8 4.0 %all-to-all-start.1 = ((bf16[128,8,128]{2,1,0:T(8,128)(2,1)}), bf16[128,8,128]{2,1,0:T(8,128)(2,1)S(1)}, u32[]{:S(2)}, u32[]{:S(2)}) async-start(bf16[128,8,128]{2,1,0:T(8,128)(2,1)} %bitcast.1), calls=%async_computation.1 | async-start | bytes 524288 | tf_op jit(solution)/shard_map/all_to_all | solution.py:343
  33.9 0.1 broadcast_in_dim.35
  33.9 0.1 broadcast_in_dim.32
  34.0 11.1 %all-to-all-done.1 = bf16[128,8,128]{2,1,0:T(8,128)(2,1)S(1)} async-done(((bf16[128,8,128]{2,1,0:T(8,128)(2,1)}), bf16[128,8,128]{2,1,0:T(8,128)(2,1)S(1)}, u32[]{:S(2)}, u32[]{:S(2)}) %all-to-all-start.1) | async-done | bytes 262176 | tf_op jit(solution)/shard_map/all_to_all | solution.py:343
  45.2 3.2 %shard_map.111 = bf16[512,128]{1,0:T(8,128)(2,1)} custom-call(bf16[1024,128]{1,0:T(8,128)(2,1)S(1)} %bitcast.10, f32[256,128]{1,0:T(8,128)S(1)} %get-tuple-element.8.mask_ref, f32[2,4,8,128]{3,2,1,0:T(8,128)S(1)} %pad_maximum_fusion.rot_ref, bf16[256,512]{1,0:T(8,128)(2,1)S(1)} %copy-done.1, bf16[256,512]{1,0:T(8,128)(2,1)S(1)} %copy-done.2, ...), custom_call_target="tpu_custom_call" | custom-call | tf_op jit(solution)/shard_map/pallas_call | solution.py:383
  48.3 4.2 %all-to-all-start.2 = ((bf16[128,4,128]{2,1,0:T(4,128)(2,1)}), bf16[128,4,128]{2,1,0:T(4,128)(2,1)S(1)}, u32[]{:S(2)}, u32[]{:S(2)}) async-start(bf16[128,4,128]{2,1,0:T(4,128)(2,1)} %bitcast.3), calls=%async_computation.2 | async-start | bytes 262144 | tf_op jit(solution)/shard_map/all_to_all | solution.py:343
  52.5 10.0 %all-to-all-done.2 = bf16[128,4,128]{2,1,0:T(4,128)(2,1)S(1)} async-done(((bf16[128,4,128]{2,1,0:T(4,128)(2,1)}), bf16[128,4,128]{2,1,0:T(4,128)(2,1)S(1)}, u32[]{:S(2)}, u32[]{:S(2)}) %all-to-all-start.2) | async-done | bytes 131104 | tf_op jit(solution)/shard_map/all_to_all | solution.py:343
  62.5 0.8 %shard_map.112 = f32[8,64]{1,0:T(8,128)} custom-call(bf16[512,128]{1,0:T(8,128)(2,1)S(1)} %bitcast.11, f32[2,64]{1,0:T(2,128)S(1)} %pad_maximum_fusion.1.scale_ref), custom_call_target="tpu_custom_call" | custom-call | tf_op jit(solution)/shard_map/pallas_call | solution.py:400
  (23 shorter events, 0.1 us)
Async XLA Ops:
  2.3 25.6 %copy-start = (bf16[1024,256]{1,0:T(8,128)(2,1)S(1)}, bf16[1024,256]{1,0:T(8,128)(2,1)}, u32[]{:S(2)}) copy-start(bf16[1024,256]{1,0:T(8,128)(2,1)} %constant.82.clone.s2_ref) | copy-start | bytes 1572868
  2.3 25.6 %copy-start.5 = (f32[4,128,128]{2,1,0:T(8,128)S(1)}, f32[4,128,128]{2,1,0:T(8,128)}, u32[]{:S(2)}) copy-start(f32[4,128,128]{2,1,0:T(8,128)} %constant.81.clone.tw_ref) | copy-start | bytes 786436
  2.3 25.6 %copy-start.6 = (f32[128,256]{1,0:T(8,128)S(1)}, f32[128,256]{1,0:T(8,128)}, u32[]{:S(2)}) copy-start(f32[128,256]{1,0:T(8,128)} %constant.84.clone.taper_ref) | copy-start | bytes 393220
  2.3 25.6 %copy-start.9 = (bf16[128,128]{1,0:T(8,128)(2,1)S(1)}, bf16[128,128]{1,0:T(8,128)(2,1)}, u32[]{:S(2)}) copy-start(bf16[128,128]{1,0:T(8,128)(2,1)} %constant.80.clone.s1_ref) | copy-start | bytes 98308
  2.3 25.5 %all-to-all-start = ((bf16[128,16,128]{2,1,0:T(8,128)(2,1)}), bf16[128,16,128]{2,1,0:T(8,128)(2,1)S(1)}, u32[]{:S(2)}, u32[]{:S(2)}) async-start(bf16[128,16,128]{2,1,0:T(8,128)(2,1)} %shard_map.109), calls=%async_computation | async-start | bytes 1048576 | tf_op jit(solution)/shard_map/all_to_all | solution.py:343
  13.8 14.1 %copy-start.7 = (bf16[128,208]{1,0:T(8,128)(2,1)S(1)}, bf16[128,208]{1,0:T(8,128)(2,1)}, u32[]{:S(2)}) copy-start(bf16[128,208]{1,0:T(8,128)(2,1)} %constant.83.clone.win_ref) | copy-start | bytes 159748
  14.1 0.7 %copy-start.8 = (s32[16,16]{1,0:T(8,128)S(1)}, s32[16,16]{1,0:T(8,128)}, u32[]{:S(2)}) copy-start(s32[16,16]{1,0:T(8,128)} %mask_ref.1) | copy-start | bytes 3076
  27.9 17.3 %copy-start.3 = (bf16[512,256]{1,0:T(8,128)(2,1)S(1)}, bf16[512,256]{1,0:T(8,128)(2,1)}, u32[]{:S(2)}) copy-start(bf16[512,256]{1,0:T(8,128)(2,1)} %constant.87.clone.dh_ref) | copy-start | bytes 786436
  27.9 17.3 %copy-start.4 = (bf16[512,256]{1,0:T(8,128)(2,1)S(1)}, bf16[512,256]{1,0:T(8,128)(2,1)}, u32[]{:S(2)}) copy-start(bf16[512,256]{1,0:T(8,128)(2,1)} %constant.88.clone.dl_ref) | copy-start | bytes 786436
  29.8 15.3 %copy-start.1 = (bf16[256,512]{1,0:T(8,128)(2,1)S(1)}, bf16[256,512]{1,0:T(8,128)(2,1)}, u32[]{:S(2)}) copy-start(bf16[256,512]{1,0:T(8,128)(2,1)} %constant.85.clone.eh_ref) | copy-start | bytes 786436
  29.8 15.3 %copy-start.2 = (bf16[256,512]{1,0:T(8,128)(2,1)S(1)}, bf16[256,512]{1,0:T(8,128)(2,1)}, u32[]{:S(2)}) copy-start(bf16[256,512]{1,0:T(8,128)(2,1)} %constant.86.clone.el_ref) | copy-start | bytes 786436
  29.8 15.3 %all-to-all-start.1 = ((bf16[128,8,128]{2,1,0:T(8,128)(2,1)}), bf16[128,8,128]{2,1,0:T(8,128)(2,1)S(1)}, u32[]{:S(2)}, u32[]{:S(2)}) async-start(bf16[128,8,128]{2,1,0:T(8,128)(2,1)} %bitcast.1), calls=%async_computation.1 | async-start | bytes 524288 | tf_op jit(solution)/shard_map/all_to_all | solution.py:343
  48.3 14.2 %all-to-all-start.2 = ((bf16[128,4,128]{2,1,0:T(4,128)(2,1)}), bf16[128,4,128]{2,1,0:T(4,128)(2,1)S(1)}, u32[]{:S(2)}, u32[]{:S(2)}) async-start(bf16[128,4,128]{2,1,0:T(4,128)(2,1)} %bitcast.3), calls=%async_computation.2 | async-start | bytes 262144 | tf_op jit(solution)/shard_map/all_to_all | solution.py:343

commit v9 on v7

--- a/solution.py
+++ b/solution.py
@@ -239,10 +239,10 @@
             for i in range(BLK - delta):
                 j = i + delta
                 live = mask_ref[pl.ds(i * BLK + j, 8, stride=0), :]
-                a_re, a_im = re[i] * live, im[i] * live
                 if delta == 0:
-                    terms = [a_re * re[j] + a_im * im[j]]
+                    terms = [live * (re[i] * re[i] + im[i] * im[i])]
                 else:
+                    a_re, a_im = re[i] * live, im[i] * live
                     terms = [(a_re + a_im) * re[j], a_im * less[j], a_re * both[j]]
                 sums = [t if s is None else s + t for s, t in zip(sums, terms)]
             if delta == 0:
@@ -252,7 +252,7 @@
                 acc_ref[2 * delta + 1] = sums[0] - sums[2] - acc_ref[2 * delta + 1]
         return carry
 
-    lax.fori_loop(0, J2 // 2, unit, 0, unroll=2)
+    lax.fori_loop(0, J2 // 2, unit, 0, unroll=4)
     first = lax.broadcasted_iota(jnp.int32, (8, DEV), 0) < 4
     lane = lax.broadcasted_iota(jnp.int32, (8, DEV), 1)
     row = lax.broadcasted_iota(jnp.int32, (8, DEV), 0)

time: 63.5 us -> 63.5 us (level)
  no operation moved by 1% of the time
where the time goes in v9:
time: 63.5 us; the launch traced here: 63.2 us
  waiting for transfers between devices  34.5 us (54%)
  starting transfers between devices  19.7 us (31%)
  Pallas kernels  8.09 us (13%)
    all_to_all x3, waiting for transfers between devices, exchange(): lax.all_to_all(x, ('blk', 'lag'), split_axis=0, concat_axis=0, tiled=True)  34.5 us
    all_to_all x3, starting transfers between devices, exchange(): lax.all_to_all(x, ('blk', 'lag'), split_axis=0, concat_axis=0, tiled=True)  19.7 us
    pallas_call x1, Pallas kernels, on_device(): pl.pallas_call(stack_kernel, out_shape=jax.ShapeDtypeStruct((4 * DEV, DEV...  3.11 us
    pallas_call x1, Pallas kernels, on_device(): pl.pallas_call(pack_kernel, out_shape=jax.ShapeDtypeStruct((DEV, BLK, DEV...  2.25 us
    pallas_call x1, Pallas kernels, on_device(): pl.pallas_call(spectra_kernel, out_shape=(jax.ShapeDtypeStruct((8 * DEV,...  1.93 us
  transfers between devices with their start and end apart: 3, of which 3 were waited for; matrix products, arithmetic and copies ran while one was open for 1% of the time, Pallas kernels for 0%

profile of v9, /device:TPU:1, one launch (start us, length us, event | category | flops | bytes accessed | tf_op | source)
XLA Modules:
  0.0 63.2 jit_solution(4359309603049749525)
XLA Ops:
  0.0 2.2 %shard_map.109 = bf16[128,16,128]{2,1,0:T(8,128)(2,1)} custom-call(f32[64,4096]{1,0:T(8,128)} %raw_ref.1), custom_call_target="tpu_custom_call" | custom-call | tf_op jit(solution)/shard_map/pallas_call | solution.py:346
  2.3 0.0 copy-start
  2.3 0.0 copy-start.7
  2.3 11.5 %all-to-all-start = ((bf16[128,16,128]{2,1,0:T(8,128)(2,1)}), bf16[128,16,128]{2,1,0:T(8,128)(2,1)S(1)}, u32[]{:S(2)}, u32[]{:S(2)}) async-start(bf16[128,16,128]{2,1,0:T(8,128)(2,1)} %shard_map.109), calls=%async_computation | async-start | bytes 1048576 | tf_op jit(solution)/shard_map/all_to_all | solution.py:341
  13.8 0.0 copy-start.6
  13.8 0.1 fusion.3
  13.9 0.1 broadcast_in_dim.35
  14.0 0.1 broadcast_in_dim.36
  14.0 0.1 broadcast_in_dim.32
  14.1 0.1 broadcast_in_dim.33
  14.2 0.1 broadcast_in_dim.37
  14.3 0.1 broadcast_in_dim.34
  14.4 13.5 %all-to-all-done = bf16[128,16,128]{2,1,0:T(8,128)(2,1)S(1)} async-done(((bf16[128,16,128]{2,1,0:T(8,128)(2,1)}), bf16[128,16,128]{2,1,0:T(8,128)(2,1)S(1)}, u32[]{:S(2)}, u32[]{:S(2)}) %all-to-all-start) | async-done | bytes 524320 | tf_op jit(solution)/shard_map/all_to_all | solution.py:341
  27.9 0.0 copy-start.3
  27.9 0.0 copy-start.4
  27.9 1.9 %shard_map.110 = (bf16[1024,128]{1,0:T(8,128)(2,1)}, f32[256,128]{1,0:T(8,128)S(1)}) custom-call(bf16[2048,128]{1,0:T(8,128)(2,1)S(1)} %bitcast.8, bf16[128,128]{1,0:T(8,128)(2,1)S(1)} %copy-done.9, f32[4,128,128]{2,1,0:T(8,128)S(1)} %copy-done.5, bf16[1024,256]{1,0:T(8,128)(2,1)S(1)} %copy-done, bf16[128,208]{1,0:T(8,128)(2,1)S(1)} %copy-done.7, ...), custom_call_target="tpu_custom_call" | custom-call | tf_op jit(solution)/shard_map/pallas_call | solution.py:361
  29.8 4.0 %all-to-all-start.1 = ((bf16[128,8,128]{2,1,0:T(8,128)(2,1)}), bf16[128,8,128]{2,1,0:T(8,128)(2,1)S(1)}, u32[]{:S(2)}, u32[]{:S(2)}) async-start(bf16[128,8,128]{2,1,0:T(8,128)(2,1)} %bitcast.1), calls=%async_computation.1 | async-start | bytes 524288 | tf_op jit(solution)/shard_map/all_to_all | solution.py:341
  33.9 0.1 select_reduce_fusion
  34.0 0.1 multiply_reduce_fusion
  34.1 11.0 %all-to-all-done.1 = bf16[128,8,128]{2,1,0:T(8,128)(2,1)S(1)} async-done(((bf16[128,8,128]{2,1,0:T(8,128)(2,1)}), bf16[128,8,128]{2,1,0:T(8,128)(2,1)S(1)}, u32[]{:S(2)}, u32[]{:S(2)}) %all-to-all-start.1) | async-done | bytes 262176 | tf_op jit(solution)/shard_map/all_to_all | solution.py:341
  45.2 3.1 %shard_map.111 = bf16[512,128]{1,0:T(8,128)(2,1)} custom-call(bf16[1024,128]{1,0:T(8,128)(2,1)S(1)} %bitcast.9, f32[256,128]{1,0:T(8,128)S(1)} %get-tuple-element.8.mask_ref, f32[2,4,8,128]{3,2,1,0:T(8,128)S(1)} %pad_maximum_fusion.rot_ref, bf16[256,512]{1,0:T(8,128)(2,1)S(1)} %copy-done.1, bf16[256,512]{1,0:T(8,128)(2,1)S(1)} %copy-done.2, ...), custom_call_target="tpu_custom_call" | custom-call | tf_op jit(solution)/shard_map/pallas_call | solution.py:381
  48.3 4.2 %all-to-all-start.2 = ((bf16[128,4,128]{2,1,0:T(4,128)(2,1)}), bf16[128,4,128]{2,1,0:T(4,128)(2,1)S(1)}, u32[]{:S(2)}, u32[]{:S(2)}) async-start(bf16[128,4,128]{2,1,0:T(4,128)(2,1)} %bitcast.3), calls=%async_computation.2 | async-start | bytes 262144 | tf_op jit(solution)/shard_map/all_to_all | solution.py:341
  52.5 10.0 %all-to-all-done.2 = bf16[128,4,128]{2,1,0:T(4,128)(2,1)S(1)} async-done(((bf16[128,4,128]{2,1,0:T(4,128)(2,1)}), bf16[128,4,128]{2,1,0:T(4,128)(2,1)S(1)}, u32[]{:S(2)}, u32[]{:S(2)}) %all-to-all-start.2) | async-done | bytes 131104 | tf_op jit(solution)/shard_map/all_to_all | solution.py:341
  62.4 0.8 %shard_map.112 = f32[8,64]{1,0:T(8,128)} custom-call(bf16[512,128]{1,0:T(8,128)(2,1)S(1)} %bitcast.10, s32[1]{0:T(128)} %bitcast.5.place_ref, f32[1,64]{1,0:T(1,128)S(1)} %rsqrt_bitcast_fusion.scale_ref), custom_call_target="tpu_custom_call" | custom-call | tf_op jit(solution)/shard_map/pallas_call | solution.py:398
  (21 shorter events, 0.1 us)
Async XLA Ops:
  2.3 25.6 %copy-start = (bf16[1024,256]{1,0:T(8,128)(2,1)S(1)}, bf16[1024,256]{1,0:T(8,128)(2,1)}, u32[]{:S(2)}) copy-start(bf16[1024,256]{1,0:T(8,128)(2,1)} %constant.80.clone.s2_ref) | copy-start | bytes 1572868
  2.3 25.6 %copy-start.5 = (f32[4,128,128]{2,1,0:T(8,128)S(1)}, f32[4,128,128]{2,1,0:T(8,128)}, u32[]{:S(2)}) copy-start(f32[4,128,128]{2,1,0:T(8,128)} %constant.79.clone.tw_ref) | copy-start | bytes 786436
  2.3 25.6 %copy-start.7 = (bf16[128,208]{1,0:T(8,128)(2,1)S(1)}, bf16[128,208]{1,0:T(8,128)(2,1)}, u32[]{:S(2)}) copy-start(bf16[128,208]{1,0:T(8,128)(2,1)} %constant.81.clone.win_ref) | copy-start | bytes 159748
  2.3 25.5 %all-to-all-start = ((bf16[128,16,128]{2,1,0:T(8,128)(2,1)}), bf16[128,16,128]{2,1,0:T(8,128)(2,1)S(1)}, u32[]{:S(2)}, u32[]{:S(2)}) async-start(bf16[128,16,128]{2,1,0:T(8,128)(2,1)} %shard_map.109), calls=%async_computation | async-start | bytes 1048576 | tf_op jit(solution)/shard_map/all_to_all | solution.py:341
  13.8 14.0 %copy-start.6 = (f32[128,256]{1,0:T(8,128)S(1)}, f32[128,256]{1,0:T(8,128)}, u32[]{:S(2)}) copy-start(f32[128,256]{1,0:T(8,128)} %constant.82.clone.taper_ref) | copy-start | bytes 393220
  14.4 13.5 %copy-start.8 = (s32[16,16]{1,0:T(8,128)S(1)}, s32[16,16]{1,0:T(8,128)}, u32[]{:S(2)}) copy-start(s32[16,16]{1,0:T(8,128)} %mask_ref.1) | copy-start | bytes 3076
  14.4 13.5 %copy-start.9 = (bf16[128,128]{1,0:T(8,128)(2,1)S(1)}, bf16[128,128]{1,0:T(8,128)(2,1)}, u32[]{:S(2)}) copy-start(bf16[128,128]{1,0:T(8,128)(2,1)} %constant.78.clone.s1_ref) | copy-start | bytes 98308
  27.9 17.3 %copy-start.3 = (bf16[512,256]{1,0:T(8,128)(2,1)S(1)}, bf16[512,256]{1,0:T(8,128)(2,1)}, u32[]{:S(2)}) copy-start(bf16[512,256]{1,0:T(8,128)(2,1)} %constant.85.clone.dh_ref) | copy-start | bytes 786436
  27.9 17.3 %copy-start.4 = (bf16[512,256]{1,0:T(8,128)(2,1)S(1)}, bf16[512,256]{1,0:T(8,128)(2,1)}, u32[]{:S(2)}) copy-start(bf16[512,256]{1,0:T(8,128)(2,1)} %constant.86.clone.dl_ref) | copy-start | bytes 786436
  29.8 15.3 %copy-start.1 = (bf16[256,512]{1,0:T(8,128)(2,1)S(1)}, bf16[256,512]{1,0:T(8,128)(2,1)}, u32[]{:S(2)}) copy-start(bf16[256,512]{1,0:T(8,128)(2,1)} %constant.83.clone.eh_ref) | copy-start | bytes 786436
  29.8 15.3 %copy-start.2 = (bf16[256,512]{1,0:T(8,128)(2,1)S(1)}, bf16[256,512]{1,0:T(8,128)(2,1)}, u32[]{:S(2)}) copy-start(bf16[256,512]{1,0:T(8,128)(2,1)} %constant.84.clone.el_ref) | copy-start | bytes 786436
  29.8 15.3 %all-to-all-start.1 = ((bf16[128,8,128]{2,1,0:T(8,128)(2,1)}), bf16[128,8,128]{2,1,0:T(8,128)(2,1)S(1)}, u32[]{:S(2)}, u32[]{:S(2)}) async-start(bf16[128,8,128]{2,1,0:T(8,128)(2,1)} %bitcast.1), calls=%async_computation.1 | async-start | bytes 524288 | tf_op jit(solution)/shard_map/all_to_all | solution.py:341
  48.3 14.2 %all-to-all-start.2 = ((bf16[128,4,128]{2,1,0:T(4,128)(2,1)}), bf16[128,4,128]{2,1,0:T(4,128)(2,1)S(1)}, u32[]{:S(2)}, u32[]{:S(2)}) async-start(bf16[128,4,128]{2,1,0:T(4,128)(2,1)} %bitcast.3), calls=%async_computation.2 | async-start | bytes 262144 | tf_op jit(solution)/shard_map/all_to_all | solution.py:341

commit v10 on v9

--- a/solution.py
+++ b/solution.py
@@ -148,20 +148,20 @@
     top_row = lax.broadcasted_iota(jnp.int32, (8, DEV), 0) == 0
     lane = lax.broadcasted_iota(jnp.int32, (1, DEV), 1) % J2
 
-    def turn(g, w=0):
+    def turn(g, w):
         rows = [
-            buf_ref[pl.ds(1024 * (g // 2) + (4 * g + s) % 8, DEV, stride=8), :]
-            for s in range(4)
+            buf_ref[pl.ds(1024 * (g // 2) + (4 * g + 2 * w + s) % 8, DEV, stride=8), :]
+            for s in range(2)
         ]
         y = dot(s1_ref[...], jnp.concatenate(rows, axis=1).astype(BF))
-        for s in range(4):
+        for s in range(2):
             re, im = y[:64, s * DEV : (s + 1) * DEV], y[64:, s * DEV : (s + 1) * DEV]
             no_im = jnp.concatenate([jnp.where(top_row, 0.0, im[:8]), im[8:]], axis=0)
             re_64 = jnp.concatenate([jnp.where(top_row, im[:8], re[:8]), re[8:]], axis=0)
             for half, real in enumerate((re, re_64)):
                 at = slice(half * 64, half * 64 + 64)
                 to = slice(g * DEV + half * 64, g * DEV + half * 64 + 64)
-                col = s
+                col = 2 * w + s
                 z_ref[to, col * DEV : (col + 1) * DEV] = (
                     real * tw_ref[0, at] + no_im * tw_ref[1, at]
                 ).astype(BF)
@@ -191,7 +191,8 @@
                 ]
 
     for g in range(4):
-        turn(g)
+        for w in range(2):
+            turn(g, w)
     spec = dot(z_ref[...], s2_ref[...])
     for h in range(2):
         whiten(h, spec[2 * h * DEV : 2 * (h + 1) * DEV])

time: 63.5 us -> 63.5 us (level)
  no operation moved by 1% of the time
where the time goes in v10:
time: 63.5 us; the launch traced here: 63.2 us
  waiting for transfers between devices  34.5 us (54%)
  starting transfers between devices  19.7 us (31%)
  Pallas kernels  8.1 us (13%)
    all_to_all x3, waiting for transfers between devices, exchange(): lax.all_to_all(x, ('blk', 'lag'), split_axis=0, concat_axis=0, tiled=True)  34.5 us
    all_to_all x3, starting transfers between devices, exchange(): lax.all_to_all(x, ('blk', 'lag'), split_axis=0, concat_axis=0, tiled=True)  19.7 us
    pallas_call x1, Pallas kernels, on_device(): pl.pallas_call(stack_kernel, out_shape=jax.ShapeDtypeStruct((4 * DEV, DEV...  3.11 us
    pallas_call x1, Pallas kernels, on_device(): pl.pallas_call(pack_kernel, out_shape=jax.ShapeDtypeStruct((DEV, BLK, DEV...  2.25 us
    pallas_call x1, Pallas kernels, on_device(): pl.pallas_call(spectra_kernel, out_shape=(jax.ShapeDtypeStruct((8 * DEV,...  1.93 us
  transfers between devices with their start and end apart: 3, of which 3 were waited for; matrix products, arithmetic and copies ran while one was open for 1% of the time, Pallas kernels for 0%

profile of v10, /device:TPU:1, one launch (start us, length us, event | category | flops | bytes accessed | tf_op | source)
XLA Modules:
  0.0 63.2 jit_solution(4579720924457927187)
XLA Ops:
  0.0 2.2 %shard_map.109 = bf16[128,16,128]{2,1,0:T(8,128)(2,1)} custom-call(f32[64,4096]{1,0:T(8,128)} %raw_ref.1), custom_call_target="tpu_custom_call" | custom-call | tf_op jit(solution)/shard_map/pallas_call | solution.py:347
  2.3 0.0 copy-start
  2.3 0.0 copy-start.7
  2.3 11.5 %all-to-all-start = ((bf16[128,16,128]{2,1,0:T(8,128)(2,1)}), bf16[128,16,128]{2,1,0:T(8,128)(2,1)S(1)}, u32[]{:S(2)}, u32[]{:S(2)}) async-start(bf16[128,16,128]{2,1,0:T(8,128)(2,1)} %shard_map.109), calls=%async_computation | async-start | bytes 1048576 | tf_op jit(solution)/shard_map/all_to_all | solution.py:342
  13.8 0.0 copy-start.6
  13.8 0.1 fusion.3
  13.9 0.1 broadcast_in_dim.35
  14.0 0.1 broadcast_in_dim.36
  14.0 0.1 broadcast_in_dim.32
  14.1 0.1 broadcast_in_dim.33
  14.2 0.1 broadcast_in_dim.37
  14.3 0.1 broadcast_in_dim.34
  14.4 13.5 %all-to-all-done = bf16[128,16,128]{2,1,0:T(8,128)(2,1)S(1)} async-done(((bf16[128,16,128]{2,1,0:T(8,128)(2,1)}), bf16[128,16,128]{2,1,0:T(8,128)(2,1)S(1)}, u32[]{:S(2)}, u32[]{:S(2)}) %all-to-all-start) | async-done | bytes 524320 | tf_op jit(solution)/shard_map/all_to_all | solution.py:342
  27.9 0.0 copy-start.3
  27.9 0.0 copy-start.4
  27.9 1.9 %shard_map.110 = (bf16[1024,128]{1,0:T(8,128)(2,1)}, f32[256,128]{1,0:T(8,128)S(1)}) custom-call(bf16[2048,128]{1,0:T(8,128)(2,1)S(1)} %bitcast.8, bf16[128,128]{1,0:T(8,128)(2,1)S(1)} %copy-done.9, f32[4,128,128]{2,1,0:T(8,128)S(1)} %copy-done.5, bf16[1024,256]{1,0:T(8,128)(2,1)S(1)} %copy-done, bf16[128,208]{1,0:T(8,128)(2,1)S(1)} %copy-done.7, ...), custom_call_target="tpu_custom_call" | custom-call | tf_op jit(solution)/shard_map/pallas_call | solution.py:362
  29.8 4.0 %all-to-all-start.1 = ((bf16[128,8,128]{2,1,0:T(8,128)(2,1)}), bf16[128,8,128]{2,1,0:T(8,128)(2,1)S(1)}, u32[]{:S(2)}, u32[]{:S(2)}) async-start(bf16[128,8,128]{2,1,0:T(8,128)(2,1)} %bitcast.1), calls=%async_computation.1 | async-start | bytes 524288 | tf_op jit(solution)/shard_map/all_to_all | solution.py:342
  33.9 0.1 select_reduce_fusion
  34.0 0.1 multiply_reduce_fusion
  34.1 11.0 %all-to-all-done.1 = bf16[128,8,128]{2,1,0:T(8,128)(2,1)S(1)} async-done(((bf16[128,8,128]{2,1,0:T(8,128)(2,1)}), bf16[128,8,128]{2,1,0:T(8,128)(2,1)S(1)}, u32[]{:S(2)}, u32[]{:S(2)}) %all-to-all-start.1) | async-done | bytes 262176 | tf_op jit(solution)/shard_map/all_to_all | solution.py:342
  45.2 3.1 %shard_map.111 = bf16[512,128]{1,0:T(8,128)(2,1)} custom-call(bf16[1024,128]{1,0:T(8,128)(2,1)S(1)} %bitcast.9, f32[256,128]{1,0:T(8,128)S(1)} %get-tuple-element.8.mask_ref, f32[2,4,8,128]{3,2,1,0:T(8,128)S(1)} %pad_maximum_fusion.rot_ref, bf16[256,512]{1,0:T(8,128)(2,1)S(1)} %copy-done.1, bf16[256,512]{1,0:T(8,128)(2,1)S(1)} %copy-done.2, ...), custom_call_target="tpu_custom_call" | custom-call | tf_op jit(solution)/shard_map/pallas_call | solution.py:382
  48.3 4.2 %all-to-all-start.2 = ((bf16[128,4,128]{2,1,0:T(4,128)(2,1)}), bf16[128,4,128]{2,1,0:T(4,128)(2,1)S(1)}, u32[]{:S(2)}, u32[]{:S(2)}) async-start(bf16[128,4,128]{2,1,0:T(4,128)(2,1)} %bitcast.3), calls=%async_computation.2 | async-start | bytes 262144 | tf_op jit(solution)/shard_map/all_to_all | solution.py:342
  52.5 10.0 %all-to-all-done.2 = bf16[128,4,128]{2,1,0:T(4,128)(2,1)S(1)} async-done(((bf16[128,4,128]{2,1,0:T(4,128)(2,1)}), bf16[128,4,128]{2,1,0:T(4,128)(2,1)S(1)}, u32[]{:S(2)}, u32[]{:S(2)}) %all-to-all-start.2) | async-done | bytes 131104 | tf_op jit(solution)/shard_map/all_to_all | solution.py:342
  62.4 0.8 %shard_map.112 = f32[8,64]{1,0:T(8,128)} custom-call(bf16[512,128]{1,0:T(8,128)(2,1)S(1)} %bitcast.10, s32[1]{0:T(128)} %bitcast.5.place_ref, f32[1,64]{1,0:T(1,128)S(1)} %rsqrt_bitcast_fusion.scale_ref), custom_call_target="tpu_custom_call" | custom-call | tf_op jit(solution)/shard_map/pallas_call | solution.py:399
  (21 shorter events, 0.1 us)
Async XLA Ops:
  2.3 25.6 %copy-start = (bf16[1024,256]{1,0:T(8,128)(2,1)S(1)}, bf16[1024,256]{1,0:T(8,128)(2,1)}, u32[]{:S(2)}) copy-start(bf16[1024,256]{1,0:T(8,128)(2,1)} %constant.80.clone.s2_ref) | copy-start | bytes 1572868
  2.3 25.6 %copy-start.5 = (f32[4,128,128]{2,1,0:T(8,128)S(1)}, f32[4,128,128]{2,1,0:T(8,128)}, u32[]{:S(2)}) copy-start(f32[4,128,128]{2,1,0:T(8,128)} %constant.79.clone.tw_ref) | copy-start | bytes 786436
  2.3 25.6 %copy-start.7 = (bf16[128,208]{1,0:T(8,128)(2,1)S(1)}, bf16[128,208]{1,0:T(8,128)(2,1)}, u32[]{:S(2)}) copy-start(bf16[128,208]{1,0:T(8,128)(2,1)} %constant.81.clone.win_ref) | copy-start | bytes 159748
  2.3 25.5 %all-to-all-start = ((bf16[128,16,128]{2,1,0:T(8,128)(2,1)}), bf16[128,16,128]{2,1,0:T(8,128)(2,1)S(1)}, u32[]{:S(2)}, u32[]{:S(2)}) async-start(bf16[128,16,128]{2,1,0:T(8,128)(2,1)} %shard_map.109), calls=%async_computation | async-start | bytes 1048576 | tf_op jit(solution)/shard_map/all_to_all | solution.py:342
  13.8 14.0 %copy-start.6 = (f32[128,256]{1,0:T(8,128)S(1)}, f32[128,256]{1,0:T(8,128)}, u32[]{:S(2)}) copy-start(f32[128,256]{1,0:T(8,128)} %constant.82.clone.taper_ref) | copy-start | bytes 393220
  14.4 13.5 %copy-start.8 = (s32[16,16]{1,0:T(8,128)S(1)}, s32[16,16]{1,0:T(8,128)}, u32[]{:S(2)}) copy-start(s32[16,16]{1,0:T(8,128)} %mask_ref.1) | copy-start | bytes 3076
  14.4 13.5 %copy-start.9 = (bf16[128,128]{1,0:T(8,128)(2,1)S(1)}, bf16[128,128]{1,0:T(8,128)(2,1)}, u32[]{:S(2)}) copy-start(bf16[128,128]{1,0:T(8,128)(2,1)} %constant.78.clone.s1_ref) | copy-start | bytes 98308
  27.9 17.3 %copy-start.3 = (bf16[512,256]{1,0:T(8,128)(2,1)S(1)}, bf16[512,256]{1,0:T(8,128)(2,1)}, u32[]{:S(2)}) copy-start(bf16[512,256]{1,0:T(8,128)(2,1)} %constant.85.clone.dh_ref) | copy-start | bytes 786436
  27.9 17.3 %copy-start.4 = (bf16[512,256]{1,0:T(8,128)(2,1)S(1)}, bf16[512,256]{1,0:T(8,128)(2,1)}, u32[]{:S(2)}) copy-start(bf16[512,256]{1,0:T(8,128)(2,1)} %constant.86.clone.dl_ref) | copy-start | bytes 786436
  29.8 15.3 %copy-start.1 = (bf16[256,512]{1,0:T(8,128)(2,1)S(1)}, bf16[256,512]{1,0:T(8,128)(2,1)}, u32[]{:S(2)}) copy-start(bf16[256,512]{1,0:T(8,128)(2,1)} %constant.83.clone.eh_ref) | copy-start | bytes 786436
  29.8 15.3 %copy-start.2 = (bf16[256,512]{1,0:T(8,128)(2,1)S(1)}, bf16[256,512]{1,0:T(8,128)(2,1)}, u32[]{:S(2)}) copy-start(bf16[256,512]{1,0:T(8,128)(2,1)} %constant.84.clone.el_ref) | copy-start | bytes 786436
  29.8 15.3 %all-to-all-start.1 = ((bf16[128,8,128]{2,1,0:T(8,128)(2,1)}), bf16[128,8,128]{2,1,0:T(8,128)(2,1)S(1)}, u32[]{:S(2)}, u32[]{:S(2)}) async-start(bf16[128,8,128]{2,1,0:T(8,128)(2,1)} %bitcast.1), calls=%async_computation.1 | async-start | bytes 524288 | tf_op jit(solution)/shard_map/all_to_all | solution.py:342
  48.3 14.2 %all-to-all-start.2 = ((bf16[128,4,128]{2,1,0:T(4,128)(2,1)}), bf16[128,4,128]{2,1,0:T(4,128)(2,1)S(1)}, u32[]{:S(2)}, u32[]{:S(2)}) async-start(bf16[128,4,128]{2,1,0:T(4,128)(2,1)} %bitcast.3), calls=%async_computation.2 | async-start | bytes 262144 | tf_op jit(solution)/shard_map/all_to_all | solution.py:342

commit v11 on v10

--- a/solution.py
+++ b/solution.py
@@ -302,7 +302,7 @@
             out_ref[at : at + 8, :] = pair.astype(BF)
 
 
-def total_kernel(in_ref, place_ref, scale_ref, out_ref):
+def total_kernel(in_ref, scale_ref, out_ref):
     total = jnp.sum(in_ref[...].astype(F32).reshape(DEV // 2, 8, DEV), axis=0)
     total = total + pltpu.roll(total, 4, 0)
     low = lax.broadcasted_iota(jnp.int32, (8, DEV), 0) < 4
@@ -310,8 +310,10 @@
     lane = lax.broadcasted_iota(jnp.int32, (8, DEV), 1)
     flipped = jnp.concatenate([lags[7 - j : 8 - j] for j in range(LAGS)], axis=0)
     flipped = jnp.take_along_axis(flipped, (63 - lane) & 127, axis=1)
-    out = jnp.where(place_ref[0] == 1, flipped, lags)
-    out_ref[...] = out[:, :64] * scale_ref[...]
+    ahead, mirrored = scale_ref[0:1, :], scale_ref[1:2, :]
+    out_ref[...] = jnp.where(
+        mirrored > 0.0, flipped[:, :64] * mirrored, lags[:, :64] * ahead
+    )
 
 
 def pair_counts(mask, columns):
@@ -394,15 +396,15 @@
     )(banded, live, rotation, *channel_table(), *offset_table())
     shares = exchange(parts, 4).reshape(4 * DEV, DEV)
     columns = device * 64 + lax.iota(jnp.int32, 64)
-    scale = stack_scale(pair_counts(mask, columns))[None, :]
-    place = (device < 64).astype(jnp.int32)[None]
+    scale = stack_scale(pair_counts(mask, columns))
+    scales = jnp.stack([scale, jnp.where(device < 64, scale, 0.0)])
     return pl.pallas_call(
         total_kernel,
         out_shape=jax.ShapeDtypeStruct((LAGS, 64), F32),
-        in_specs=[VM, SM, VM],
+        in_specs=[VM, VM],
         out_specs=VM,
         compiler_params=LIMIT,
-    )(shares, place, scale)
+    )(shares, scales)
 
 
 def solution(mesh):

time: 63.5 us -> 63.5 us (level)
  waiting for transfers between devices: 34.5 us -> 33.8 us
where the time goes in v11:
time: 63.5 us; the launch traced here: 63.2 us
  waiting for transfers between devices  33.8 us (53%)
  starting transfers between devices  19.7 us (31%)
  Pallas kernels  8.1 us (13%)
  local copies, waits for them, and re-layouts  1.11 us (2%)
    all_to_all x3, waiting for transfers between devices, exchange(): lax.all_to_all(x, ('blk', 'lag'), split_axis=0, concat_axis=0, tiled=True)  33.8 us
    all_to_all x3, starting transfers between devices, exchange(): lax.all_to_all(x, ('blk', 'lag'), split_axis=0, concat_axis=0, tiled=True)  19.7 us
    pallas_call x1, Pallas kernels, on_device(): pl.pallas_call(stack_kernel, out_shape=jax.ShapeDtypeStruct((4 * DEV, DEV...  3.11 us
    pallas_call x1, Pallas kernels, on_device(): pl.pallas_call(pack_kernel, out_shape=jax.ShapeDtypeStruct((DEV, BLK, DEV...  2.25 us
    pallas_call x1, Pallas kernels, on_device(): pl.pallas_call(spectra_kernel, out_shape=(jax.ShapeDtypeStruct((8 * DEV,...  1.93 us
  transfers between devices with their start and end apart: 3, of which 3 were waited for; matrix products, arithmetic and copies ran while one was open for 1% of the time, Pallas kernels for 0%

profile of v11, /device:TPU:1, one launch (start us, length us, event | category | flops | bytes accessed | tf_op | source)
XLA Modules:
  0.0 63.2 jit_solution(1900872392565442273)
XLA Ops:
  0.0 2.2 %shard_map.109 = bf16[128,16,128]{2,1,0:T(8,128)(2,1)} custom-call(f32[64,4096]{1,0:T(8,128)} %raw_ref.1), custom_call_target="tpu_custom_call" | custom-call | tf_op jit(solution)/shard_map/pallas_call | solution.py:349
  2.3 0.0 copy-start
  2.3 0.0 copy-start.6
  2.3 0.0 copy-start.9
  2.3 11.5 %all-to-all-start = ((bf16[128,16,128]{2,1,0:T(8,128)(2,1)}), bf16[128,16,128]{2,1,0:T(8,128)(2,1)S(1)}, u32[]{:S(2)}, u32[]{:S(2)}) async-start(bf16[128,16,128]{2,1,0:T(8,128)(2,1)} %shard_map.109), calls=%async_computation | async-start | bytes 1048576 | tf_op jit(solution)/shard_map/all_to_all | solution.py:344
  13.8 0.0 copy-start.7
  13.9 0.1 fusion.3
  13.9 0.1 broadcast_in_dim.33
  14.0 0.1 broadcast_in_dim.34
  14.1 0.1 broadcast_in_dim.30
  14.1 0.1 broadcast_in_dim.31
  14.2 0.6 copy-done.8
  14.8 0.1 select_reduce_fusion
  15.0 0.1 multiply_reduce_fusion
  15.1 12.8 %all-to-all-done = bf16[128,16,128]{2,1,0:T(8,128)(2,1)S(1)} async-done(((bf16[128,16,128]{2,1,0:T(8,128)(2,1)}), bf16[128,16,128]{2,1,0:T(8,128)(2,1)S(1)}, u32[]{:S(2)}, u32[]{:S(2)}) %all-to-all-start) | async-done | bytes 524320 | tf_op jit(solution)/shard_map/all_to_all | solution.py:344
  27.9 1.9 %shard_map.110 = (bf16[1024,128]{1,0:T(8,128)(2,1)}, f32[256,128]{1,0:T(8,128)S(1)}) custom-call(bf16[2048,128]{1,0:T(8,128)(2,1)S(1)} %bitcast.9, bf16[128,128]{1,0:T(8,128)(2,1)S(1)} %copy-done.9, f32[4,128,128]{2,1,0:T(8,128)S(1)} %copy-done.5, bf16[1024,256]{1,0:T(8,128)(2,1)S(1)} %copy-done, bf16[128,208]{1,0:T(8,128)(2,1)S(1)} %copy-done.7, ...), custom_call_target="tpu_custom_call" | custom-call | tf_op jit(solution)/shard_map/pallas_call | solution.py:364
  29.8 4.0 %all-to-all-start.1 = ((bf16[128,8,128]{2,1,0:T(8,128)(2,1)}), bf16[128,8,128]{2,1,0:T(8,128)(2,1)S(1)}, u32[]{:S(2)}, u32[]{:S(2)}) async-start(bf16[128,8,128]{2,1,0:T(8,128)(2,1)} %bitcast.1), calls=%async_computation.1 | async-start | bytes 524288 | tf_op jit(solution)/shard_map/all_to_all | solution.py:344
  33.9 0.1 broadcast_in_dim.35
  33.9 0.1 broadcast_in_dim.32
  34.0 11.1 %all-to-all-done.1 = bf16[128,8,128]{2,1,0:T(8,128)(2,1)S(1)} async-done(((bf16[128,8,128]{2,1,0:T(8,128)(2,1)}), bf16[128,8,128]{2,1,0:T(8,128)(2,1)S(1)}, u32[]{:S(2)}, u32[]{:S(2)}) %all-to-all-start.1) | async-done | bytes 262176 | tf_op jit(solution)/shard_map/all_to_all | solution.py:344
  45.2 3.1 %shard_map.111 = bf16[512,128]{1,0:T(8,128)(2,1)} custom-call(bf16[1024,128]{1,0:T(8,128)(2,1)S(1)} %bitcast.10, f32[256,128]{1,0:T(8,128)S(1)} %get-tuple-element.8.mask_ref, f32[2,4,8,128]{3,2,1,0:T(8,128)S(1)} %pad_maximum_fusion.rot_ref, bf16[256,512]{1,0:T(8,128)(2,1)S(1)} %copy-done.1, bf16[256,512]{1,0:T(8,128)(2,1)S(1)} %copy-done.2, ...), custom_call_target="tpu_custom_call" | custom-call | tf_op jit(solution)/shard_map/pallas_call | solution.py:384
  48.3 4.2 %all-to-all-start.2 = ((bf16[128,4,128]{2,1,0:T(4,128)(2,1)}), bf16[128,4,128]{2,1,0:T(4,128)(2,1)S(1)}, u32[]{:S(2)}, u32[]{:S(2)}) async-start(bf16[128,4,128]{2,1,0:T(4,128)(2,1)} %bitcast.3), calls=%async_computation.2 | async-start | bytes 262144 | tf_op jit(solution)/shard_map/all_to_all | solution.py:344
  52.5 10.0 %all-to-all-done.2 = bf16[128,4,128]{2,1,0:T(4,128)(2,1)S(1)} async-done(((bf16[128,4,128]{2,1,0:T(4,128)(2,1)}), bf16[128,4,128]{2,1,0:T(4,128)(2,1)S(1)}, u32[]{:S(2)}, u32[]{:S(2)}) %all-to-all-start.2) | async-done | bytes 131104 | tf_op jit(solution)/shard_map/all_to_all | solution.py:344
  62.4 0.8 %shard_map.112 = f32[8,64]{1,0:T(8,128)} custom-call(bf16[512,128]{1,0:T(8,128)(2,1)S(1)} %bitcast.11, f32[2,64]{1,0:T(2,128)S(1)} %pad_maximum_fusion.1.scale_ref), custom_call_target="tpu_custom_call" | custom-call | tf_op jit(solution)/shard_map/pallas_call | solution.py:401
  (23 shorter events, 0.1 us)
Async XLA Ops:
  2.3 25.6 %copy-start = (bf16[1024,256]{1,0:T(8,128)(2,1)S(1)}, bf16[1024,256]{1,0:T(8,128)(2,1)}, u32[]{:S(2)}) copy-start(bf16[1024,256]{1,0:T(8,128)(2,1)} %constant.82.clone.s2_ref) | copy-start | bytes 1572868
  2.3 25.6 %copy-start.5 = (f32[4,128,128]{2,1,0:T(8,128)S(1)}, f32[4,128,128]{2,1,0:T(8,128)}, u32[]{:S(2)}) copy-start(f32[4,128,128]{2,1,0:T(8,128)} %constant.81.clone.tw_ref) | copy-start | bytes 786436
  2.3 25.6 %copy-start.6 = (f32[128,256]{1,0:T(8,128)S(1)}, f32[128,256]{1,0:T(8,128)}, u32[]{:S(2)}) copy-start(f32[128,256]{1,0:T(8,128)} %constant.84.clone.taper_ref) | copy-start | bytes 393220
  2.3 25.6 %copy-start.9 = (bf16[128,128]{1,0:T(8,128)(2,1)S(1)}, bf16[128,128]{1,0:T(8,128)(2,1)}, u32[]{:S(2)}) copy-start(bf16[128,128]{1,0:T(8,128)(2,1)} %constant.80.clone.s1_ref) | copy-start | bytes 98308
  2.3 25.5 %all-to-all-start = ((bf16[128,16,128]{2,1,0:T(8,128)(2,1)}), bf16[128,16,128]{2,1,0:T(8,128)(2,1)S(1)}, u32[]{:S(2)}, u32[]{:S(2)}) async-start(bf16[128,16,128]{2,1,0:T(8,128)(2,1)} %shard_map.109), calls=%async_computation | async-start | bytes 1048576 | tf_op jit(solution)/shard_map/all_to_all | solution.py:344
  13.8 14.1 %copy-start.7 = (bf16[128,208]{1,0:T(8,128)(2,1)S(1)}, bf16[128,208]{1,0:T(8,128)(2,1)}, u32[]{:S(2)}) copy-start(bf16[128,208]{1,0:T(8,128)(2,1)} %constant.83.clone.win_ref) | copy-start | bytes 159748
  14.1 0.7 %copy-start.8 = (s32[16,16]{1,0:T(8,128)S(1)}, s32[16,16]{1,0:T(8,128)}, u32[]{:S(2)}) copy-start(s32[16,16]{1,0:T(8,128)} %mask_ref.1) | copy-start | bytes 3076
  27.9 17.3 %copy-start.3 = (bf16[512,256]{1,0:T(8,128)(2,1)S(1)}, bf16[512,256]{1,0:T(8,128)(2,1)}, u32[]{:S(2)}) copy-start(bf16[512,256]{1,0:T(8,128)(2,1)} %constant.87.clone.dh_ref) | copy-start | bytes 786436
  27.9 17.3 %copy-start.4 = (bf16[512,256]{1,0:T(8,128)(2,1)S(1)}, bf16[512,256]{1,0:T(8,128)(2,1)}, u32[]{:S(2)}) copy-start(bf16[512,256]{1,0:T(8,128)(2,1)} %constant.88.clone.dl_ref) | copy-start | bytes 786436
  29.8 15.3 %copy-start.1 = (bf16[256,512]{1,0:T(8,128)(2,1)S(1)}, bf16[256,512]{1,0:T(8,128)(2,1)}, u32[]{:S(2)}) copy-start(bf16[256,512]{1,0:T(8,128)(2,1)} %constant.85.clone.eh_ref) | copy-start | bytes 786436
  29.8 15.3 %copy-start.2 = (bf16[256,512]{1,0:T(8,128)(2,1)S(1)}, bf16[256,512]{1,0:T(8,128)(2,1)}, u32[]{:S(2)}) copy-start(bf16[256,512]{1,0:T(8,128)(2,1)} %constant.86.clone.el_ref) | copy-start | bytes 786436
  29.8 15.3 %all-to-all-start.1 = ((bf16[128,8,128]{2,1,0:T(8,128)(2,1)}), bf16[128,8,128]{2,1,0:T(8,128)(2,1)S(1)}, u32[]{:S(2)}, u32[]{:S(2)}) async-start(bf16[128,8,128]{2,1,0:T(8,128)(2,1)} %bitcast.1), calls=%async_computation.1 | async-start | bytes 524288 | tf_op jit(solution)/shard_map/all_to_all | solution.py:344
  48.3 14.2 %all-to-all-start.2 = ((bf16[128,4,128]{2,1,0:T(4,128)(2,1)}), bf16[128,4,128]{2,1,0:T(4,128)(2,1)S(1)}, u32[]{:S(2)}, u32[]{:S(2)}) async-start(bf16[128,4,128]{2,1,0:T(4,128)(2,1)} %bitcast.3), calls=%async_computation.2 | async-start | bytes 262144 | tf_op jit(solution)/shard_map/all_to_all | solution.py:344
